TPU v7x, 256 devices: a whole 4x4x8 slice. The times are simulated.
256 devices in a mesh: gx: 32 (over x, z), gy: 8 (over y, core).
Axes of the slice: x: 4, y: 4, z: 8, core: 2. Of those that a mesh axis runs over, the one named last changes fastest.
Arguments:
- source: float32 [6, 256, 128, 128], P(None, 'gx', 'gy'), may hold values from -6 to 6
- cell_class: int32 [256, 128, 128], P('gx', 'gy'), may hold values from 0 to 7
- class_conductivity: float32 [8], replicated, may hold values from 0.1 to 3
- layer_of_depth: int32 [64], replicated, may hold values from 0 to 7
- inverses: float32 [8, 192, 192], replicated, as said below
Outputs:
- correction: float32 [6, 256, 128, 128], P(None, 'gx', 'gy')
Inputs may be any that keep to these rules, and one draw needn't show every extreme that they name: `inverses`: each matrix has a positive diagonal.
All inputs are finite; a program needn't handle non-finite values.
Results may differ from a plain program's by a relative error of at most 0.000054.
Values sent between devices are 32-bit elements; how exact they have to be, the bound alone decides.
No kernel may reach another device: no remote copies, remote signals or barrier semaphores. Data moves between devices by JAX's collectives and lax.ppermute only.
A program may use at most 128 MiB of HBM per device.

v0:
```python
import jax
import jax.numpy as jnp
from jax import lax
from jax.experimental import pallas as pl
from jax.experimental.pallas import tpu as pltpu
from jax.sharding import PartitionSpec as P

damping = 0.8
F32 = jnp.float32
BF16 = jnp.bfloat16


def lane_of(shape):
    return lax.broadcasted_iota(jnp.int32, shape, 1)


def row_of(shape):
    return lax.broadcasted_iota(jnp.int32, shape, 0)


def take_lanes(v, index):
    return jnp.take_along_axis(v, index, axis=1, mode="promise_in_bounds")


def take_rows(v, index):
    return jnp.take_along_axis(v, index, axis=0, mode="promise_in_bounds")


def split_index(shape):
    j = lane_of(shape)
    return ((j & 63) << 1) | (j >> 6)


def join_index(shape):
    j = lane_of(shape)
    return ((j & 1) << 6) | (j >> 1)


class Blocker:
    def __init__(self, half):
        s = row_of((8, 128))
        j = lane_of((8, 128))
        self.half = half
        self.stay = (s < 4) == ((j & (2 * half - 1)) < half)
        self.to = ((s & 1) << 2) | (s >> 1)
        self.back = ((s & 3) << 1) | (s >> 2)

    def swap(self, v):
        return jnp.where(self.stay, v, pltpu.roll(pltpu.roll(v, 4, 0), self.half, 1))

    def forward(self, v):
        return take_rows(self.swap(v), self.to)

    def inverse(self, v):
        return self.swap(take_rows(v, self.back))


def dot(a, b):
    return lax.dot_general(a, b, (((1,), (0,)), ((), ())), preferred_element_type=F32)


def block_product(x, high, low, layer):
    x_high = x.astype(BF16)
    x_low = (x - x_high.astype(F32)).astype(BF16)
    total = jnp.zeros(x.shape, F32)
    for index in range(high.shape[0]):
        part = dot(high[index], x_high) + dot(low[index], x_high) + dot(high[index], x_low)
        total = jnp.where(layer == index, part, total)
    return total


def fine_layers(depth_ref):
    v = depth_ref[...]
    return jnp.concatenate([v, v, v, v], axis=1)


def coarse_layers(depth_ref):
    v = depth_ref[...]
    v = jnp.broadcast_to(jnp.concatenate([v, v], axis=1), (8, 128))
    return take_lanes(v, (lane_of((8, 128)) & 31) << 1)[0:1]


def fine_columns(blocker, get, put):
    for c in range(6):
        for x in range(8):
            v = get(c, x)
            for t in range(2):
                put(c * 32 + (x % 4) * 8, ((x // 4) * 2 + t) * 128, blocker.forward(v[8 * t : 8 * t + 8]))


def fine_smooth(blocker, columns, high, low, layer, put):
    for bx in range(2):
        total = block_product(columns[:, bx * 256 : bx * 256 + 256], high, low, layer) * damping
        for c in range(6):
            for x in range(4):
                row = c * 32 + x * 8
                for t in range(2):
                    put(c, 4 * bx + x, t, blocker.inverse(total[row : row + 8, 128 * t : 128 * t + 128]))


def store_columns(columns):
    def put(row, lane, v):
        columns[row : row + 8, lane : lane + 128] = v

    return put


def coarse_smooth(blocker, columns, get, high, low, layer):
    for c in range(6):
        for x in range(4):
            row = c * 32 + x * 8
            columns[row : row + 8, :] = blocker.forward(get(c, x))
    total = block_product(columns[...], high, low, layer) * (damping * 4.0)
    return lambda c, x: blocker.inverse(total[c * 32 + x * 8 : c * 32 + x * 8 + 8])


def first_kernel(source, depth, inverses, x0, high, low, x_first, x_last, y_first, y_last, columns):
    blocker = Blocker(64)
    for index in range(8):
        m = inverses[index]
        m_high = m.astype(BF16)
        high[index] = m_high
        low[index] = (m - m_high.astype(F32)).astype(BF16)
    split = split_index((16, 128))
    fine_columns(blocker, lambda c, x: take_lanes(source[c, x], split), store_columns(columns))

    def put(c, x, t, v):
        x0[c, x, 8 * t : 8 * t + 8, :] = v
        if x == 0:
            x_first[c, 8 * t : 8 * t + 8, :] = v
        if x == 7:
            x_last[c, 8 * t : 8 * t + 8, :] = v
        if t == 0:
            y_first[c, x : x + 1, :] = v[0:1]
        if t == 1:
            y_last[c, x : x + 1, :] = v[7:8]

    fine_smooth(blocker, columns, high, low, fine_layers(depth), put)


def around(u, y_before, y_after, half, other, keep, row):
    size = u.shape[0]
    before = jnp.where(row == 0, y_before, pltpu.roll(u, 1, 0))
    after = jnp.where(row == size - 1, y_after, pltpu.roll(u, size - 1, 0))
    return before + after + pltpu.roll(u, half, 1) + jnp.where(keep, take_lanes(u, other), 0.0)


def fine_other(shape):
    j = lane_of(shape)
    return jnp.where(j < 64, jnp.maximum(j + 63, 64), jnp.minimum(j - 63, 63)), (j != 0) & (j != 127)


def coarse_other(shape):
    j = lane_of(shape) & 63
    return jnp.where(j < 32, jnp.maximum(j + 31, 32), jnp.minimum(j - 31, 31)), (j != 0) & (j != 63)


def second_kernel(
    conductivity, source, classes, depth, x0, x_before, x_after, y_before, y_after, high, low,
    r0, b1, x1, sigma0, sigma1, x_first, x_last, y_first, y_last, rows, columns,
):
    shape = (16, 128)
    split = split_index(shape)
    other, keep = fine_other(shape)
    row = row_of(shape)
    j = lane_of(shape)
    pair = ((j & 31) << 1) | ((j >> 5) & 1)

    def restrict(v, slot):
        rows[slot] = take_lanes(v + pltpu.roll(v, 64, 1), pair)
        return (rows[slot, pl.ds(0, 8, stride=2), :] + rows[slot, pl.ds(1, 8, stride=2), :]) * 0.125

    for xx in range(4):
        sums = [None] * 7
        for x in (2 * xx, 2 * xx + 1):
            kind = take_lanes(classes[x], split)
            sigma = jnp.zeros(shape, F32)
            for index in range(8):
                sigma = jnp.where(kind == index, conductivity[index], sigma)
            sigma0[x] = sigma
            for c in range(3):
                re = x0[c, x]
                im = x0[c + 3, x]
                for comp, u, turn in ((c, re, -im), (c + 3, im, re)):
                    beside = around(
                        u, y_before[comp, x : x + 1], y_after[comp, x : x + 1], 64, other, keep, row
                    )
                    beside = beside + (x0[comp, x - 1] if x > 0 else x_before[comp])
                    beside = beside + (x0[comp, x + 1] if x < 7 else x_after[comp])
                    rest = take_lanes(source[comp, x], split) - (6.0 * u - beside + sigma * turn)
                    r0[comp, x] = rest
                    sums[comp] = rest if sums[comp] is None else sums[comp] + rest
            sums[6] = sigma if sums[6] is None else sums[6] + sigma
        for c in range(6):
            b1[c, xx] = restrict(sums[c], xx * 7 + c)
        sigma1[xx] = restrict(sums[6], xx * 7 + 6)
    result = coarse_smooth(Blocker(32), columns, lambda c, x: b1[c, x], high, low, coarse_layers(depth))
    store_coarse(result, x1, x_first, x_last, y_first, y_last)


def store_coarse(result, x1, x_first, x_last, y_first, y_last):
    for c in range(6):
        for x in range(4):
            v = result(c, x)
            x1[c, x] = v
            if x == 0:
                x_first[c] = v
            if x == 3:
                x_last[c] = v
            y_first[c, x : x + 1, :] = v[0:1]
            y_last[c, x : x + 1, :] = v[7:8]


def middle_kernel(depth, x0, r0, high, low, y0, columns):
    blocker = Blocker(64)
    fine_columns(blocker, lambda c, x: r0[c, x], store_columns(columns))

    def put(c, x, t, v):
        y0[c, x, 8 * t : 8 * t + 8, :] = x0[c, x, 8 * t : 8 * t + 8, :] + v

    fine_smooth(blocker, columns, high, low, fine_layers(depth), put)


def third_kernel(
    depth, b1, x1a, sigma1, x_before, x_after, y_before, y_after, high, low,
    x1, x_first, x_last, y_first, y_last, columns,
):
    shape = (8, 128)
    other, keep = coarse_other(shape)
    row = row_of(shape)

    def residual(c, x):
        u = x1a[c, x]
        turn = -x1a[c + 3, x] if c < 3 else x1a[c - 3, x]
        beside = around(u, y_before[c, x : x + 1], y_after[c, x : x + 1], 32, other, keep, row)
        beside = beside + (x1a[c, x - 1] if x > 0 else x_before[c])
        beside = beside + (x1a[c, x + 1] if x < 3 else x_after[c])
        return b1[c, x] - ((6.0 * u - beside) * 0.25 + sigma1[x] * turn)

    more = coarse_smooth(Blocker(32), columns, residual, high, low, coarse_layers(depth))
    store_coarse(lambda c, x: x1a[c, x] + more(c, x), x1, x_first, x_last, y_first, y_last)


def last_kernel(
    depth, y0, x1, sigma0, x_before, x_after, y_before, y_after, high, low, out, coarse, image, base, columns
):
    shape = (8, 128)
    j = lane_of(shape)
    row = row_of(shape)
    k = j & 63
    self_index = ((k & 1) << 5) | (k >> 1)
    beyond = jnp.where(j < 64, k - 1, k + 1)
    inside = (beyond >= 0) & (beyond < 64)
    beyond = jnp.clip(beyond, 0, 63)
    next_index = ((beyond & 1) << 5) | (beyond >> 1)

    for c in range(6):
        coarse[c, 0] = take_lanes(x_before[c], self_index)
        coarse[c, 5] = take_lanes(x_after[c], self_index)
        for x in range(4):
            coarse[c, x + 1] = take_lanes(x1[c, x], self_index)
    for xx in range(4):
        for c in range(3):
            own = {}
            for comp in (c, c + 3):
                v = coarse[comp, xx + 1]
                beside = jnp.where(inside, take_lanes(x1[comp, xx], next_index), 0.0)
                low_y = take_lanes(jnp.broadcast_to(y_before[comp, xx : xx + 1], shape), self_index)
                high_y = take_lanes(jnp.broadcast_to(y_after[comp, xx : xx + 1], shape), self_index)
                before = jnp.where(row == 0, low_y, pltpu.roll(v, 1, 0))
                after = jnp.where(row == 7, high_y, pltpu.roll(v, 7, 0))
                own[comp] = (v, 3.0 * v - beside, before, after)
            for half in range(2):
                x = 2 * xx + half
                for parity in range(2):
                    sigma = sigma0[x, pl.ds(parity, 8, stride=2), :]
                    for comp, partner, sign in ((c, c + 3, -1.0), (c + 3, c, 1.0)):
                        v, kept, before, after = own[comp]
                        turned = kept - coarse[comp, xx + 2 * half] - (before, after)[parity]
                        value = turned + sign * sigma * own[partner][0]
                        image[comp, x, pl.ds(parity, 8, stride=2), :] = value
            for comp in (c, c + 3):
                base[comp, xx, pl.ds(0, 8, stride=2), :] = own[comp][0]
                base[comp, xx, pl.ds(1, 8, stride=2), :] = own[comp][0]

    blocker = Blocker(64)
    fine_columns(blocker, lambda c, x: image[c, x], store_columns(columns))
    join = join_index(shape)

    def put(c, x, t, v):
        part = slice(8 * t, 8 * t + 8)
        out[c, x, part, :] = take_lanes(y0[c, x, part, :] + base[c, x // 2, part, :] - v, join)

    fine_smooth(blocker, columns, high, low, fine_layers(depth), put)


def call(kernel, outs, args, scratch, scalars=0):
    vmem = pl.BlockSpec(memory_space=pltpu.VMEM)
    smem = pl.BlockSpec(memory_space=pltpu.SMEM)
    return pl.pallas_call(
        kernel,
        out_shape=[jax.ShapeDtypeStruct(shape, dtype) for shape, dtype in outs],
        in_specs=[smem] * scalars + [vmem] * (len(args) - scalars),
        out_specs=[vmem] * len(outs),
        scratch_shapes=[pltpu.VMEM(shape, F32) for shape in scratch],
        name=kernel.__name__,
    )(*args)


def exchange(x_first, x_last, y_first, y_last):
    def shifted(array, axis, step):
        size = lax.axis_size(axis)
        return lax.ppermute(array, axis, [(i, i + step) for i in range(size) if 0 <= i + step < size])

    return (
        shifted(x_last, "gx", 1),
        shifted(x_first, "gx", -1),
        shifted(y_last, "gy", 1),
        shifted(y_first, "gy", -1),
    )


def per_device(source, cell_class, class_conductivity, layer_of_depth, inverses):
    depth = layer_of_depth.reshape(1, 64)
    fine = ((6, 8, 16, 128), F32)
    coarse = ((6, 4, 8, 128), F32)
    matrices = ((8, 192, 192), BF16)
    fine_faces = [((6, 16, 128), F32)] * 2 + [((6, 8, 128), F32)] * 2
    coarse_faces = [((6, 8, 128), F32)] * 2 + [((6, 4, 128), F32)] * 2

    x0, high, low, *faces = call(
        first_kernel, [fine, matrices, matrices] + fine_faces, (source, depth, inverses), [(192, 512)]
    )
    halos = exchange(*faces)
    r0, b1, x1a, sigma0, sigma1, *faces = call(
        second_kernel,
        [fine, coarse, coarse, ((8, 16, 128), F32), ((4, 8, 128), F32)] + coarse_faces,
        (class_conductivity, source, cell_class, depth, x0, *halos, high, low),
        [(28, 16, 128), (192, 128)],
        scalars=1,
    )
    halos = exchange(*faces)
    (y0,) = call(middle_kernel, [fine], (depth, x0, r0, high, low), [(192, 512)])
    x1, *faces = call(
        third_kernel, [coarse] + coarse_faces, (depth, b1, x1a, sigma1, *halos, high, low), [(192, 128)]
    )
    halos = exchange(*faces)
    (out,) = call(
        last_kernel,
        [fine],
        (depth, y0, x1, sigma0, *halos, high, low),
        [(6, 6, 8, 128), (6, 8, 16, 128), (6, 4, 16, 128), (192, 512)],
    )
    return out


def solution(mesh):
    placed = (P(None, "gx", "gy", None), P("gx", "gy", None), P(), P(), P())
    return jax.shard_map(
        per_device, mesh=mesh, in_specs=placed, out_specs=P(None, "gx", "gy", None), check_vma=False
    )
```

profile of v0, /device:TPU:7, one launch (start us, length us, event | category | flops | bytes accessed | tf_op | source)
XLA Modules:
  0.0 67.3 jit_solution(7213740986594409384)
XLA Ops:
  0.0 4.0 %first_kernel.1 = (f32[6,8,16,128]{3,2,1,0:T(8,128)}, bf16[8,192,192]{2,1,0:T(8,128)(2,1)}, bf16[8,192,192]{2,1,0:T(8,128)(2,1)}, f32[6,16,128]{2,1,0:T(8,128)},...) custom-call(f32[6,8,16,128]{3,2,1,0:T(8,128)} %source.3, s32[1,64]{1,0:T(1,128)} %bitcast.1, ...), custom_call_target="tpu_custom_call" | custom-call | tf_op jit(solution)/shard_map/first_kernel/pallas_call | solution.py:300
  4.0 3.5 %collective-permute-start = (f32[6,16,128]{2,1,0:T(8,128)}, f32[6,16,128]{2,1,0:T(8,128)S(1)}, u32[]{:S(2)}, u32[]{:S(2)}) collective-permute-start(f32[6,16,128]{2,1,0:T(8,128)} %get-tuple-element.27), channel_id=1, source_target_pairs={{0,8},{8,16},{16,24},{24,32},{32,40},{40,48},{48,56},{56,64},{64,7... | collective-permute-start | bytes 147464 | tf_op jit(solution)/shard_map/ppermute | solution.py:313
  7.5 6.1 %collective-permute-start.1 = (f32[6,16,128]{2,1,0:T(8,128)}, f32[6,16,128]{2,1,0:T(8,128)S(1)}, u32[]{:S(2)}, u32[]{:S(2)}) collective-permute-start(f32[6,16,128]{2,1,0:T(8,128)} %get-tuple-element.28), channel_id=1, source_target_pairs={{8,0},{16,8},{24,16},{32,24},{40,32},{48,40},{56,48},{64,56},{72,6... | collective-permute-start | bytes 147464 | tf_op jit(solution)/shard_map/ppermute | solution.py:313
  13.6 4.0 %collective-permute-start.2 = (f32[6,8,128]{2,1,0:T(8,128)}, f32[6,8,128]{2,1,0:T(8,128)S(1)}, u32[]{:S(2)}, u32[]{:S(2)}) collective-permute-start(f32[6,8,128]{2,1,0:T(8,128)} %get-tuple-element.29), channel_id=1, source_target_pairs={{0,1},{1,2},{2,3},{3,4},{4,5},{5,6},{6,7},{8,9},{9,10},{10,11},{11... | collective-permute-start | bytes 73736 | tf_op jit(solution)/shard_map/ppermute | solution.py:313
  17.7 1.9 %collective-permute-start.3 = (f32[6,8,128]{2,1,0:T(8,128)}, f32[6,8,128]{2,1,0:T(8,128)S(1)}, u32[]{:S(2)}, u32[]{:S(2)}) collective-permute-start(f32[6,8,128]{2,1,0:T(8,128)} %get-tuple-element.30), channel_id=1, source_target_pairs={{1,0},{2,1},{3,2},{4,3},{5,4},{6,5},{7,6},{9,8},{10,9},{11,10},{12... | collective-permute-start | bytes 73736 | tf_op jit(solution)/shard_map/ppermute | solution.py:313
  19.6 0.0 collective-permute-done.2.y_before
  19.6 0.0 copy-start.6
  19.6 3.4 %collective-permute-done.3.y_after = f32[6,8,128]{2,1,0:T(8,128)S(1)} collective-permute-done((f32[6,8,128]{2,1,0:T(8,128)}, f32[6,8,128]{2,1,0:T(8,128)S(1)}, u32[]{:S(2)}, u32[]{:S(2)}) %collective-permute-start.3) | collective-permute-done | bytes 24608 | tf_op jit(solution)/shard_map/ppermute | solution.py:313
  23.1 0.0 copy-start.7
  23.1 0.0 collective-permute-done.x_before
  23.1 0.0 copy-start
  23.1 0.0 collective-permute-done.1.x_after
  23.1 0.0 copy-start.1
  23.1 0.0 copy-done.6
  23.1 0.6 copy-done.7
  23.7 0.0 copy-done
  23.7 0.0 copy-done.1
  23.7 4.0 %second_kernel.1 = (f32[6,8,16,128]{3,2,1,0:T(8,128)}, f32[6,4,8,128]{3,2,1,0:T(8,128)}, f32[6,4,8,128]{3,2,1,0:T(8,128)}, f32[8,16,128]{2,1,0:T(8,128)}, f32[4,...) custom-call(f32[8]{0:T(128)} %conductivity.1, ...), custom_call_target="tpu_custom_call" | custom-call | tf_op jit(solution)/shard_map/second_kernel/pallas_call | solution.py:300
  27.7 1.9 %collective-permute-start.4 = (f32[6,8,128]{2,1,0:T(8,128)}, f32[6,8,128]{2,1,0:T(8,128)S(1)}, u32[]{:S(2)}, u32[]{:S(2)}) collective-permute-start(f32[6,8,128]{2,1,0:T(8,128)} %get-tuple-element.37), channel_id=1, source_target_pairs={{0,8},{8,16},{16,24},{24,32},{32,40},{40,48},{48,56},{56,64},{64,7... | collective-permute-start | bytes 73736 | tf_op jit(solution)/shard_map/ppermute | solution.py:313
  29.6 5.5 %collective-permute-start.5 = (f32[6,8,128]{2,1,0:T(8,128)}, f32[6,8,128]{2,1,0:T(8,128)S(1)}, u32[]{:S(2)}, u32[]{:S(2)}) collective-permute-start(f32[6,8,128]{2,1,0:T(8,128)} %get-tuple-element.38), channel_id=1, source_target_pairs={{8,0},{16,8},{24,16},{32,24},{40,32},{48,40},{56,48},{64,56},{72,6... | collective-permute-start | bytes 73736 | tf_op jit(solution)/shard_map/ppermute | solution.py:313
  35.1 2.5 %collective-permute-start.6 = (f32[6,4,128]{2,1,0:T(4,128)}, f32[6,4,128]{2,1,0:T(4,128)S(1)}, u32[]{:S(2)}, u32[]{:S(2)}) collective-permute-start(f32[6,4,128]{2,1,0:T(4,128)} %get-tuple-element.39), channel_id=1, source_target_pairs={{0,1},{1,2},{2,3},{3,4},{4,5},{5,6},{6,7},{8,9},{9,10},{10,11},{11... | collective-permute-start | bytes 36872 | tf_op jit(solution)/shard_map/ppermute | solution.py:313
  37.6 1.9 %collective-permute-start.7 = (f32[6,4,128]{2,1,0:T(4,128)}, f32[6,4,128]{2,1,0:T(4,128)S(1)}, u32[]{:S(2)}, u32[]{:S(2)}) collective-permute-start(f32[6,4,128]{2,1,0:T(4,128)} %get-tuple-element.40), channel_id=1, source_target_pairs={{1,0},{2,1},{3,2},{4,3},{5,4},{6,5},{7,6},{9,8},{10,9},{11,10},{12... | collective-permute-start | bytes 36872 | tf_op jit(solution)/shard_map/ppermute | solution.py:313
  39.5 0.0 collective-permute-done.6.y_before
  39.5 0.0 copy-start.9
  39.5 3.3 %collective-permute-done.7.y_after = f32[6,4,128]{2,1,0:T(4,128)S(1)} collective-permute-done((f32[6,4,128]{2,1,0:T(4,128)}, f32[6,4,128]{2,1,0:T(4,128)S(1)}, u32[]{:S(2)}, u32[]{:S(2)}) %collective-permute-start.7) | collective-permute-done | bytes 12320 | tf_op jit(solution)/shard_map/ppermute | solution.py:313
  42.8 0.0 copy-start.11
  42.8 0.0 collective-permute-done.4.x_before
  42.8 0.0 copy-start.3
  42.8 0.0 collective-permute-done.5.x_after
  42.8 0.0 copy-start.5
  42.8 0.0 copy-done.9
  42.8 0.6 copy-done.11
  43.4 0.0 copy-done.3
  43.4 0.0 copy-done.5
  43.4 3.3 %third_kernel.1 = (f32[6,4,8,128]{3,2,1,0:T(8,128)}, f32[6,8,128]{2,1,0:T(8,128)}, f32[6,8,128]{2,1,0:T(8,128)}, f32[6,4,128]{2,1,0:T(4,128)}, f32[6,4,128]{2,1,0:T(4,128)}) custom-call(s32[1,64]{1,0:T(1,128)} %bitcast.3, f32[6,4,8,128]{3,2,1,0:T(8,128)} %get-tuple-element.34.b1, f32[6,4,8,128]{3,2,1,0:T(8,128)} %get-tuple-element.35.x1a, ...), custom_call_target="tpu_custom_call" | custom-call | tf_op jit(solution)/shard_map/third_kernel/pallas_call | solution.py:300
  46.7 1.9 %collective-permute-start.8 = (f32[6,8,128]{2,1,0:T(8,128)}, f32[6,8,128]{2,1,0:T(8,128)S(1)}, u32[]{:S(2)}, u32[]{:S(2)}) collective-permute-start(f32[6,8,128]{2,1,0:T(8,128)} %get-tuple-element.43), channel_id=1, source_target_pairs={{0,8},{8,16},{16,24},{24,32},{32,40},{40,48},{48,56},{56,64},{64,7... | collective-permute-start | bytes 73736 | tf_op jit(solution)/shard_map/ppermute | solution.py:313
  48.6 5.5 %collective-permute-start.9 = (f32[6,8,128]{2,1,0:T(8,128)}, f32[6,8,128]{2,1,0:T(8,128)S(1)}, u32[]{:S(2)}, u32[]{:S(2)}) collective-permute-start(f32[6,8,128]{2,1,0:T(8,128)} %get-tuple-element.44), channel_id=1, source_target_pairs={{8,0},{16,8},{24,16},{32,24},{40,32},{48,40},{56,48},{64,56},{72,6... | collective-permute-start | bytes 73736 | tf_op jit(solution)/shard_map/ppermute | solution.py:313
  54.1 2.5 %collective-permute-start.10 = (f32[6,4,128]{2,1,0:T(4,128)}, f32[6,4,128]{2,1,0:T(4,128)S(1)}, u32[]{:S(2)}, u32[]{:S(2)}) collective-permute-start(f32[6,4,128]{2,1,0:T(4,128)} %get-tuple-element.45), channel_id=1, source_target_pairs={{0,1},{1,2},{2,3},{3,4},{4,5},{5,6},{6,7},{8,9},{9,10},{10,11},{11... | collective-permute-start | bytes 36872 | tf_op jit(solution)/shard_map/ppermute | solution.py:313
  56.6 1.9 %collective-permute-start.11 = (f32[6,4,128]{2,1,0:T(4,128)}, f32[6,4,128]{2,1,0:T(4,128)S(1)}, u32[]{:S(2)}, u32[]{:S(2)}) collective-permute-start(f32[6,4,128]{2,1,0:T(4,128)} %get-tuple-element.46), channel_id=1, source_target_pairs={{1,0},{2,1},{3,2},{4,3},{5,4},{6,5},{7,6},{9,8},{10,9},{11,10},{12... | collective-permute-start | bytes 36872 | tf_op jit(solution)/shard_map/ppermute | solution.py:313
  58.5 3.9 %middle_kernel.1.y0 = f32[6,8,16,128]{3,2,1,0:T(8,128)} custom-call(s32[1,64]{1,0:T(1,128)} %bitcast.4, f32[6,8,16,128]{3,2,1,0:T(8,128)} %get-tuple-element.26.x0, f32[6,8,16,128]{3,2,1,0:T(8,128)} %get-tuple-element.33.r0, bf16[8,192,192]{2,1,0:T(8,128)(2,1)} %get-tuple-element.31.high, bf16[8,192,192]{2,1,0:T(8,128)(2,1)} %get-tuple-element.32.low), custom_call_target="tpu_custom_call" | custom-call | tf_op jit(solution)/shard_map/middle_kernel/pallas_call | solution.py:300
  62.5 0.0 collective-permute-done.10.y_before
  62.5 0.0 copy-start.8
  62.5 0.0 collective-permute-done.11.y_after
  62.5 0.0 copy-start.10
  62.5 0.0 collective-permute-done.8.x_before
  62.5 0.0 copy-start.2
  62.5 0.0 collective-permute-done.9.x_after
  62.5 0.0 copy-start.4
  62.5 0.5 copy-done.8
  63.1 0.0 copy-done.10
  63.1 0.0 copy-done.2
  63.1 0.0 copy-done.4
  63.1 4.2 %last_kernel.1 = f32[6,8,16,128]{3,2,1,0:T(8,128)} custom-call(s32[1,64]{1,0:T(1,128)} %bitcast.5, f32[6,8,16,128]{3,2,1,0:T(8,128)} %middle_kernel.1.y0, f32[6,4,8,128]{3,2,1,0:T(8,128)} %get-tuple-element.41.x1, f32[8,16,128]{2,1,0:T(8,128)} %get-tuple-element.42.sigma0, f32[6,8,128]{2,1,0:T(8,128)} %copy-done.2, f32[6,8,128]{2,1,0:T(8,128)} %copy-done.4, ...), custom_call_target="tpu_custom_call" | custom-call | tf_op jit(solution)/shard_map/last_kernel/pallas_call | solution.py:300
Async XLA Ops:
  4.0 19.1 %collective-permute-start = (f32[6,16,128]{2,1,0:T(8,128)}, f32[6,16,128]{2,1,0:T(8,128)S(1)}, u32[]{:S(2)}, u32[]{:S(2)}) collective-permute-start(f32[6,16,128]{2,1,0:T(8,128)} %get-tuple-element.27), channel_id=1, source_target_pairs={{0,8},{8,16},{16,24},{24,32},{32,40},{40,48},{48,56},{56,64},{64,7... | collective-permute-start | bytes 147464 | tf_op jit(solution)/shard_map/ppermute | solution.py:313
  7.5 15.6 %collective-permute-start.1 = (f32[6,16,128]{2,1,0:T(8,128)}, f32[6,16,128]{2,1,0:T(8,128)S(1)}, u32[]{:S(2)}, u32[]{:S(2)}) collective-permute-start(f32[6,16,128]{2,1,0:T(8,128)} %get-tuple-element.28), channel_id=1, source_target_pairs={{8,0},{16,8},{24,16},{32,24},{40,32},{48,40},{56,48},{64,56},{72,6... | collective-permute-start | bytes 147464 | tf_op jit(solution)/shard_map/ppermute | solution.py:313
  13.6 6.0 %collective-permute-start.2 = (f32[6,8,128]{2,1,0:T(8,128)}, f32[6,8,128]{2,1,0:T(8,128)S(1)}, u32[]{:S(2)}, u32[]{:S(2)}) collective-permute-start(f32[6,8,128]{2,1,0:T(8,128)} %get-tuple-element.29), channel_id=1, source_target_pairs={{0,1},{1,2},{2,3},{3,4},{4,5},{5,6},{6,7},{8,9},{9,10},{10,11},{11... | collective-permute-start | bytes 73736 | tf_op jit(solution)/shard_map/ppermute | solution.py:313
  17.7 5.4 %collective-permute-start.3 = (f32[6,8,128]{2,1,0:T(8,128)}, f32[6,8,128]{2,1,0:T(8,128)S(1)}, u32[]{:S(2)}, u32[]{:S(2)}) collective-permute-start(f32[6,8,128]{2,1,0:T(8,128)} %get-tuple-element.30), channel_id=1, source_target_pairs={{1,0},{2,1},{3,2},{4,3},{5,4},{6,5},{7,6},{9,8},{10,9},{11,10},{12... | collective-permute-start | bytes 73736 | tf_op jit(solution)/shard_map/ppermute | solution.py:313
  19.6 3.4 %copy-start.6 = (f32[6,8,128]{2,1,0:T(8,128)}, f32[6,8,128]{2,1,0:T(8,128)S(1)}, u32[]{:S(2)}) copy-start(f32[6,8,128]{2,1,0:T(8,128)S(1)} %collective-permute-done.2.y_before) | copy-start | bytes 73732
  23.1 0.6 copy-start.7
  23.1 0.6 copy-start
  23.1 0.6 copy-start.1
  27.7 15.1 %collective-permute-start.4 = (f32[6,8,128]{2,1,0:T(8,128)}, f32[6,8,128]{2,1,0:T(8,128)S(1)}, u32[]{:S(2)}, u32[]{:S(2)}) collective-permute-start(f32[6,8,128]{2,1,0:T(8,128)} %get-tuple-element.37), channel_id=1, source_target_pairs={{0,8},{8,16},{16,24},{24,32},{32,40},{40,48},{48,56},{56,64},{64,7... | collective-permute-start | bytes 73736 | tf_op jit(solution)/shard_map/ppermute | solution.py:313
  29.6 13.2 %collective-permute-start.5 = (f32[6,8,128]{2,1,0:T(8,128)}, f32[6,8,128]{2,1,0:T(8,128)S(1)}, u32[]{:S(2)}, u32[]{:S(2)}) collective-permute-start(f32[6,8,128]{2,1,0:T(8,128)} %get-tuple-element.38), channel_id=1, source_target_pairs={{8,0},{16,8},{24,16},{32,24},{40,32},{48,40},{56,48},{64,56},{72,6... | collective-permute-start | bytes 73736 | tf_op jit(solution)/shard_map/ppermute | solution.py:313
  35.1 4.4 %collective-permute-start.6 = (f32[6,4,128]{2,1,0:T(4,128)}, f32[6,4,128]{2,1,0:T(4,128)S(1)}, u32[]{:S(2)}, u32[]{:S(2)}) collective-permute-start(f32[6,4,128]{2,1,0:T(4,128)} %get-tuple-element.39), channel_id=1, source_target_pairs={{0,1},{1,2},{2,3},{3,4},{4,5},{5,6},{6,7},{8,9},{9,10},{10,11},{11... | collective-permute-start | bytes 36872 | tf_op jit(solution)/shard_map/ppermute | solution.py:313
  37.6 5.2 %collective-permute-start.7 = (f32[6,4,128]{2,1,0:T(4,128)}, f32[6,4,128]{2,1,0:T(4,128)S(1)}, u32[]{:S(2)}, u32[]{:S(2)}) collective-permute-start(f32[6,4,128]{2,1,0:T(4,128)} %get-tuple-element.40), channel_id=1, source_target_pairs={{1,0},{2,1},{3,2},{4,3},{5,4},{6,5},{7,6},{9,8},{10,9},{11,10},{12... | collective-permute-start | bytes 36872 | tf_op jit(solution)/shard_map/ppermute | solution.py:313
  39.5 3.3 %copy-start.9 = (f32[6,4,128]{2,1,0:T(4,128)}, f32[6,4,128]{2,1,0:T(4,128)S(1)}, u32[]{:S(2)}) copy-start(f32[6,4,128]{2,1,0:T(4,128)S(1)} %collective-permute-done.6.y_before) | copy-start | bytes 36868
  42.8 0.6 copy-start.11
  42.8 0.6 copy-start.3
  42.8 0.6 copy-start.5
  46.7 15.8 %collective-permute-start.8 = (f32[6,8,128]{2,1,0:T(8,128)}, f32[6,8,128]{2,1,0:T(8,128)S(1)}, u32[]{:S(2)}, u32[]{:S(2)}) collective-permute-start(f32[6,8,128]{2,1,0:T(8,128)} %get-tuple-element.43), channel_id=1, source_target_pairs={{0,8},{8,16},{16,24},{24,32},{32,40},{40,48},{48,56},{56,64},{64,7... | collective-permute-start | bytes 73736 | tf_op jit(solution)/shard_map/ppermute | solution.py:313
  48.6 13.9 %collective-permute-start.9 = (f32[6,8,128]{2,1,0:T(8,128)}, f32[6,8,128]{2,1,0:T(8,128)S(1)}, u32[]{:S(2)}, u32[]{:S(2)}) collective-permute-start(f32[6,8,128]{2,1,0:T(8,128)} %get-tuple-element.44), channel_id=1, source_target_pairs={{8,0},{16,8},{24,16},{32,24},{40,32},{48,40},{56,48},{64,56},{72,6... | collective-permute-start | bytes 73736 | tf_op jit(solution)/shard_map/ppermute | solution.py:313
  54.1 8.4 %collective-permute-start.10 = (f32[6,4,128]{2,1,0:T(4,128)}, f32[6,4,128]{2,1,0:T(4,128)S(1)}, u32[]{:S(2)}, u32[]{:S(2)}) collective-permute-start(f32[6,4,128]{2,1,0:T(4,128)} %get-tuple-element.45), channel_id=1, source_target_pairs={{0,1},{1,2},{2,3},{3,4},{4,5},{5,6},{6,7},{8,9},{9,10},{10,11},{11... | collective-permute-start | bytes 36872 | tf_op jit(solution)/shard_map/ppermute | solution.py:313
  56.6 5.9 %collective-permute-start.11 = (f32[6,4,128]{2,1,0:T(4,128)}, f32[6,4,128]{2,1,0:T(4,128)S(1)}, u32[]{:S(2)}, u32[]{:S(2)}) collective-permute-start(f32[6,4,128]{2,1,0:T(4,128)} %get-tuple-element.46), channel_id=1, source_target_pairs={{1,0},{2,1},{3,2},{4,3},{5,4},{6,5},{7,6},{9,8},{10,9},{11,10},{12... | collective-permute-start | bytes 36872 | tf_op jit(solution)/shard_map/ppermute | solution.py:313
  62.5 0.6 copy-start.8
  62.5 0.6 copy-start.10
  62.5 0.6 copy-start.2
  62.5 0.6 copy-start.4
where the time goes:
time: 67.9 us; the launch traced here: 67.3 us
  starting transfers between devices  39.2 us (58%)
  Pallas kernels  19.4 us (29%)
  waiting for transfers between devices  6.71 us (10%)
  local copies, waits for them, and re-layouts  1.85 us (3%)
    ppermute x12, starting transfers between devices, shifted(): lax.ppermute(array, axis, [(i, i + step) for i in range(size) if 0 <= i +...  39.2 us
    pallas_call x5, Pallas kernels, call(): pl.pallas_call(kernel, out_shape=[jax.ShapeDtypeStruct(shape, dtype) for...  19.4 us
    ppermute x12, waiting for transfers between devices, shifted(): lax.ppermute(array, axis, [(i, i + step) for i in range(size) if 0 <= i +...  6.71 us
    unnamed x24, local copies, waits for them, and re-layouts  1.85 us
  transfers between devices with their start and end apart: 12, of which 2 were waited for; matrix products, arithmetic and copies ran while one was open for 0% of the time, Pallas kernels for 6%

commit v1 on v0

--- a/solution.py
+++ b/solution.py
@@ -114,7 +114,7 @@
     return lambda c, x: blocker.inverse(total[c * 32 + x * 8 : c * 32 + x * 8 + 8])
 
 
-def first_kernel(source, depth, inverses, x0, high, low, x_first, x_last, y_first, y_last, columns):
+def first_kernel(source, depth, inverses, x0, high, low, x_near, x_far, y_near, y_far, columns):
     blocker = Blocker(64)
     for index in range(8):
         m = inverses[index]
@@ -126,16 +126,11 @@
 
     def put(c, x, t, v):
         x0[c, x, 8 * t : 8 * t + 8, :] = v
-        if x == 0:
-            x_first[c, 8 * t : 8 * t + 8, :] = v
-        if x == 7:
-            x_last[c, 8 * t : 8 * t + 8, :] = v
-        if t == 0:
-            y_first[c, x : x + 1, :] = v[0:1]
-        if t == 1:
-            y_last[c, x : x + 1, :] = v[7:8]
 
     fine_smooth(blocker, columns, high, low, fine_layers(depth), put)
+    for c in range(6):
+        x_near[c], x_far[c] = near_far("gx", x0[c, 0], x0[c, 7])
+        y_near[c], y_far[c] = near_far("gy", x0[c, :, 0, :], x0[c, :, 15, :])
 
 
 def around(u, y_before, y_after, half, other, keep, row):
@@ -156,9 +151,11 @@
 
 
 def second_kernel(
-    conductivity, source, classes, depth, x0, x_before, x_after, y_before, y_after, high, low,
-    r0, b1, x1, sigma0, sigma1, x_first, x_last, y_first, y_last, rows, columns,
+    conductivity, source, classes, depth, x0, x_near_in, x_far_in, y_near_in, y_far_in, high, low,
+    r0, b1, x1, sigma0, sigma1, x_near, x_far, y_near, y_far, rows, columns,
 ):
+    x_halo = [before_after("gx", x_near_in[c], x_far_in[c]) for c in range(6)]
+    y_halo = [before_after("gy", y_near_in[c], y_far_in[c]) for c in range(6)]
     shape = (16, 128)
     split = split_index(shape)
     other, keep = fine_other(shape)
@@ -183,10 +180,10 @@
                 im = x0[c + 3, x]
                 for comp, u, turn in ((c, re, -im), (c + 3, im, re)):
                     beside = around(
-                        u, y_before[comp, x : x + 1], y_after[comp, x : x + 1], 64, other, keep, row
+                        u, y_halo[comp][0][x : x + 1], y_halo[comp][1][x : x + 1], 64, other, keep, row
                     )
-                    beside = beside + (x0[comp, x - 1] if x > 0 else x_before[comp])
-                    beside = beside + (x0[comp, x + 1] if x < 7 else x_after[comp])
+                    beside = beside + (x0[comp, x - 1] if x > 0 else x_halo[comp][0])
+                    beside = beside + (x0[comp, x + 1] if x < 7 else x_halo[comp][1])
                     rest = take_lanes(source[comp, x], split) - (6.0 * u - beside + sigma * turn)
                     r0[comp, x] = rest
                     sums[comp] = rest if sums[comp] is None else sums[comp] + rest
@@ -195,20 +192,15 @@
             b1[c, xx] = restrict(sums[c], xx * 7 + c)
         sigma1[xx] = restrict(sums[6], xx * 7 + 6)
     result = coarse_smooth(Blocker(32), columns, lambda c, x: b1[c, x], high, low, coarse_layers(depth))
-    store_coarse(result, x1, x_first, x_last, y_first, y_last)
-
-
-def store_coarse(result, x1, x_first, x_last, y_first, y_last):
+    store_coarse(result, x1, x_near, x_far, y_near, y_far)
+
+
+def store_coarse(result, x1, x_near, x_far, y_near, y_far):
     for c in range(6):
         for x in range(4):
-            v = result(c, x)
-            x1[c, x] = v
-            if x == 0:
-                x_first[c] = v
-            if x == 3:
-                x_last[c] = v
-            y_first[c, x : x + 1, :] = v[0:1]
-            y_last[c, x : x + 1, :] = v[7:8]
+            x1[c, x] = result(c, x)
+        x_near[c], x_far[c] = near_far("gx", x1[c, 0], x1[c, 3])
+        y_near[c], y_far[c] = near_far("gy", x1[c, :, 0, :], x1[c, :, 7, :])
 
 
 def middle_kernel(depth, x0, r0, high, low, y0, columns):
@@ -222,9 +214,11 @@
 
 
 def third_kernel(
-    depth, b1, x1a, sigma1, x_before, x_after, y_before, y_after, high, low,
-    x1, x_first, x_last, y_first, y_last, columns,
+    depth, b1, x1a, sigma1, x_near_in, x_far_in, y_near_in, y_far_in, high, low,
+    x1, x_near, x_far, y_near, y_far, columns,
 ):
+    x_halo = [before_after("gx", x_near_in[c], x_far_in[c]) for c in range(6)]
+    y_halo = [before_after("gy", y_near_in[c], y_far_in[c]) for c in range(6)]
     shape = (8, 128)
     other, keep = coarse_other(shape)
     row = row_of(shape)
@@ -232,18 +226,20 @@
     def residual(c, x):
         u = x1a[c, x]
         turn = -x1a[c + 3, x] if c < 3 else x1a[c - 3, x]
-        beside = around(u, y_before[c, x : x + 1], y_after[c, x : x + 1], 32, other, keep, row)
-        beside = beside + (x1a[c, x - 1] if x > 0 else x_before[c])
-        beside = beside + (x1a[c, x + 1] if x < 3 else x_after[c])
+        beside = around(u, y_halo[c][0][x : x + 1], y_halo[c][1][x : x + 1], 32, other, keep, row)
+        beside = beside + (x1a[c, x - 1] if x > 0 else x_halo[c][0])
+        beside = beside + (x1a[c, x + 1] if x < 3 else x_halo[c][1])
         return b1[c, x] - ((6.0 * u - beside) * 0.25 + sigma1[x] * turn)
 
     more = coarse_smooth(Blocker(32), columns, residual, high, low, coarse_layers(depth))
-    store_coarse(lambda c, x: x1a[c, x] + more(c, x), x1, x_first, x_last, y_first, y_last)
+    store_coarse(lambda c, x: x1a[c, x] + more(c, x), x1, x_near, x_far, y_near, y_far)
 
 
 def last_kernel(
-    depth, y0, x1, sigma0, x_before, x_after, y_before, y_after, high, low, out, coarse, image, base, columns
+    depth, y0, x1, sigma0, x_near_in, x_far_in, y_near_in, y_far_in, high, low, out, coarse, image, base, columns
 ):
+    x_halo = [before_after("gx", x_near_in[c], x_far_in[c]) for c in range(6)]
+    y_halo = [before_after("gy", y_near_in[c], y_far_in[c]) for c in range(6)]
     shape = (8, 128)
     j = lane_of(shape)
     row = row_of(shape)
@@ -255,8 +251,8 @@
     next_index = ((beyond & 1) << 5) | (beyond >> 1)
 
     for c in range(6):
-        coarse[c, 0] = take_lanes(x_before[c], self_index)
-        coarse[c, 5] = take_lanes(x_after[c], self_index)
+        coarse[c, 0] = take_lanes(x_halo[c][0], self_index)
+        coarse[c, 5] = take_lanes(x_halo[c][1], self_index)
         for x in range(4):
             coarse[c, x + 1] = take_lanes(x1[c, x], self_index)
     for xx in range(4):
@@ -265,8 +261,8 @@
             for comp in (c, c + 3):
                 v = coarse[comp, xx + 1]
                 beside = jnp.where(inside, take_lanes(x1[comp, xx], next_index), 0.0)
-                low_y = take_lanes(jnp.broadcast_to(y_before[comp, xx : xx + 1], shape), self_index)
-                high_y = take_lanes(jnp.broadcast_to(y_after[comp, xx : xx + 1], shape), self_index)
+                low_y = take_lanes(jnp.broadcast_to(y_halo[comp][0][xx : xx + 1], shape), self_index)
+                high_y = take_lanes(jnp.broadcast_to(y_halo[comp][1][xx : xx + 1], shape), self_index)
                 before = jnp.where(row == 0, low_y, pltpu.roll(v, 1, 0))
                 after = jnp.where(row == 7, high_y, pltpu.roll(v, 7, 0))
                 own[comp] = (v, 3.0 * v - beside, before, after)
@@ -294,30 +290,45 @@
     fine_smooth(blocker, columns, high, low, fine_layers(depth), put)
 
 
-def call(kernel, outs, args, scratch, scalars=0):
+def call(kernel, outs, args, scratch, scalars=0, outside=1, last=False):
     vmem = pl.BlockSpec(memory_space=pltpu.VMEM)
     smem = pl.BlockSpec(memory_space=pltpu.SMEM)
+    args = list(args[:outside]) + [pltpu.with_memory_space_constraint(arg, pltpu.VMEM) for arg in args[outside:]]
     return pl.pallas_call(
         kernel,
-        out_shape=[jax.ShapeDtypeStruct(shape, dtype) for shape, dtype in outs],
+        out_shape=[jax.ShapeDtypeStruct(*out) if last else pltpu.VMEM(*out) for out in outs],
         in_specs=[smem] * scalars + [vmem] * (len(args) - scalars),
         out_specs=[vmem] * len(outs),
         scratch_shapes=[pltpu.VMEM(shape, F32) for shape in scratch],
+        compiler_params=pltpu.CompilerParams(vmem_limit_bytes=12 << 20),
         name=kernel.__name__,
     )(*args)
 
 
-def exchange(x_first, x_last, y_first, y_last):
-    def shifted(array, axis, step):
+def exchange(x_near, x_far, y_near, y_far):
+    def swapped(array, axis, first):
         size = lax.axis_size(axis)
-        return lax.ppermute(array, axis, [(i, i + step) for i in range(size) if 0 <= i + step < size])
-
-    return (
-        shifted(x_last, "gx", 1),
-        shifted(x_first, "gx", -1),
-        shifted(y_last, "gy", 1),
-        shifted(y_first, "gy", -1),
-    )
+        pairs = [(i, (i + 1) % size) for i in range(first, size, 2)]
+        return lax.ppermute(array, axis, pairs + [(j, i) for i, j in pairs])
+
+    y_near = swapped(y_near, "gy", 0)
+    x_near = swapped(x_near, "gx", 0)
+    y_far = swapped(y_far, "gy", 1)
+    x_far = swapped(x_far, "gx", 1)
+    return x_near, x_far, y_near, y_far
+
+
+def near_far(axis, first, last):
+    even = lax.axis_index(axis) % 2 == 0
+    return jnp.where(even, last, first), jnp.where(even, first, last)
+
+
+def before_after(axis, near, far):
+    place = lax.axis_index(axis)
+    even = place % 2 == 0
+    before = jnp.where(place > 0, jnp.where(even, far, near), 0.0)
+    after = jnp.where(place < lax.axis_size(axis) - 1, jnp.where(even, near, far), 0.0)
+    return before, after
 
 
 def per_device(source, cell_class, class_conductivity, layer_of_depth, inverses):
@@ -329,7 +340,7 @@
     coarse_faces = [((6, 8, 128), F32)] * 2 + [((6, 4, 128), F32)] * 2
 
     x0, high, low, *faces = call(
-        first_kernel, [fine, matrices, matrices] + fine_faces, (source, depth, inverses), [(192, 512)]
+        first_kernel, [fine, matrices, matrices] + fine_faces, (source, depth, inverses), [(192, 512)], outside=3
     )
     halos = exchange(*faces)
     r0, b1, x1a, sigma0, sigma1, *faces = call(
@@ -338,6 +349,7 @@
         (class_conductivity, source, cell_class, depth, x0, *halos, high, low),
         [(28, 16, 128), (192, 128)],
         scalars=1,
+        outside=4,
     )
     halos = exchange(*faces)
     (y0,) = call(middle_kernel, [fine], (depth, x0, r0, high, low), [(192, 512)])
@@ -350,6 +362,7 @@
         [fine],
         (depth, y0, x1, sigma0, *halos, high, low),
         [(6, 6, 8, 128), (6, 8, 16, 128), (6, 4, 16, 128), (192, 512)],
+        last=True,
     )
     return out
 

time: 67.9 us -> 39.8 us (0.59)
  the two profiles are of different devices: /device:TPU:7 before, /device:TPU:25 now
where the time goes in v1:
time: 39.8 us; the launch traced here: 39.7 us
  starting transfers between devices  15.9 us (40%)
  waiting for transfers between devices  11.5 us (29%)
  Pallas kernels  9.1 us (23%)
  local copies, waits for them, and re-layouts  3.08 us (8%)
    ppermute x12, starting transfers between devices, swapped(): return lax.ppermute(array, axis, pairs + [(j, i) for i, j in pairs])  15.9 us
    ppermute x12, waiting for transfers between devices, swapped(): return lax.ppermute(array, axis, pairs + [(j, i) for i, j in pairs])  11.5 us
    pallas_call x5, Pallas kernels, call(): pl.pallas_call(kernel, out_shape=[jax.ShapeDtypeStruct(*out) if last else...  9.1 us
    unnamed x10, local copies, waits for them, and re-layouts  3.08 us
  transfers between devices with their start and end apart: 12, of which 5 were waited for; matrix products, arithmetic and copies ran while one was open for 0% of the time, Pallas kernels for 4%

profile of v1, /device:TPU:25, one launch (start us, length us, event | category | flops | bytes accessed | tf_op | source)
XLA Modules:
  0.0 39.7 jit_solution(3909737536715593270)
XLA Ops:
  0.0 0.0 copy-start.4
  0.0 0.0 copy-start
  0.0 1.0 %copy-done = f32[6,8,16,128]{3,2,1,0:T(8,128)S(1)} copy-done((f32[6,8,16,128]{3,2,1,0:T(8,128)S(1)}, f32[6,8,16,128]{3,2,1,0:T(8,128)}, u32[]{:S(2)}) %copy-start) | copy-done | bytes 393240
  1.0 0.0 copy-start.1
  1.0 1.4 %copy-done.1 = f32[8,192,192]{2,1,0:T(8,128)S(1)} copy-done((f32[8,192,192]{2,1,0:T(8,128)S(1)}, f32[8,192,192]{2,1,0:T(8,128)}, u32[]{:S(2)}) %copy-start.1) | copy-done | bytes 1179672
  2.4 0.0 copy-start.3
  2.4 0.7 %copy-done.3 = s32[64]{0:T(128)S(1)} copy-done((s32[64]{0:T(128)S(1)}, s32[64]{0:T(128)}, u32[]{:S(2)}) %copy-start.3) | copy-done | bytes 280
  3.1 0.0 copy-start.2
  3.1 1.7 %first_kernel.1 = (f32[6,8,16,128]{3,2,1,0:T(8,128)S(1)}, bf16[8,192,192]{2,1,0:T(8,128)(2,1)S(1)}, bf16[8,192,192]{2,1,0:T(8,128)(2,1)S(1)}, f32[6,16,128]{2,1,...) custom-call(f32[6,8,16,128]{3,2,1,0:T(8,128)S(1)} %copy-done, ...), custom_call_target="tpu_custom_call" | custom-call | tf_op jit(solution)/shard_map/first_kernel/pallas_call | solution.py:297
  4.8 1.7 %collective-permute-start = (f32[6,16,128]{2,1,0:T(8,128)S(1)}, f32[6,16,128]{2,1,0:T(8,128)S(1)}, u32[]{:S(2)}, u32[]{:S(2)}) collective-permute-start(f32[6,16,128]{2,1,0:T(8,128)S(1)} %get-tuple-element.27), channel_id=1, source_target_pairs={{0,8},{16,24},{32,40},{48,56},{64,72},{80,88},{96,104},{112,120},{... | collective-permute-start | bytes 147464 | tf_op jit(solution)/shard_map/ppermute | solution.py:312
  6.6 6.9 %collective-permute-start.1 = (f32[6,16,128]{2,1,0:T(8,128)S(1)}, f32[6,16,128]{2,1,0:T(8,128)S(1)}, u32[]{:S(2)}, u32[]{:S(2)}) collective-permute-start(f32[6,16,128]{2,1,0:T(8,128)S(1)} %get-tuple-element.28), channel_id=1, source_target_pairs={{8,16},{24,32},{40,48},{56,64},{72,80},{88,96},{104,112},{120,128}... | collective-permute-start | bytes 147464 | tf_op jit(solution)/shard_map/ppermute | solution.py:312
  13.4 1.2 %collective-permute-start.2 = (f32[6,8,128]{2,1,0:T(8,128)S(1)}, f32[6,8,128]{2,1,0:T(8,128)S(1)}, u32[]{:S(2)}, u32[]{:S(2)}) collective-permute-start(f32[6,8,128]{2,1,0:T(8,128)S(1)} %get-tuple-element.29), channel_id=1, source_target_pairs={{0,1},{2,3},{4,5},{6,7},{1,0},{3,2},{5,4},{7,6},{8,9},{10,11},{12,... | collective-permute-start | bytes 73736 | tf_op jit(solution)/shard_map/ppermute | solution.py:312
  14.7 0.0 collective-permute-start.3
  14.7 0.8 %collective-permute-done.2.y_near_in = f32[6,8,128]{2,1,0:T(8,128)S(1)} collective-permute-done((f32[6,8,128]{2,1,0:T(8,128)S(1)}, f32[6,8,128]{2,1,0:T(8,128)S(1)}, u32[]{:S(2)}, u32[]{:S(2)}) %collective-permute-start.2) | collective-permute-done | bytes 24608 | tf_op jit(solution)/shard_map/ppermute | solution.py:312
  15.5 3.6 %collective-permute-done.3.y_far_in = f32[6,8,128]{2,1,0:T(8,128)S(1)} collective-permute-done((f32[6,8,128]{2,1,0:T(8,128)S(1)}, f32[6,8,128]{2,1,0:T(8,128)S(1)}, u32[]{:S(2)}, u32[]{:S(2)}) %collective-permute-start.3) | collective-permute-done | bytes 24608 | tf_op jit(solution)/shard_map/ppermute | solution.py:312
  19.1 0.0 collective-permute-done.x_near_in
  19.1 0.0 collective-permute-done.1.x_far_in
  19.1 0.0 copy-done.4
  19.1 0.0 copy-done.2
  19.1 2.1 %second_kernel.1 = (f32[6,8,16,128]{3,2,1,0:T(8,128)S(1)}, f32[6,4,8,128]{3,2,1,0:T(8,128)S(1)}, f32[6,4,8,128]{3,2,1,0:T(8,128)S(1)}, f32[8,16,128]{2,1,0:T(8,1...) custom-call(f32[8]{0:T(128)S(1)} %copy-done.4, ...), custom_call_target="tpu_custom_call" | custom-call | tf_op jit(solution)/shard_map/second_kernel/pallas_call | solution.py:297
  21.3 0.1 collective-permute-start.4
  21.4 1.4 %collective-permute-start.5 = (f32[6,8,128]{2,1,0:T(8,128)S(1)}, f32[6,8,128]{2,1,0:T(8,128)S(1)}, u32[]{:S(2)}, u32[]{:S(2)}) collective-permute-start(f32[6,8,128]{2,1,0:T(8,128)S(1)} %get-tuple-element.38), channel_id=1, source_target_pairs={{8,16},{24,32},{40,48},{56,64},{72,80},{88,96},{104,112},{120,128}... | collective-permute-start | bytes 73736 | tf_op jit(solution)/shard_map/ppermute | solution.py:312
  22.8 1.6 %collective-permute-start.6 = (f32[6,4,128]{2,1,0:T(4,128)S(1)}, f32[6,4,128]{2,1,0:T(4,128)S(1)}, u32[]{:S(2)}, u32[]{:S(2)}) collective-permute-start(f32[6,4,128]{2,1,0:T(4,128)S(1)} %get-tuple-element.39), channel_id=1, source_target_pairs={{0,1},{2,3},{4,5},{6,7},{1,0},{3,2},{5,4},{7,6},{8,9},{10,11},{12,... | collective-permute-start | bytes 36872 | tf_op jit(solution)/shard_map/ppermute | solution.py:312
  24.4 0.0 collective-permute-start.7
  24.4 0.8 %collective-permute-done.6.y_near_in = f32[6,4,128]{2,1,0:T(4,128)S(1)} collective-permute-done((f32[6,4,128]{2,1,0:T(4,128)S(1)}, f32[6,4,128]{2,1,0:T(4,128)S(1)}, u32[]{:S(2)}, u32[]{:S(2)}) %collective-permute-start.6) | collective-permute-done | bytes 12320 | tf_op jit(solution)/shard_map/ppermute | solution.py:312
  25.2 3.5 %collective-permute-done.7.y_far_in = f32[6,4,128]{2,1,0:T(4,128)S(1)} collective-permute-done((f32[6,4,128]{2,1,0:T(4,128)S(1)}, f32[6,4,128]{2,1,0:T(4,128)S(1)}, u32[]{:S(2)}, u32[]{:S(2)}) %collective-permute-start.7) | collective-permute-done | bytes 12320 | tf_op jit(solution)/shard_map/ppermute | solution.py:312
  28.7 0.0 collective-permute-done.4.x_near_in
  28.7 0.0 collective-permute-done.5.x_far_in
  28.7 1.1 %third_kernel.1 = (f32[6,4,8,128]{3,2,1,0:T(8,128)S(1)}, f32[6,8,128]{2,1,0:T(8,128)S(1)}, f32[6,8,128]{2,1,0:T(8,128)S(1)}, f32[6,4,128]{2,1,0:T(4,128)S(1)}, f32[6,4,128]{2,1,0:T(4,128)S(1)}) custom-call(s32[1,64]{1,0:T(1,128)S(1)} %bitcast.3, f32[6,4,8,128]{3,2,1,0:T(8,128)S(1)} %get-tuple-element.34.b1, f32[6,4,8,128]{3,2,1,0:T(8,128)S(1)} %get-tuple-element.35.x1a, ...), custom_call_target="tpu_custom_call" | custom-call | tf_op jit(solution)/shard_map/third_kernel/pallas_call | solution.py:297
  29.8 0.1 collective-permute-start.8
  29.9 2.2 %collective-permute-start.9 = (f32[6,8,128]{2,1,0:T(8,128)S(1)}, f32[6,8,128]{2,1,0:T(8,128)S(1)}, u32[]{:S(2)}, u32[]{:S(2)}) collective-permute-start(f32[6,8,128]{2,1,0:T(8,128)S(1)} %get-tuple-element.44), channel_id=1, source_target_pairs={{8,16},{24,32},{40,48},{56,64},{72,80},{88,96},{104,112},{120,128}... | collective-permute-start | bytes 73736 | tf_op jit(solution)/shard_map/ppermute | solution.py:312
  32.1 0.7 %collective-permute-start.10 = (f32[6,4,128]{2,1,0:T(4,128)S(1)}, f32[6,4,128]{2,1,0:T(4,128)S(1)}, u32[]{:S(2)}, u32[]{:S(2)}) collective-permute-start(f32[6,4,128]{2,1,0:T(4,128)S(1)} %get-tuple-element.45), channel_id=1, source_target_pairs={{0,1},{2,3},{4,5},{6,7},{1,0},{3,2},{5,4},{7,6},{8,9},{10,11},{12,... | collective-permute-start | bytes 36872 | tf_op jit(solution)/shard_map/ppermute | solution.py:312
  32.8 0.0 collective-permute-start.11
  32.8 1.6 %middle_kernel.1.y0 = f32[6,8,16,128]{3,2,1,0:T(8,128)S(1)} custom-call(s32[1,64]{1,0:T(1,128)S(1)} %bitcast.4, f32[6,8,16,128]{3,2,1,0:T(8,128)S(1)} %get-tuple-element.26.x0, f32[6,8,16,128]{3,2,1,0:T(8,128)S(1)} %get-tuple-element.33.r0, bf16[8,192,192]{2,1,0:T(8,128)(2,1)S(1)} %get-tuple-element.31.high, bf16[8,192,192]{2,1,0:T(8,128)(2,1)S(1)} %get-tuple-element.32.low), custom_call_target="tpu_custom_call" | custom-call | tf_op jit(solution)/shard_map/middle_kernel/pallas_call | solution.py:297
  34.4 0.0 collective-permute-done.10.y_near_in
  34.4 2.7 %collective-permute-done.11.y_far_in = f32[6,4,128]{2,1,0:T(4,128)S(1)} collective-permute-done((f32[6,4,128]{2,1,0:T(4,128)S(1)}, f32[6,4,128]{2,1,0:T(4,128)S(1)}, u32[]{:S(2)}, u32[]{:S(2)}) %collective-permute-start.11) | collective-permute-done | bytes 12320 | tf_op jit(solution)/shard_map/ppermute | solution.py:312
  37.1 0.0 collective-permute-done.8.x_near_in
  37.1 0.0 collective-permute-done.9.x_far_in
  37.1 2.6 %last_kernel.1 = f32[6,8,16,128]{3,2,1,0:T(8,128)} custom-call(s32[1,64]{1,0:T(1,128)S(1)} %bitcast.5, f32[6,8,16,128]{3,2,1,0:T(8,128)S(1)} %middle_kernel.1.y0, f32[6,4,8,128]{3,2,1,0:T(8,128)S(1)} %get-tuple-element.41.x1, f32[8,16,128]{2,1,0:T(8,128)S(1)} %get-tuple-element.42.sigma0, f32[6,8,128]{2,1,0:T(8,128)S(1)} %collective-permute-done.8.x_near_in, ...), custom_call_target="tpu_custom_call" | custom-call | tf_op jit(solution)/shard_map/last_kernel/pallas_call | solution.py:297
Async XLA Ops:
  0.0 19.1 %copy-start.4 = (f32[8]{0:T(128)S(1)}, f32[8]{0:T(128)}, u32[]{:S(2)}) copy-start(f32[8]{0:T(128)} %conductivity.1) | copy-start | bytes 100
  0.0 1.0 %copy-start = (f32[6,8,16,128]{3,2,1,0:T(8,128)S(1)}, f32[6,8,16,128]{3,2,1,0:T(8,128)}, u32[]{:S(2)}) copy-start(f32[6,8,16,128]{3,2,1,0:T(8,128)} %source.3) | copy-start | bytes 1179652
  1.0 1.4 %copy-start.1 = (f32[8,192,192]{2,1,0:T(8,128)S(1)}, f32[8,192,192]{2,1,0:T(8,128)}, u32[]{:S(2)}) copy-start(f32[8,192,192]{2,1,0:T(8,128)} %inverses.1) | copy-start | bytes 3538948
  2.4 0.7 %copy-start.3 = (s32[64]{0:T(128)S(1)}, s32[64]{0:T(128)}, u32[]{:S(2)}) copy-start(s32[64]{0:T(128)} %param.8) | copy-start | bytes 772
  3.1 16.1 %copy-start.2 = (s32[8,16,128]{2,1,0:T(8,128)S(1)}, s32[8,16,128]{2,1,0:T(8,128)}, u32[]{:S(2)}) copy-start(s32[8,16,128]{2,1,0:T(8,128)} %classes.1) | copy-start | bytes 196612
  4.8 14.3 %collective-permute-start = (f32[6,16,128]{2,1,0:T(8,128)S(1)}, f32[6,16,128]{2,1,0:T(8,128)S(1)}, u32[]{:S(2)}, u32[]{:S(2)}) collective-permute-start(f32[6,16,128]{2,1,0:T(8,128)S(1)} %get-tuple-element.27), channel_id=1, source_target_pairs={{0,8},{16,24},{32,40},{48,56},{64,72},{80,88},{96,104},{112,120},{... | collective-permute-start | bytes 147464 | tf_op jit(solution)/shard_map/ppermute | solution.py:312
  6.6 12.6 %collective-permute-start.1 = (f32[6,16,128]{2,1,0:T(8,128)S(1)}, f32[6,16,128]{2,1,0:T(8,128)S(1)}, u32[]{:S(2)}, u32[]{:S(2)}) collective-permute-start(f32[6,16,128]{2,1,0:T(8,128)S(1)} %get-tuple-element.28), channel_id=1, source_target_pairs={{8,16},{24,32},{40,48},{56,64},{72,80},{88,96},{104,112},{120,128}... | collective-permute-start | bytes 147464 | tf_op jit(solution)/shard_map/ppermute | solution.py:312
  13.4 2.1 %collective-permute-start.2 = (f32[6,8,128]{2,1,0:T(8,128)S(1)}, f32[6,8,128]{2,1,0:T(8,128)S(1)}, u32[]{:S(2)}, u32[]{:S(2)}) collective-permute-start(f32[6,8,128]{2,1,0:T(8,128)S(1)} %get-tuple-element.29), channel_id=1, source_target_pairs={{0,1},{2,3},{4,5},{6,7},{1,0},{3,2},{5,4},{7,6},{8,9},{10,11},{12,... | collective-permute-start | bytes 73736 | tf_op jit(solution)/shard_map/ppermute | solution.py:312
  14.7 4.5 %collective-permute-start.3 = (f32[6,8,128]{2,1,0:T(8,128)S(1)}, f32[6,8,128]{2,1,0:T(8,128)S(1)}, u32[]{:S(2)}, u32[]{:S(2)}) collective-permute-start(f32[6,8,128]{2,1,0:T(8,128)S(1)} %get-tuple-element.30), channel_id=1, source_target_pairs={{1,2},{3,4},{5,6},{7,0},{2,1},{4,3},{6,5},{0,7},{9,10},{11,12},{13... | collective-permute-start | bytes 73736 | tf_op jit(solution)/shard_map/ppermute | solution.py:312
  21.3 7.4 %collective-permute-start.4 = (f32[6,8,128]{2,1,0:T(8,128)S(1)}, f32[6,8,128]{2,1,0:T(8,128)S(1)}, u32[]{:S(2)}, u32[]{:S(2)}) collective-permute-start(f32[6,8,128]{2,1,0:T(8,128)S(1)} %get-tuple-element.37), channel_id=1, source_target_pairs={{0,8},{16,24},{32,40},{48,56},{64,72},{80,88},{96,104},{112,120},{... | collective-permute-start | bytes 73736 | tf_op jit(solution)/shard_map/ppermute | solution.py:312
  21.4 7.4 %collective-permute-start.5 = (f32[6,8,128]{2,1,0:T(8,128)S(1)}, f32[6,8,128]{2,1,0:T(8,128)S(1)}, u32[]{:S(2)}, u32[]{:S(2)}) collective-permute-start(f32[6,8,128]{2,1,0:T(8,128)S(1)} %get-tuple-element.38), channel_id=1, source_target_pairs={{8,16},{24,32},{40,48},{56,64},{72,80},{88,96},{104,112},{120,128}... | collective-permute-start | bytes 73736 | tf_op jit(solution)/shard_map/ppermute | solution.py:312
  22.8 2.4 %collective-permute-start.6 = (f32[6,4,128]{2,1,0:T(4,128)S(1)}, f32[6,4,128]{2,1,0:T(4,128)S(1)}, u32[]{:S(2)}, u32[]{:S(2)}) collective-permute-start(f32[6,4,128]{2,1,0:T(4,128)S(1)} %get-tuple-element.39), channel_id=1, source_target_pairs={{0,1},{2,3},{4,5},{6,7},{1,0},{3,2},{5,4},{7,6},{8,9},{10,11},{12,... | collective-permute-start | bytes 36872 | tf_op jit(solution)/shard_map/ppermute | solution.py:312
  24.4 4.3 %collective-permute-start.7 = (f32[6,4,128]{2,1,0:T(4,128)S(1)}, f32[6,4,128]{2,1,0:T(4,128)S(1)}, u32[]{:S(2)}, u32[]{:S(2)}) collective-permute-start(f32[6,4,128]{2,1,0:T(4,128)S(1)} %get-tuple-element.40), channel_id=1, source_target_pairs={{1,2},{3,4},{5,6},{7,0},{2,1},{4,3},{6,5},{0,7},{9,10},{11,12},{13... | collective-permute-start | bytes 36872 | tf_op jit(solution)/shard_map/ppermute | solution.py:312
  29.8 7.3 %collective-permute-start.8 = (f32[6,8,128]{2,1,0:T(8,128)S(1)}, f32[6,8,128]{2,1,0:T(8,128)S(1)}, u32[]{:S(2)}, u32[]{:S(2)}) collective-permute-start(f32[6,8,128]{2,1,0:T(8,128)S(1)} %get-tuple-element.43), channel_id=1, source_target_pairs={{0,8},{16,24},{32,40},{48,56},{64,72},{80,88},{96,104},{112,120},{... | collective-permute-start | bytes 73736 | tf_op jit(solution)/shard_map/ppermute | solution.py:312
  29.9 7.2 %collective-permute-start.9 = (f32[6,8,128]{2,1,0:T(8,128)S(1)}, f32[6,8,128]{2,1,0:T(8,128)S(1)}, u32[]{:S(2)}, u32[]{:S(2)}) collective-permute-start(f32[6,8,128]{2,1,0:T(8,128)S(1)} %get-tuple-element.44), channel_id=1, source_target_pairs={{8,16},{24,32},{40,48},{56,64},{72,80},{88,96},{104,112},{120,128}... | collective-permute-start | bytes 73736 | tf_op jit(solution)/shard_map/ppermute | solution.py:312
  32.1 2.3 %collective-permute-start.10 = (f32[6,4,128]{2,1,0:T(4,128)S(1)}, f32[6,4,128]{2,1,0:T(4,128)S(1)}, u32[]{:S(2)}, u32[]{:S(2)}) collective-permute-start(f32[6,4,128]{2,1,0:T(4,128)S(1)} %get-tuple-element.45), channel_id=1, source_target_pairs={{0,1},{2,3},{4,5},{6,7},{1,0},{3,2},{5,4},{7,6},{8,9},{10,11},{12,... | collective-permute-start | bytes 36872 | tf_op jit(solution)/shard_map/ppermute | solution.py:312
  32.8 4.3 %collective-permute-start.11 = (f32[6,4,128]{2,1,0:T(4,128)S(1)}, f32[6,4,128]{2,1,0:T(4,128)S(1)}, u32[]{:S(2)}, u32[]{:S(2)}) collective-permute-start(f32[6,4,128]{2,1,0:T(4,128)S(1)} %get-tuple-element.46), channel_id=1, source_target_pairs={{1,2},{3,4},{5,6},{7,0},{2,1},{4,3},{6,5},{0,7},{9,10},{11,12},{13... | collective-permute-start | bytes 36872 | tf_op jit(solution)/shard_map/ppermute | solution.py:312

commit v2 on v1

--- a/solution.py
+++ b/solution.py
@@ -114,23 +114,47 @@
     return lambda c, x: blocker.inverse(total[c * 32 + x * 8 : c * 32 + x * 8 + 8])
 
 
-def first_kernel(source, depth, inverses, x0, high, low, x_near, x_far, y_near, y_far, columns):
+def first_kernel(
+    source_hbm, depth_hbm, inverses_hbm, x0, b0, high, low, layers, y_near, x_near, y_far, x_far,
+    source, depth, inverses, columns, done,
+):
+    copies = [
+        pltpu.make_async_copy(source_hbm, source, done.at[0]),
+        pltpu.make_async_copy(depth_hbm, depth, done.at[1]),
+    ]
+    for index in range(8):
+        copies.append(pltpu.make_async_copy(inverses_hbm.at[index], inverses.at[index], done.at[2 + index]))
+    for copy in copies:
+        copy.start()
     blocker = Blocker(64)
+    split = split_index((16, 128))
+    copies[0].wait()
+
+    def get(c, x):
+        v = take_lanes(source[c, x], split)
+        b0[c, x] = v
+        return v
+
+    fine_columns(blocker, get, store_columns(columns))
+    copies[1].wait()
+    layers[0:1, :] = fine_layers(depth)
+    layers[1:2, 0:128] = coarse_layers(depth)
     for index in range(8):
+        copies[2 + index].wait()
         m = inverses[index]
         m_high = m.astype(BF16)
         high[index] = m_high
         low[index] = (m - m_high.astype(F32)).astype(BF16)
-    split = split_index((16, 128))
-    fine_columns(blocker, lambda c, x: take_lanes(source[c, x], split), store_columns(columns))
 
     def put(c, x, t, v):
         x0[c, x, 8 * t : 8 * t + 8, :] = v
 
-    fine_smooth(blocker, columns, high, low, fine_layers(depth), put)
+    fine_smooth(blocker, columns, high, low, layers[0:1, :], put)
     for c in range(6):
         x_near[c], x_far[c] = near_far("gx", x0[c, 0], x0[c, 7])
-        y_near[c], y_far[c] = near_far("gy", x0[c, :, 0, :], x0[c, :, 15, :])
+        y_near[c, 0:8], y_far[c, 0:8] = near_far("gy", x0[c, :, 0, :], x0[c, :, 15, :])
+        y_near[c, 8:16] = y_near[c, 0:8]
+        y_far[c, 8:16] = y_far[c, 0:8]
 
 
 def around(u, y_before, y_after, half, other, keep, row):
@@ -151,8 +175,8 @@
 
 
 def second_kernel(
-    conductivity, source, classes, depth, x0, x_near_in, x_far_in, y_near_in, y_far_in, high, low,
-    r0, b1, x1, sigma0, sigma1, x_near, x_far, y_near, y_far, rows, columns,
+    conductivity, classes, b0, layers, x0, y_near_in, x_near_in, y_far_in, x_far_in, high, low,
+    r0, b1, x1, sigma0, sigma1, y_near, x_near, y_far, x_far, rows, columns,
 ):
     x_halo = [before_after("gx", x_near_in[c], x_far_in[c]) for c in range(6)]
     y_halo = [before_after("gy", y_near_in[c], y_far_in[c]) for c in range(6)]
@@ -184,38 +208,40 @@
                     )
                     beside = beside + (x0[comp, x - 1] if x > 0 else x_halo[comp][0])
                     beside = beside + (x0[comp, x + 1] if x < 7 else x_halo[comp][1])
-                    rest = take_lanes(source[comp, x], split) - (6.0 * u - beside + sigma * turn)
+                    rest = b0[comp, x] - (6.0 * u - beside + sigma * turn)
                     r0[comp, x] = rest
                     sums[comp] = rest if sums[comp] is None else sums[comp] + rest
             sums[6] = sigma if sums[6] is None else sums[6] + sigma
         for c in range(6):
             b1[c, xx] = restrict(sums[c], xx * 7 + c)
         sigma1[xx] = restrict(sums[6], xx * 7 + 6)
-    result = coarse_smooth(Blocker(32), columns, lambda c, x: b1[c, x], high, low, coarse_layers(depth))
-    store_coarse(result, x1, x_near, x_far, y_near, y_far)
-
-
-def store_coarse(result, x1, x_near, x_far, y_near, y_far):
+    result = coarse_smooth(Blocker(32), columns, lambda c, x: b1[c, x], high, low, layers[1:2, 0:128])
+    store_coarse(result, x1, y_near, x_near, y_far, x_far)
+
+
+def store_coarse(result, x1, y_near, x_near, y_far, x_far):
     for c in range(6):
         for x in range(4):
             x1[c, x] = result(c, x)
         x_near[c], x_far[c] = near_far("gx", x1[c, 0], x1[c, 3])
-        y_near[c], y_far[c] = near_far("gy", x1[c, :, 0, :], x1[c, :, 7, :])
-
-
-def middle_kernel(depth, x0, r0, high, low, y0, columns):
+        y_near[c, 0:4], y_far[c, 0:4] = near_far("gy", x1[c, :, 0, :], x1[c, :, 7, :])
+        y_near[c, 4:8] = y_near[c, 0:4]
+        y_far[c, 4:8] = y_far[c, 0:4]
+
+
+def middle_kernel(layers, x0, r0, high, low, y0, columns):
     blocker = Blocker(64)
     fine_columns(blocker, lambda c, x: r0[c, x], store_columns(columns))
 
     def put(c, x, t, v):
         y0[c, x, 8 * t : 8 * t + 8, :] = x0[c, x, 8 * t : 8 * t + 8, :] + v
 
-    fine_smooth(blocker, columns, high, low, fine_layers(depth), put)
+    fine_smooth(blocker, columns, high, low, layers[0:1, :], put)
 
 
 def third_kernel(
-    depth, b1, x1a, sigma1, x_near_in, x_far_in, y_near_in, y_far_in, high, low,
-    x1, x_near, x_far, y_near, y_far, columns,
+    layers, b1, x1a, sigma1, y_near_in, x_near_in, y_far_in, x_far_in, high, low,
+    x1, y_near, x_near, y_far, x_far, columns,
 ):
     x_halo = [before_after("gx", x_near_in[c], x_far_in[c]) for c in range(6)]
     y_halo = [before_after("gy", y_near_in[c], y_far_in[c]) for c in range(6)]
@@ -231,12 +257,12 @@
         beside = beside + (x1a[c, x + 1] if x < 3 else x_halo[c][1])
         return b1[c, x] - ((6.0 * u - beside) * 0.25 + sigma1[x] * turn)
 
-    more = coarse_smooth(Blocker(32), columns, residual, high, low, coarse_layers(depth))
-    store_coarse(lambda c, x: x1a[c, x] + more(c, x), x1, x_near, x_far, y_near, y_far)
+    more = coarse_smooth(Blocker(32), columns, residual, high, low, layers[1:2, 0:128])
+    store_coarse(lambda c, x: x1a[c, x] + more(c, x), x1, y_near, x_near, y_far, x_far)
 
 
 def last_kernel(
-    depth, y0, x1, sigma0, x_near_in, x_far_in, y_near_in, y_far_in, high, low, out, coarse, image, base, columns
+    layers, y0, x1, sigma0, y_near_in, x_near_in, y_far_in, x_far_in, high, low, out, coarse, image, base, columns
 ):
     x_halo = [before_after("gx", x_near_in[c], x_far_in[c]) for c in range(6)]
     y_halo = [before_after("gy", y_near_in[c], y_far_in[c]) for c in range(6)]
@@ -287,35 +313,36 @@
         part = slice(8 * t, 8 * t + 8)
         out[c, x, part, :] = take_lanes(y0[c, x, part, :] + base[c, x // 2, part, :] - v, join)
 
-    fine_smooth(blocker, columns, high, low, fine_layers(depth), put)
-
-
-def call(kernel, outs, args, scratch, scalars=0, outside=1, last=False):
+    fine_smooth(blocker, columns, high, low, layers[0:1, :], put)
+
+
+def call(kernel, outs, args, scratch, spaces=(), last=False):
     vmem = pl.BlockSpec(memory_space=pltpu.VMEM)
-    smem = pl.BlockSpec(memory_space=pltpu.SMEM)
-    args = list(args[:outside]) + [pltpu.with_memory_space_constraint(arg, pltpu.VMEM) for arg in args[outside:]]
+    own = len(spaces)
+    args = [pltpu.with_memory_space_constraint(arg, space) for arg, space in zip(args, spaces)] + [pltpu.with_memory_space_constraint(arg, pltpu.VMEM) for arg in args[own:]]
     return pl.pallas_call(
         kernel,
         out_shape=[jax.ShapeDtypeStruct(*out) if last else pltpu.VMEM(*out) for out in outs],
-        in_specs=[smem] * scalars + [vmem] * (len(args) - scalars),
+        in_specs=[pl.BlockSpec(memory_space=space) for space in spaces] + [vmem] * (len(args) - own),
         out_specs=[vmem] * len(outs),
-        scratch_shapes=[pltpu.VMEM(shape, F32) for shape in scratch],
+        scratch_shapes=scratch,
         compiler_params=pltpu.CompilerParams(vmem_limit_bytes=12 << 20),
         name=kernel.__name__,
     )(*args)
 
 
-def exchange(x_near, x_far, y_near, y_far):
+def exchange(y_near, x_near, y_far, x_far):
     def swapped(array, axis, first):
         size = lax.axis_size(axis)
-        pairs = [(i, (i + 1) % size) for i in range(first, size, 2)]
-        return lax.ppermute(array, axis, pairs + [(j, i) for i, j in pairs])
+        pairs = [(i, i + 1) for i in range(first, size - 1, 2)]
+        alone = [(i, i) for i in (0, size - 1) if first == 1]
+        return lax.ppermute(array, axis, pairs + [(j, i) for i, j in pairs] + alone)
 
     y_near = swapped(y_near, "gy", 0)
     x_near = swapped(x_near, "gx", 0)
     y_far = swapped(y_far, "gy", 1)
     x_far = swapped(x_far, "gx", 1)
-    return x_near, x_far, y_near, y_far
+    return y_near, x_near, y_far, x_far
 
 
 def near_far(axis, first, last):
@@ -332,36 +359,46 @@
 
 
 def per_device(source, cell_class, class_conductivity, layer_of_depth, inverses):
-    depth = layer_of_depth.reshape(1, 64)
     fine = ((6, 8, 16, 128), F32)
     coarse = ((6, 4, 8, 128), F32)
     matrices = ((8, 192, 192), BF16)
-    fine_faces = [((6, 16, 128), F32)] * 2 + [((6, 8, 128), F32)] * 2
-    coarse_faces = [((6, 8, 128), F32)] * 2 + [((6, 4, 128), F32)] * 2
-
-    x0, high, low, *faces = call(
-        first_kernel, [fine, matrices, matrices] + fine_faces, (source, depth, inverses), [(192, 512)], outside=3
+    fine_faces = [((6, 16, 128), F32)] * 4
+    coarse_faces = [((6, 8, 128), F32)] * 4
+    columns = pltpu.VMEM((192, 512), F32)
+    coarse_columns = pltpu.VMEM((192, 128), F32)
+
+    x0, b0, high, low, layers, *faces = call(
+        first_kernel,
+        [fine, fine, matrices, matrices, ((8, 256), jnp.int32)] + fine_faces,
+        (source, layer_of_depth.reshape(1, 64), inverses),
+        [
+            pltpu.VMEM(source.shape, F32),
+            pltpu.VMEM((1, 64), jnp.int32),
+            pltpu.VMEM(inverses.shape, F32),
+            columns,
+            pltpu.SemaphoreType.DMA((10,)),
+        ],
+        spaces=(pltpu.HBM,) * 3,
     )
     halos = exchange(*faces)
     r0, b1, x1a, sigma0, sigma1, *faces = call(
         second_kernel,
         [fine, coarse, coarse, ((8, 16, 128), F32), ((4, 8, 128), F32)] + coarse_faces,
-        (class_conductivity, source, cell_class, depth, x0, *halos, high, low),
-        [(28, 16, 128), (192, 128)],
-        scalars=1,
-        outside=4,
+        (class_conductivity, cell_class, b0, layers, x0, *halos, high, low),
+        [pltpu.VMEM((28, 16, 128), F32), coarse_columns],
+        spaces=(pltpu.SMEM, pltpu.VMEM),
     )
     halos = exchange(*faces)
-    (y0,) = call(middle_kernel, [fine], (depth, x0, r0, high, low), [(192, 512)])
+    (y0,) = call(middle_kernel, [fine], (layers, x0, r0, high, low), [columns])
     x1, *faces = call(
-        third_kernel, [coarse] + coarse_faces, (depth, b1, x1a, sigma1, *halos, high, low), [(192, 128)]
+        third_kernel, [coarse] + coarse_faces, (layers, b1, x1a, sigma1, *halos, high, low), [coarse_columns]
     )
     halos = exchange(*faces)
     (out,) = call(
         last_kernel,
         [fine],
-        (depth, y0, x1, sigma0, *halos, high, low),
-        [(6, 6, 8, 128), (6, 8, 16, 128), (6, 4, 16, 128), (192, 512)],
+        (layers, y0, x1, sigma0, *halos, high, low),
+        [pltpu.VMEM((6, 6, 8, 128), F32), pltpu.VMEM(*fine), pltpu.VMEM((6, 4, 16, 128), F32), columns],
         last=True,
     )
     return out

time: 39.8 us -> 46 us (1.16)
  the two profiles are of different devices: /device:TPU:25 before, /device:TPU:7 now
where the time goes in v2:
time: 46 us; the launch traced here: 45.7 us
  starting transfers between devices  31 us (67%)
  Pallas kernels  11.8 us (26%)
  waiting for transfers between devices  2.63 us (6%)
    ppermute x12, starting transfers between devices, swapped(): return lax.ppermute(array, axis, pairs + [(j, i) for i, j in pairs] + alone)  31 us
    pallas_call x5, Pallas kernels, call(): pl.pallas_call(kernel, out_shape=[jax.ShapeDtypeStruct(*out) if last else...  11.8 us
    ppermute x12, waiting for transfers between devices, swapped(): return lax.ppermute(array, axis, pairs + [(j, i) for i, j in pairs] + alone)  2.63 us
  transfers between devices with their start and end apart: 12, of which 2 were waited for; matrix products, arithmetic and copies ran while one was open for 0% of the time, Pallas kernels for 3%

profile of v2, /device:TPU:7, one launch (start us, length us, event | category | flops | bytes accessed | tf_op | source)
XLA Modules:
  0.0 45.7 jit_solution(9813526481384927053)
XLA Ops:
  0.0 0.0 copy-start.1
  0.0 0.0 copy-start
  0.0 4.6 %first_kernel.1 = (f32[6,8,16,128]{3,2,1,0:T(8,128)S(1)}, f32[6,8,16,128]{3,2,1,0:T(8,128)S(1)}, bf16[8,192,192]{2,1,0:T(8,128)(2,1)S(1)}, bf16[8,192,192]{2,1,0...) custom-call(f32[6,8,16,128]{3,2,1,0:T(8,128)} %source_hbm.1, ...), custom_call_target="tpu_custom_call" | custom-call | tf_op jit(solution)/shard_map/first_kernel/pallas_call | solution.py:323
  4.6 0.8 %collective-permute-start = (f32[6,16,128]{2,1,0:T(8,128)S(1)}, f32[6,16,128]{2,1,0:T(8,128)S(1)}, u32[]{:S(2)}, u32[]{:S(2)}) collective-permute-start(f32[6,16,128]{2,1,0:T(8,128)S(1)} %get-tuple-element.31), channel_id=1, source_target_pairs={{0,1},{2,3},{4,5},{6,7},{1,0},{3,2},{5,4},{7,6},{8,9},{10,11},{12,... | collective-permute-start | bytes 147464 | tf_op jit(solution)/shard_map/ppermute | solution.py:339
  5.4 1.7 %collective-permute-start.1 = (f32[6,16,128]{2,1,0:T(8,128)S(1)}, f32[6,16,128]{2,1,0:T(8,128)S(1)}, u32[]{:S(2)}, u32[]{:S(2)}) collective-permute-start(f32[6,16,128]{2,1,0:T(8,128)S(1)} %get-tuple-element.32), channel_id=1, source_target_pairs={{0,8},{16,24},{32,40},{48,56},{64,72},{80,88},{96,104},{112,120},{... | collective-permute-start | bytes 147464 | tf_op jit(solution)/shard_map/ppermute | solution.py:339
  7.0 3.4 %collective-permute-start.2 = (f32[6,16,128]{2,1,0:T(8,128)S(1)}, f32[6,16,128]{2,1,0:T(8,128)S(1)}, u32[]{:S(2)}, u32[]{:S(2)}) collective-permute-start(f32[6,16,128]{2,1,0:T(8,128)S(1)} %get-tuple-element.33), channel_id=1, source_target_pairs={{1,2},{3,4},{5,6},{2,1},{4,3},{6,5},{0,0},{7,7},{9,10},{11,12},{13... | collective-permute-start | bytes 147464 | tf_op jit(solution)/shard_map/ppermute | solution.py:339
  10.5 6.8 %collective-permute-start.3 = (f32[6,16,128]{2,1,0:T(8,128)S(1)}, f32[6,16,128]{2,1,0:T(8,128)S(1)}, u32[]{:S(2)}, u32[]{:S(2)}) collective-permute-start(f32[6,16,128]{2,1,0:T(8,128)S(1)} %get-tuple-element.34), channel_id=1, source_target_pairs={{8,16},{24,32},{40,48},{56,64},{72,80},{88,96},{104,112},{120,128}... | collective-permute-start | bytes 147464 | tf_op jit(solution)/shard_map/ppermute | solution.py:339
  17.3 0.0 collective-permute-done.y_near_in
  17.3 0.0 collective-permute-done.1.x_near_in
  17.3 0.0 collective-permute-done.2.y_far_in
  17.3 1.4 %collective-permute-done.3.x_far_in = f32[6,16,128]{2,1,0:T(8,128)S(1)} collective-permute-done((f32[6,16,128]{2,1,0:T(8,128)S(1)}, f32[6,16,128]{2,1,0:T(8,128)S(1)}, u32[]{:S(2)}, u32[]{:S(2)}) %collective-permute-start.3) | collective-permute-done | bytes 49184 | tf_op jit(solution)/shard_map/ppermute | solution.py:339
  18.8 0.0 copy-done.1
  18.8 0.0 copy-done
  18.8 2.0 %second_kernel.1 = (f32[6,8,16,128]{3,2,1,0:T(8,128)S(1)}, f32[6,4,8,128]{3,2,1,0:T(8,128)S(1)}, f32[6,4,8,128]{3,2,1,0:T(8,128)S(1)}, f32[8,16,128]{2,1,0:T(8,1...) custom-call(f32[8]{0:T(128)S(1)} %copy-done.1, ...), custom_call_target="tpu_custom_call" | custom-call | tf_op jit(solution)/shard_map/second_kernel/pallas_call | solution.py:323
  20.8 0.1 collective-permute-start.4
  20.9 0.1 collective-permute-start.5
  21.0 3.5 %collective-permute-start.6 = (f32[6,8,128]{2,1,0:T(8,128)S(1)}, f32[6,8,128]{2,1,0:T(8,128)S(1)}, u32[]{:S(2)}, u32[]{:S(2)}) collective-permute-start(f32[6,8,128]{2,1,0:T(8,128)S(1)} %get-tuple-element.43), channel_id=1, source_target_pairs={{1,2},{3,4},{5,6},{2,1},{4,3},{6,5},{0,0},{7,7},{9,10},{11,12},{13... | collective-permute-start | bytes 73736 | tf_op jit(solution)/shard_map/ppermute | solution.py:339
  24.5 5.5 %collective-permute-start.7 = (f32[6,8,128]{2,1,0:T(8,128)S(1)}, f32[6,8,128]{2,1,0:T(8,128)S(1)}, u32[]{:S(2)}, u32[]{:S(2)}) collective-permute-start(f32[6,8,128]{2,1,0:T(8,128)S(1)} %get-tuple-element.44), channel_id=1, source_target_pairs={{8,16},{24,32},{40,48},{56,64},{72,80},{88,96},{104,112},{120,128}... | collective-permute-start | bytes 73736 | tf_op jit(solution)/shard_map/ppermute | solution.py:339
  30.0 0.0 collective-permute-done.4.y_near_in
  30.0 0.0 collective-permute-done.5.x_near_in
  30.0 0.0 collective-permute-done.6.y_far_in
  30.0 1.2 %collective-permute-done.7.x_far_in = f32[6,8,128]{2,1,0:T(8,128)S(1)} collective-permute-done((f32[6,8,128]{2,1,0:T(8,128)S(1)}, f32[6,8,128]{2,1,0:T(8,128)S(1)}, u32[]{:S(2)}, u32[]{:S(2)}) %collective-permute-start.7) | collective-permute-done | bytes 24608 | tf_op jit(solution)/shard_map/ppermute | solution.py:339
  31.2 1.1 %third_kernel.1 = (f32[6,4,8,128]{3,2,1,0:T(8,128)S(1)}, f32[6,8,128]{2,1,0:T(8,128)S(1)}, f32[6,8,128]{2,1,0:T(8,128)S(1)}, f32[6,8,128]{2,1,0:T(8,128)S(1)}, f32[6,8,128]{2,1,0:T(8,128)S(1)}) custom-call(s32[8,256]{1,0:T(8,128)S(1)} %get-tuple-element.28.layers, f32[6,4,8,128]{3,2,1,0:T(8,128)S(1)} %get-tuple-element.38.b1, ...), custom_call_target="tpu_custom_call" | custom-call | tf_op jit(solution)/shard_map/third_kernel/pallas_call | solution.py:323
  32.2 0.1 collective-permute-start.8
  32.3 0.1 collective-permute-start.9
  32.4 3.5 %collective-permute-start.10 = (f32[6,8,128]{2,1,0:T(8,128)S(1)}, f32[6,8,128]{2,1,0:T(8,128)S(1)}, u32[]{:S(2)}, u32[]{:S(2)}) collective-permute-start(f32[6,8,128]{2,1,0:T(8,128)S(1)} %get-tuple-element.49), channel_id=1, source_target_pairs={{1,2},{3,4},{5,6},{2,1},{4,3},{6,5},{0,0},{7,7},{9,10},{11,12},{13... | collective-permute-start | bytes 73736 | tf_op jit(solution)/shard_map/ppermute | solution.py:339
  36.0 5.5 %collective-permute-start.11 = (f32[6,8,128]{2,1,0:T(8,128)S(1)}, f32[6,8,128]{2,1,0:T(8,128)S(1)}, u32[]{:S(2)}, u32[]{:S(2)}) collective-permute-start(f32[6,8,128]{2,1,0:T(8,128)S(1)} %get-tuple-element.50), channel_id=1, source_target_pairs={{8,16},{24,32},{40,48},{56,64},{72,80},{88,96},{104,112},{120,128}... | collective-permute-start | bytes 73736 | tf_op jit(solution)/shard_map/ppermute | solution.py:339
  41.5 1.6 %middle_kernel.1.y0 = f32[6,8,16,128]{3,2,1,0:T(8,128)S(1)} custom-call(s32[8,256]{1,0:T(8,128)S(1)} %get-tuple-element.28.layers, f32[6,8,16,128]{3,2,1,0:T(8,128)S(1)} %get-tuple-element.29.x0, f32[6,8,16,128]{3,2,1,0:T(8,128)S(1)} %get-tuple-element.37.r0, bf16[8,192,192]{2,1,0:T(8,128)(2,1)S(1)} %get-tuple-element.35.high, ...), custom_call_target="tpu_custom_call" | custom-call | tf_op jit(solution)/shard_map/middle_kernel/pallas_call | solution.py:323
  43.0 0.0 collective-permute-done.8.y_near_in
  43.0 0.0 collective-permute-done.9.x_near_in
  43.1 0.0 collective-permute-done.10.y_far_in
  43.1 0.0 collective-permute-done.11.x_far_in
  43.1 2.6 %last_kernel.1 = f32[6,8,16,128]{3,2,1,0:T(8,128)} custom-call(s32[8,256]{1,0:T(8,128)S(1)} %get-tuple-element.28.layers, f32[6,8,16,128]{3,2,1,0:T(8,128)S(1)} %middle_kernel.1.y0, f32[6,4,8,128]{3,2,1,0:T(8,128)S(1)} %get-tuple-element.45.x1, f32[8,16,128]{2,1,0:T(8,128)S(1)} %get-tuple-element.46.sigma0, ...), custom_call_target="tpu_custom_call" | custom-call | tf_op jit(solution)/shard_map/last_kernel/pallas_call | solution.py:323
Async XLA Ops:
  0.0 18.8 %copy-start.1 = (f32[8]{0:T(128)S(1)}, f32[8]{0:T(128)}, u32[]{:S(2)}) copy-start(f32[8]{0:T(128)} %conductivity.1) | copy-start | bytes 100
  0.0 18.8 %copy-start = (s32[8,16,128]{2,1,0:T(8,128)S(1)}, s32[8,16,128]{2,1,0:T(8,128)}, u32[]{:S(2)}) copy-start(s32[8,16,128]{2,1,0:T(8,128)} %classes.1) | copy-start | bytes 196612
  4.6 12.7 %collective-permute-start = (f32[6,16,128]{2,1,0:T(8,128)S(1)}, f32[6,16,128]{2,1,0:T(8,128)S(1)}, u32[]{:S(2)}, u32[]{:S(2)}) collective-permute-start(f32[6,16,128]{2,1,0:T(8,128)S(1)} %get-tuple-element.31), channel_id=1, source_target_pairs={{0,1},{2,3},{4,5},{6,7},{1,0},{3,2},{5,4},{7,6},{8,9},{10,11},{12,... | collective-permute-start | bytes 147464 | tf_op jit(solution)/shard_map/ppermute | solution.py:339
  5.4 12.0 %collective-permute-start.1 = (f32[6,16,128]{2,1,0:T(8,128)S(1)}, f32[6,16,128]{2,1,0:T(8,128)S(1)}, u32[]{:S(2)}, u32[]{:S(2)}) collective-permute-start(f32[6,16,128]{2,1,0:T(8,128)S(1)} %get-tuple-element.32), channel_id=1, source_target_pairs={{0,8},{16,24},{32,40},{48,56},{64,72},{80,88},{96,104},{112,120},{... | collective-permute-start | bytes 147464 | tf_op jit(solution)/shard_map/ppermute | solution.py:339
  7.0 10.3 %collective-permute-start.2 = (f32[6,16,128]{2,1,0:T(8,128)S(1)}, f32[6,16,128]{2,1,0:T(8,128)S(1)}, u32[]{:S(2)}, u32[]{:S(2)}) collective-permute-start(f32[6,16,128]{2,1,0:T(8,128)S(1)} %get-tuple-element.33), channel_id=1, source_target_pairs={{1,2},{3,4},{5,6},{2,1},{4,3},{6,5},{0,0},{7,7},{9,10},{11,12},{13... | collective-permute-start | bytes 147464 | tf_op jit(solution)/shard_map/ppermute | solution.py:339
  10.5 8.3 %collective-permute-start.3 = (f32[6,16,128]{2,1,0:T(8,128)S(1)}, f32[6,16,128]{2,1,0:T(8,128)S(1)}, u32[]{:S(2)}, u32[]{:S(2)}) collective-permute-start(f32[6,16,128]{2,1,0:T(8,128)S(1)} %get-tuple-element.34), channel_id=1, source_target_pairs={{8,16},{24,32},{40,48},{56,64},{72,80},{88,96},{104,112},{120,128}... | collective-permute-start | bytes 147464 | tf_op jit(solution)/shard_map/ppermute | solution.py:339
  20.8 9.2 %collective-permute-start.4 = (f32[6,8,128]{2,1,0:T(8,128)S(1)}, f32[6,8,128]{2,1,0:T(8,128)S(1)}, u32[]{:S(2)}, u32[]{:S(2)}) collective-permute-start(f32[6,8,128]{2,1,0:T(8,128)S(1)} %get-tuple-element.41), channel_id=1, source_target_pairs={{0,1},{2,3},{4,5},{6,7},{1,0},{3,2},{5,4},{7,6},{8,9},{10,11},{12,... | collective-permute-start | bytes 73736 | tf_op jit(solution)/shard_map/ppermute | solution.py:339
  20.9 9.1 %collective-permute-start.5 = (f32[6,8,128]{2,1,0:T(8,128)S(1)}, f32[6,8,128]{2,1,0:T(8,128)S(1)}, u32[]{:S(2)}, u32[]{:S(2)}) collective-permute-start(f32[6,8,128]{2,1,0:T(8,128)S(1)} %get-tuple-element.42), channel_id=1, source_target_pairs={{0,8},{16,24},{32,40},{48,56},{64,72},{80,88},{96,104},{112,120},{... | collective-permute-start | bytes 73736 | tf_op jit(solution)/shard_map/ppermute | solution.py:339
  21.0 9.0 %collective-permute-start.6 = (f32[6,8,128]{2,1,0:T(8,128)S(1)}, f32[6,8,128]{2,1,0:T(8,128)S(1)}, u32[]{:S(2)}, u32[]{:S(2)}) collective-permute-start(f32[6,8,128]{2,1,0:T(8,128)S(1)} %get-tuple-element.43), channel_id=1, source_target_pairs={{1,2},{3,4},{5,6},{2,1},{4,3},{6,5},{0,0},{7,7},{9,10},{11,12},{13... | collective-permute-start | bytes 73736 | tf_op jit(solution)/shard_map/ppermute | solution.py:339
  24.5 6.7 %collective-permute-start.7 = (f32[6,8,128]{2,1,0:T(8,128)S(1)}, f32[6,8,128]{2,1,0:T(8,128)S(1)}, u32[]{:S(2)}, u32[]{:S(2)}) collective-permute-start(f32[6,8,128]{2,1,0:T(8,128)S(1)} %get-tuple-element.44), channel_id=1, source_target_pairs={{8,16},{24,32},{40,48},{56,64},{72,80},{88,96},{104,112},{120,128}... | collective-permute-start | bytes 73736 | tf_op jit(solution)/shard_map/ppermute | solution.py:339
  32.2 10.8 %collective-permute-start.8 = (f32[6,8,128]{2,1,0:T(8,128)S(1)}, f32[6,8,128]{2,1,0:T(8,128)S(1)}, u32[]{:S(2)}, u32[]{:S(2)}) collective-permute-start(f32[6,8,128]{2,1,0:T(8,128)S(1)} %get-tuple-element.47), channel_id=1, source_target_pairs={{0,1},{2,3},{4,5},{6,7},{1,0},{3,2},{5,4},{7,6},{8,9},{10,11},{12,... | collective-permute-start | bytes 73736 | tf_op jit(solution)/shard_map/ppermute | solution.py:339
  32.3 10.7 %collective-permute-start.9 = (f32[6,8,128]{2,1,0:T(8,128)S(1)}, f32[6,8,128]{2,1,0:T(8,128)S(1)}, u32[]{:S(2)}, u32[]{:S(2)}) collective-permute-start(f32[6,8,128]{2,1,0:T(8,128)S(1)} %get-tuple-element.48), channel_id=1, source_target_pairs={{0,8},{16,24},{32,40},{48,56},{64,72},{80,88},{96,104},{112,120},{... | collective-permute-start | bytes 73736 | tf_op jit(solution)/shard_map/ppermute | solution.py:339
  32.4 10.6 %collective-permute-start.10 = (f32[6,8,128]{2,1,0:T(8,128)S(1)}, f32[6,8,128]{2,1,0:T(8,128)S(1)}, u32[]{:S(2)}, u32[]{:S(2)}) collective-permute-start(f32[6,8,128]{2,1,0:T(8,128)S(1)} %get-tuple-element.49), channel_id=1, source_target_pairs={{1,2},{3,4},{5,6},{2,1},{4,3},{6,5},{0,0},{7,7},{9,10},{11,12},{13... | collective-permute-start | bytes 73736 | tf_op jit(solution)/shard_map/ppermute | solution.py:339
  36.0 7.1 %collective-permute-start.11 = (f32[6,8,128]{2,1,0:T(8,128)S(1)}, f32[6,8,128]{2,1,0:T(8,128)S(1)}, u32[]{:S(2)}, u32[]{:S(2)}) collective-permute-start(f32[6,8,128]{2,1,0:T(8,128)S(1)} %get-tuple-element.50), channel_id=1, source_target_pairs={{8,16},{24,32},{40,48},{56,64},{72,80},{88,96},{104,112},{120,128}... | collective-permute-start | bytes 73736 | tf_op jit(solution)/shard_map/ppermute | solution.py:339

commit v3 on v2

--- a/solution.py
+++ b/solution.py
@@ -115,15 +115,14 @@
 
 
 def first_kernel(
-    source_hbm, depth_hbm, inverses_hbm, x0, b0, high, low, layers, y_near, x_near, y_far, x_far,
+    source_hbm, depth_hbm, inverses_hbm, x0, b0, high, low, layers, x_near, x_far, y_near, y_far,
     source, depth, inverses, columns, done,
 ):
     copies = [
         pltpu.make_async_copy(source_hbm, source, done.at[0]),
         pltpu.make_async_copy(depth_hbm, depth, done.at[1]),
+        pltpu.make_async_copy(inverses_hbm, inverses, done.at[2]),
     ]
-    for index in range(8):
-        copies.append(pltpu.make_async_copy(inverses_hbm.at[index], inverses.at[index], done.at[2 + index]))
     for copy in copies:
         copy.start()
     blocker = Blocker(64)
@@ -139,8 +138,8 @@
     copies[1].wait()
     layers[0:1, :] = fine_layers(depth)
     layers[1:2, 0:128] = coarse_layers(depth)
+    copies[2].wait()
     for index in range(8):
-        copies[2 + index].wait()
         m = inverses[index]
         m_high = m.astype(BF16)
         high[index] = m_high
@@ -174,18 +173,17 @@
     return jnp.where(j < 32, jnp.maximum(j + 31, 32), jnp.minimum(j - 31, 31)), (j != 0) & (j != 63)
 
 
-def second_kernel(
-    conductivity, classes, b0, layers, x0, y_near_in, x_near_in, y_far_in, x_far_in, high, low,
-    r0, b1, x1, sigma0, sigma1, y_near, x_near, y_far, x_far, rows, columns,
-):
-    x_halo = [before_after("gx", x_near_in[c], x_far_in[c]) for c in range(6)]
-    y_halo = [before_after("gy", y_near_in[c], y_far_in[c]) for c in range(6)]
+def pair_index(shape):
+    j = lane_of(shape)
+    return ((j & 31) << 1) | ((j >> 5) & 1)
+
+
+def own_kernel(conductivity, classes, b0, x0, r0, b1, sigma0, sigma1, rows):
     shape = (16, 128)
     split = split_index(shape)
     other, keep = fine_other(shape)
     row = row_of(shape)
-    j = lane_of(shape)
-    pair = ((j & 31) << 1) | ((j >> 5) & 1)
+    pair = pair_index(shape)
 
     def restrict(v, slot):
         rows[slot] = take_lanes(v + pltpu.roll(v, 64, 1), pair)
@@ -203,11 +201,11 @@
                 re = x0[c, x]
                 im = x0[c + 3, x]
                 for comp, u, turn in ((c, re, -im), (c + 3, im, re)):
-                    beside = around(
-                        u, y_halo[comp][0][x : x + 1], y_halo[comp][1][x : x + 1], 64, other, keep, row
-                    )
-                    beside = beside + (x0[comp, x - 1] if x > 0 else x_halo[comp][0])
-                    beside = beside + (x0[comp, x + 1] if x < 7 else x_halo[comp][1])
+                    beside = around(u, 0.0, 0.0, 64, other, keep, row)
+                    if x > 0:
+                        beside = beside + x0[comp, x - 1]
+                    if x < 7:
+                        beside = beside + x0[comp, x + 1]
                     rest = b0[comp, x] - (6.0 * u - beside + sigma * turn)
                     r0[comp, x] = rest
                     sums[comp] = rest if sums[comp] is None else sums[comp] + rest
@@ -215,11 +213,39 @@
         for c in range(6):
             b1[c, xx] = restrict(sums[c], xx * 7 + c)
         sigma1[xx] = restrict(sums[6], xx * 7 + 6)
+
+
+def second_kernel(
+    own_b1, layers, x_near_in, x_far_in, y_near_in, y_far_in, high, low,
+    b1, x1, x_near, x_far, y_near, y_far, rows, columns,
+):
+    shape = (16, 128)
+    pair = pair_index(shape)
+    narrow = (8, 128)
+    row = row_of(narrow)
+    for c in range(6):
+        added = []
+        for side, v in enumerate(before_after("gx", x_near_in[c], x_far_in[c])):
+            slot = 2 * c + side
+            rows[slot] = take_lanes(v + pltpu.roll(v, 64, 1), pair)
+            added.append((rows[slot, pl.ds(0, 8, stride=2), :] + rows[slot, pl.ds(1, 8, stride=2), :]) * 0.125)
+        edges = []
+        for v in before_after("gy", y_near_in[c, 0:8], y_far_in[c, 0:8]):
+            v = take_lanes(v + pltpu.roll(v, 64, 1), pair[0:8])
+            edges.append((v + pltpu.roll(v, 7, 0)) * 0.125)
+        for x in range(4):
+            v = own_b1[c, x] + jnp.where(row == 0, edges[0][2 * x : 2 * x + 1], 0.0)
+            v = v + jnp.where(row == 7, edges[1][2 * x : 2 * x + 1], 0.0)
+            if x == 0:
+                v = v + added[0]
+            if x == 3:
+                v = v + added[1]
+            b1[c, x] = v
     result = coarse_smooth(Blocker(32), columns, lambda c, x: b1[c, x], high, low, layers[1:2, 0:128])
-    store_coarse(result, x1, y_near, x_near, y_far, x_far)
-
-
-def store_coarse(result, x1, y_near, x_near, y_far, x_far):
+    store_coarse(result, x1, x_near, x_far, y_near, y_far)
+
+
+def store_coarse(result, x1, x_near, x_far, y_near, y_far):
     for c in range(6):
         for x in range(4):
             x1[c, x] = result(c, x)
@@ -229,9 +255,22 @@
         y_far[c, 4:8] = y_far[c, 0:4]
 
 
-def middle_kernel(layers, x0, r0, high, low, y0, columns):
+def middle_kernel(layers, x0, r0, x_near_in, x_far_in, y_near_in, y_far_in, high, low, y0, columns):
     blocker = Blocker(64)
-    fine_columns(blocker, lambda c, x: r0[c, x], store_columns(columns))
+    row = row_of((16, 128))
+    x_halo = [before_after("gx", x_near_in[c], x_far_in[c]) for c in range(6)]
+    y_halo = [before_after("gy", y_near_in[c, 0:8], y_far_in[c, 0:8]) for c in range(6)]
+
+    def get(c, x):
+        v = r0[c, x] + jnp.where(row == 0, y_halo[c][0][x : x + 1], 0.0)
+        v = v + jnp.where(row == 15, y_halo[c][1][x : x + 1], 0.0)
+        if x == 0:
+            v = v + x_halo[c][0]
+        if x == 7:
+            v = v + x_halo[c][1]
+        return v
+
+    fine_columns(blocker, get, store_columns(columns))
 
     def put(c, x, t, v):
         y0[c, x, 8 * t : 8 * t + 8, :] = x0[c, x, 8 * t : 8 * t + 8, :] + v
@@ -240,8 +279,8 @@
 
 
 def third_kernel(
-    layers, b1, x1a, sigma1, y_near_in, x_near_in, y_far_in, x_far_in, high, low,
-    x1, y_near, x_near, y_far, x_far, columns,
+    layers, y0, b1, x1a, sigma1, x_near_in, x_far_in, y_near_in, y_far_in, high, low,
+    x1, x_near, x_far, y_near, y_far, columns,
 ):
     x_halo = [before_after("gx", x_near_in[c], x_far_in[c]) for c in range(6)]
     y_halo = [before_after("gy", y_near_in[c], y_far_in[c]) for c in range(6)]
@@ -258,60 +297,82 @@
         return b1[c, x] - ((6.0 * u - beside) * 0.25 + sigma1[x] * turn)
 
     more = coarse_smooth(Blocker(32), columns, residual, high, low, layers[1:2, 0:128])
-    store_coarse(lambda c, x: x1a[c, x] + more(c, x), x1, y_near, x_near, y_far, x_far)
-
-
-def last_kernel(
-    layers, y0, x1, sigma0, y_near_in, x_near_in, y_far_in, x_far_in, high, low, out, coarse, image, base, columns
-):
-    x_halo = [before_after("gx", x_near_in[c], x_far_in[c]) for c in range(6)]
-    y_halo = [before_after("gy", y_near_in[c], y_far_in[c]) for c in range(6)]
+    store_coarse(lambda c, x: x1a[c, x] + more(c, x), x1, x_near, x_far, y_near, y_far)
+
+
+def self_index(shape):
+    k = lane_of(shape) & 63
+    return ((k & 1) << 5) | (k >> 1)
+
+
+def prolong_kernel(x1, sigma0, y0, image, base, coarse, rows):
     shape = (8, 128)
     j = lane_of(shape)
     row = row_of(shape)
     k = j & 63
-    self_index = ((k & 1) << 5) | (k >> 1)
     beyond = jnp.where(j < 64, k - 1, k + 1)
     inside = (beyond >= 0) & (beyond < 64)
     beyond = jnp.clip(beyond, 0, 63)
     next_index = ((beyond & 1) << 5) | (beyond >> 1)
-
-    for c in range(6):
-        coarse[c, 0] = take_lanes(x_halo[c][0], self_index)
-        coarse[c, 5] = take_lanes(x_halo[c][1], self_index)
+    own_index = self_index(shape)
+
+    for c in range(6):
         for x in range(4):
-            coarse[c, x + 1] = take_lanes(x1[c, x], self_index)
+            coarse[c, x] = take_lanes(x1[c, x], own_index)
     for xx in range(4):
         for c in range(3):
             own = {}
             for comp in (c, c + 3):
-                v = coarse[comp, xx + 1]
+                v = coarse[comp, xx]
                 beside = jnp.where(inside, take_lanes(x1[comp, xx], next_index), 0.0)
-                low_y = take_lanes(jnp.broadcast_to(y_halo[comp][0][xx : xx + 1], shape), self_index)
-                high_y = take_lanes(jnp.broadcast_to(y_halo[comp][1][xx : xx + 1], shape), self_index)
-                before = jnp.where(row == 0, low_y, pltpu.roll(v, 1, 0))
-                after = jnp.where(row == 7, high_y, pltpu.roll(v, 7, 0))
+                before = jnp.where(row == 0, 0.0, pltpu.roll(v, 1, 0))
+                after = jnp.where(row == 7, 0.0, pltpu.roll(v, 7, 0))
                 own[comp] = (v, 3.0 * v - beside, before, after)
+                rows[comp, xx, pl.ds(0, 8, stride=2), :] = v
+                rows[comp, xx, pl.ds(1, 8, stride=2), :] = v
             for half in range(2):
                 x = 2 * xx + half
+                next_x = xx - 1 + 2 * half
                 for parity in range(2):
                     sigma = sigma0[x, pl.ds(parity, 8, stride=2), :]
                     for comp, partner, sign in ((c, c + 3, -1.0), (c + 3, c, 1.0)):
                         v, kept, before, after = own[comp]
-                        turned = kept - coarse[comp, xx + 2 * half] - (before, after)[parity]
-                        value = turned + sign * sigma * own[partner][0]
+                        value = kept - (before, after)[parity] + sign * sigma * own[partner][0]
+                        if 0 <= next_x < 4:
+                            value = value - coarse[comp, next_x]
                         image[comp, x, pl.ds(parity, 8, stride=2), :] = value
-            for comp in (c, c + 3):
-                base[comp, xx, pl.ds(0, 8, stride=2), :] = own[comp][0]
-                base[comp, xx, pl.ds(1, 8, stride=2), :] = own[comp][0]
+                for comp in (c, c + 3):
+                    base[comp, x] = y0[comp, x] + rows[comp, xx]
+
+
+def last_kernel(layers, image, base, x_near_in, x_far_in, y_near_in, y_far_in, high, low, out, rows, columns):
+    shape = (8, 128)
+    own_index = self_index(shape)
+    row = row_of((16, 128))
+    y_halo = []
+    for c in range(6):
+        for side, v in enumerate(before_after("gx", x_near_in[c], x_far_in[c])):
+            v = take_lanes(v, own_index)
+            slot = 2 * c + side
+            rows[slot, pl.ds(0, 8, stride=2), :] = v
+            rows[slot, pl.ds(1, 8, stride=2), :] = v
+        y_halo.append([take_lanes(v, own_index) for v in before_after("gy", y_near_in[c], y_far_in[c])])
+
+    def get(c, x):
+        v = image[c, x] - jnp.where(row == 0, y_halo[c][0][x // 2 : x // 2 + 1], 0.0)
+        v = v - jnp.where(row == 15, y_halo[c][1][x // 2 : x // 2 + 1], 0.0)
+        if x == 0:
+            v = v - rows[2 * c]
+        if x == 7:
+            v = v - rows[2 * c + 1]
+        return v
 
     blocker = Blocker(64)
-    fine_columns(blocker, lambda c, x: image[c, x], store_columns(columns))
+    fine_columns(blocker, get, store_columns(columns))
     join = join_index(shape)
 
     def put(c, x, t, v):
-        part = slice(8 * t, 8 * t + 8)
-        out[c, x, part, :] = take_lanes(y0[c, x, part, :] + base[c, x // 2, part, :] - v, join)
+        out[c, x, 8 * t : 8 * t + 8, :] = take_lanes(base[c, x, 8 * t : 8 * t + 8, :] - v, join)
 
     fine_smooth(blocker, columns, high, low, layers[0:1, :], put)
 
@@ -319,7 +380,7 @@
 def call(kernel, outs, args, scratch, spaces=(), last=False):
     vmem = pl.BlockSpec(memory_space=pltpu.VMEM)
     own = len(spaces)
-    args = [pltpu.with_memory_space_constraint(arg, space) for arg, space in zip(args, spaces)] + [pltpu.with_memory_space_constraint(arg, pltpu.VMEM) for arg in args[own:]]
+    args = [arg if space == pltpu.SMEM else pltpu.with_memory_space_constraint(arg, space) for arg, space in zip(args, spaces)] + [pltpu.with_memory_space_constraint(arg, pltpu.VMEM) for arg in args[own:]]
     return pl.pallas_call(
         kernel,
         out_shape=[jax.ShapeDtypeStruct(*out) if last else pltpu.VMEM(*out) for out in outs],
@@ -331,18 +392,28 @@
     )(*args)
 
 
-def exchange(y_near, x_near, y_far, x_far):
-    def swapped(array, axis, first):
-        size = lax.axis_size(axis)
-        pairs = [(i, i + 1) for i in range(first, size - 1, 2)]
-        alone = [(i, i) for i in (0, size - 1) if first == 1]
-        return lax.ppermute(array, axis, pairs + [(j, i) for i, j in pairs] + alone)
-
-    y_near = swapped(y_near, "gy", 0)
-    x_near = swapped(x_near, "gx", 0)
-    y_far = swapped(y_far, "gy", 1)
-    x_far = swapped(x_far, "gx", 1)
-    return y_near, x_near, y_far, x_far
+def exchange(x_near, x_far, y_near, y_far):
+    nx, ny = lax.axis_size("gx"), lax.axis_size("gy")
+
+    def swapped(array, partner):
+        pairs = [(i * ny + j, partner(i, j)) for i in range(nx) for j in range(ny)]
+        return lax.ppermute(array, ("gx", "gy"), [(a, i * ny + j) for a, (i, j) in pairs])
+
+    def far(i):
+        return i + 1 if i % 2 else i - 1
+
+    def x_far_partner(i, j):
+        return (i, j ^ 1) if i in (0, nx - 1) else (far(i), j)
+
+    def y_far_partner(i, j):
+        return (i ^ 1, j) if j in (0, ny - 1) else (i, far(j))
+
+    return (
+        swapped(x_near, lambda i, j: (i ^ 1, j)),
+        swapped(x_far, x_far_partner),
+        swapped(y_near, lambda i, j: (i, j ^ 1)),
+        swapped(y_far, y_far_partner),
+    )
 
 
 def near_far(axis, first, last):
@@ -376,29 +447,42 @@
             pltpu.VMEM((1, 64), jnp.int32),
             pltpu.VMEM(inverses.shape, F32),
             columns,
-            pltpu.SemaphoreType.DMA((10,)),
+            pltpu.SemaphoreType.DMA((3,)),
         ],
         spaces=(pltpu.HBM,) * 3,
     )
     halos = exchange(*faces)
-    r0, b1, x1a, sigma0, sigma1, *faces = call(
+    r0, own_b1, sigma0, sigma1 = call(
+        own_kernel,
+        [fine, coarse, ((8, 16, 128), F32), ((4, 8, 128), F32)],
+        (class_conductivity, cell_class, b0, x0),
+        [pltpu.VMEM((28, 16, 128), F32)],
+        spaces=(pltpu.SMEM, pltpu.VMEM),
+    )
+    b1, x1a, *faces = call(
         second_kernel,
-        [fine, coarse, coarse, ((8, 16, 128), F32), ((4, 8, 128), F32)] + coarse_faces,
-        (class_conductivity, cell_class, b0, layers, x0, *halos, high, low),
-        [pltpu.VMEM((28, 16, 128), F32), coarse_columns],
-        spaces=(pltpu.SMEM, pltpu.VMEM),
-    )
+        [coarse, coarse] + coarse_faces,
+        (own_b1, layers, *halos, high, low),
+        [pltpu.VMEM((12, 16, 128), F32), coarse_columns],
+    )
+    fine_halos = halos
     halos = exchange(*faces)
-    (y0,) = call(middle_kernel, [fine], (layers, x0, r0, high, low), [columns])
+    (y0,) = call(middle_kernel, [fine], (layers, x0, r0, *fine_halos, high, low), [columns])
     x1, *faces = call(
-        third_kernel, [coarse] + coarse_faces, (layers, b1, x1a, sigma1, *halos, high, low), [coarse_columns]
+        third_kernel, [coarse] + coarse_faces, (layers, y0, b1, x1a, sigma1, *halos, high, low), [coarse_columns]
     )
     halos = exchange(*faces)
+    image, base = call(
+        prolong_kernel,
+        [fine, fine],
+        (x1, sigma0, y0),
+        [pltpu.VMEM((6, 4, 8, 128), F32), pltpu.VMEM((6, 4, 16, 128), F32)],
+    )
     (out,) = call(
         last_kernel,
         [fine],
-        (layers, y0, x1, sigma0, *halos, high, low),
-        [pltpu.VMEM((6, 6, 8, 128), F32), pltpu.VMEM(*fine), pltpu.VMEM((6, 4, 16, 128), F32), columns],
+        (layers, image, base, *halos, high, low),
+        [pltpu.VMEM((12, 16, 128), F32), columns],
         last=True,
     )
     return out

time: 46 us -> 33.3 us (0.72)
  starting transfers between devices: 31 us -> 16.8 us
  Pallas kernels: 11.8 us -> 13.1 us
  waiting for transfers between devices: 2.63 us -> 3.11 us
    ppermute x12, starting transfers between devices: 31 us -> 16.8 us  [swapped(): lax.ppermute(array, ('gx', 'gy'), [(a, i * ny + j) for a, (i, j) in pairs])]
    pallas_call x5 -> x7, Pallas kernels: 11.8 us -> 13.1 us  [call(): pl.pallas_call(kernel, out_shape=[jax.ShapeDtypeStruct(*out) if last else...]
    ppermute x12, waiting for transfers between devices: 2.63 us -> 3.11 us  [swapped(): lax.ppermute(array, ('gx', 'gy'), [(a, i * ny + j) for a, (i, j) in pairs])]
  transfers between devices with their start and end apart: 12 -> 12, of which waited for: 2 -> 4; matrix products, arithmetic and copies ran while one was open for 0% -> 0% of each run, Pallas kernels for 3% -> 12%
where the time goes in v3:
time: 33.3 us; the launch traced here: 33.1 us
  starting transfers between devices  16.8 us (50%)
  Pallas kernels  13.1 us (39%)
  waiting for transfers between devices  3.11 us (9%)
    ppermute x12, starting transfers between devices, swapped(): lax.ppermute(array, ('gx', 'gy'), [(a, i * ny + j) for a, (i, j) in pairs])  16.8 us
    pallas_call x7, Pallas kernels, call(): pl.pallas_call(kernel, out_shape=[jax.ShapeDtypeStruct(*out) if last else...  13.1 us
    ppermute x12, waiting for transfers between devices, swapped(): lax.ppermute(array, ('gx', 'gy'), [(a, i * ny + j) for a, (i, j) in pairs])  3.11 us
  transfers between devices with their start and end apart: 12, of which 4 were waited for; matrix products, arithmetic and copies ran while one was open for 0% of the time, Pallas kernels for 12%

profile of v3, /device:TPU:7, one launch (start us, length us, event | category | flops | bytes accessed | tf_op | source)
XLA Modules:
  0.0 33.1 jit_solution(934470656821674846)
XLA Ops:
  0.0 0.0 copy-start.1
  0.0 0.0 copy-start
  0.0 4.4 %first_kernel.1 = (f32[6,8,16,128]{3,2,1,0:T(8,128)S(1)}, f32[6,8,16,128]{3,2,1,0:T(8,128)S(1)}, bf16[8,192,192]{2,1,0:T(8,128)(2,1)S(1)}, bf16[8,192,192]{2,1,0...) custom-call(f32[6,8,16,128]{3,2,1,0:T(8,128)} %source_hbm.1, ...), custom_call_target="tpu_custom_call" | custom-call | tf_op jit(solution)/shard_map/first_kernel/pallas_call | solution.py:384
  4.4 1.7 %collective-permute-start = (f32[6,16,128]{2,1,0:T(8,128)S(1)}, f32[6,16,128]{2,1,0:T(8,128)S(1)}, u32[]{:S(2)}, u32[]{:S(2)}) collective-permute-start(f32[6,16,128]{2,1,0:T(8,128)S(1)} %get-tuple-element.35), channel_id=1, source_target_pairs={{0,8},{1,9},{2,10},{3,11},{4,12},{5,13},{6,14},{7,15},{8,0},{9,1},... | collective-permute-start | bytes 147464 | tf_op jit(solution)/shard_map/ppermute | solution.py:400
  6.2 4.9 %collective-permute-start.1 = (f32[6,16,128]{2,1,0:T(8,128)S(1)}, f32[6,16,128]{2,1,0:T(8,128)S(1)}, u32[]{:S(2)}, u32[]{:S(2)}) collective-permute-start(f32[6,16,128]{2,1,0:T(8,128)S(1)} %get-tuple-element.36), channel_id=1, source_target_pairs={{0,1},{1,0},{2,3},{3,2},{4,5},{5,4},{6,7},{7,6},{8,16},{9,17},{10,... | collective-permute-start | bytes 147464 | tf_op jit(solution)/shard_map/ppermute | solution.py:400
  11.1 1.2 %collective-permute-start.2 = (f32[6,16,128]{2,1,0:T(8,128)S(1)}, f32[6,16,128]{2,1,0:T(8,128)S(1)}, u32[]{:S(2)}, u32[]{:S(2)}) collective-permute-start(f32[6,16,128]{2,1,0:T(8,128)S(1)} %get-tuple-element.37), channel_id=1, source_target_pairs={{0,1},{1,0},{2,3},{3,2},{4,5},{5,4},{6,7},{7,6},{8,9},{9,8},{10,11... | collective-permute-start | bytes 147464 | tf_op jit(solution)/shard_map/ppermute | solution.py:400
  12.3 1.2 %collective-permute-start.3 = (f32[6,16,128]{2,1,0:T(8,128)S(1)}, f32[6,16,128]{2,1,0:T(8,128)S(1)}, u32[]{:S(2)}, u32[]{:S(2)}) collective-permute-start(f32[6,16,128]{2,1,0:T(8,128)S(1)} %get-tuple-element.38), channel_id=1, source_target_pairs={{0,8},{1,2},{2,1},{3,4},{4,3},{5,6},{6,5},{7,15},{8,0},{9,10},{10,... | collective-permute-start | bytes 147464 | tf_op jit(solution)/shard_map/ppermute | solution.py:400
  13.5 0.0 copy-done.1
  13.5 0.0 copy-done
  13.5 2.1 %own_kernel.1 = (f32[6,8,16,128]{3,2,1,0:T(8,128)S(1)}, f32[6,4,8,128]{3,2,1,0:T(8,128)S(1)}, f32[8,16,128]{2,1,0:T(8,128)S(1)}, f32[4,8,128]{2,1,0:T(8,128)S(1)}) custom-call(f32[8]{0:T(128)S(1)} %copy-done.1, s32[8,16,128]{2,1,0:T(8,128)S(1)} %copy-done, f32[6,8,16,128]{3,2,1,0:T(8,128)S(1)} %get-tuple-element.33.b0, ...), custom_call_target="tpu_custom_call" | custom-call | tf_op jit(solution)/shard_map/own_kernel/pallas_call | solution.py:384
  15.7 0.0 collective-permute-done.x_near_in
  15.7 0.0 collective-permute-done.1.x_far_in
  15.7 0.0 collective-permute-done.2.y_near_in
  15.7 0.3 collective-permute-done.3.y_far_in
  16.0 1.1 %second_kernel.1 = (f32[6,4,8,128]{3,2,1,0:T(8,128)S(1)}, f32[6,4,8,128]{3,2,1,0:T(8,128)S(1)}, f32[6,8,128]{2,1,0:T(8,128)S(1)}, f32[6,8,128]{2,1,0:T(8,128)S(1...) custom-call(f32[6,4,8,128]{3,2,1,0:T(8,128)S(1)} %get-tuple-element.41.own_b1, ...), custom_call_target="tpu_custom_call" | custom-call | tf_op jit(solution)/shard_map/second_kernel/pallas_call | solution.py:384
  17.2 0.1 collective-permute-start.4
  17.3 1.4 %collective-permute-start.5 = (f32[6,8,128]{2,1,0:T(8,128)S(1)}, f32[6,8,128]{2,1,0:T(8,128)S(1)}, u32[]{:S(2)}, u32[]{:S(2)}) collective-permute-start(f32[6,8,128]{2,1,0:T(8,128)S(1)} %get-tuple-element.46), channel_id=1, source_target_pairs={{0,1},{1,0},{2,3},{3,2},{4,5},{5,4},{6,7},{7,6},{8,16},{9,17},{10,... | collective-permute-start | bytes 73736 | tf_op jit(solution)/shard_map/ppermute | solution.py:400
  18.7 1.2 %collective-permute-start.6 = (f32[6,8,128]{2,1,0:T(8,128)S(1)}, f32[6,8,128]{2,1,0:T(8,128)S(1)}, u32[]{:S(2)}, u32[]{:S(2)}) collective-permute-start(f32[6,8,128]{2,1,0:T(8,128)S(1)} %get-tuple-element.47), channel_id=1, source_target_pairs={{0,1},{1,0},{2,3},{3,2},{4,5},{5,4},{6,7},{7,6},{8,9},{9,8},{10,11... | collective-permute-start | bytes 73736 | tf_op jit(solution)/shard_map/ppermute | solution.py:400
  19.9 1.2 %collective-permute-start.7 = (f32[6,8,128]{2,1,0:T(8,128)S(1)}, f32[6,8,128]{2,1,0:T(8,128)S(1)}, u32[]{:S(2)}, u32[]{:S(2)}) collective-permute-start(f32[6,8,128]{2,1,0:T(8,128)S(1)} %get-tuple-element.48), channel_id=1, source_target_pairs={{0,8},{1,2},{2,1},{3,4},{4,3},{5,6},{6,5},{7,15},{8,0},{9,10},{10,... | collective-permute-start | bytes 73736 | tf_op jit(solution)/shard_map/ppermute | solution.py:400
  21.0 1.6 %middle_kernel.1.y0 = f32[6,8,16,128]{3,2,1,0:T(8,128)S(1)} custom-call(s32[8,256]{1,0:T(8,128)S(1)} %get-tuple-element.31.layers, f32[6,8,16,128]{3,2,1,0:T(8,128)S(1)} %get-tuple-element.32.x0, f32[6,8,16,128]{3,2,1,0:T(8,128)S(1)} %get-tuple-element.34.r0, f32[6,16,128]{2,1,0:T(8,128)S(1)} %collective-permute-done.x_near_in, ...), custom_call_target="tpu_custom_call" | custom-call | tf_op jit(solution)/shard_map/middle_kernel/pallas_call | solution.py:384
  22.7 0.0 collective-permute-done.4.x_near_in
  22.7 0.0 collective-permute-done.5.x_far_in
  22.7 0.0 collective-permute-done.6.y_near_in
  22.7 0.6 %collective-permute-done.7.y_far_in = f32[6,8,128]{2,1,0:T(8,128)S(1)} collective-permute-done((f32[6,8,128]{2,1,0:T(8,128)S(1)}, f32[6,8,128]{2,1,0:T(8,128)S(1)}, u32[]{:S(2)}, u32[]{:S(2)}) %collective-permute-start.7) | collective-permute-done | bytes 24608 | tf_op jit(solution)/shard_map/ppermute | solution.py:400
  23.3 1.1 %third_kernel.1 = (f32[6,4,8,128]{3,2,1,0:T(8,128)S(1)}, f32[6,8,128]{2,1,0:T(8,128)S(1)}, f32[6,8,128]{2,1,0:T(8,128)S(1)}, f32[6,8,128]{2,1,0:T(8,128)S(1)}, f32[6,8,128]{2,1,0:T(8,128)S(1)}) custom-call(s32[8,256]{1,0:T(8,128)S(1)} %get-tuple-element.31.layers, f32[6,8,16,128]{3,2,1,0:T(8,128)S(1)} %middle_kernel.1.y0, ...), custom_call_target="tpu_custom_call" | custom-call | tf_op jit(solution)/shard_map/third_kernel/pallas_call | solution.py:384
  24.4 0.3 collective-permute-start.8
  24.7 1.6 %collective-permute-start.9 = (f32[6,8,128]{2,1,0:T(8,128)S(1)}, f32[6,8,128]{2,1,0:T(8,128)S(1)}, u32[]{:S(2)}, u32[]{:S(2)}) collective-permute-start(f32[6,8,128]{2,1,0:T(8,128)S(1)} %get-tuple-element.54), channel_id=1, source_target_pairs={{0,1},{1,0},{2,3},{3,2},{4,5},{5,4},{6,7},{7,6},{8,16},{9,17},{10,... | collective-permute-start | bytes 73736 | tf_op jit(solution)/shard_map/ppermute | solution.py:400
  26.4 0.7 %collective-permute-start.10 = (f32[6,8,128]{2,1,0:T(8,128)S(1)}, f32[6,8,128]{2,1,0:T(8,128)S(1)}, u32[]{:S(2)}, u32[]{:S(2)}) collective-permute-start(f32[6,8,128]{2,1,0:T(8,128)S(1)} %get-tuple-element.55), channel_id=1, source_target_pairs={{0,1},{1,0},{2,3},{3,2},{4,5},{5,4},{6,7},{7,6},{8,9},{9,8},{10,11... | collective-permute-start | bytes 73736 | tf_op jit(solution)/shard_map/ppermute | solution.py:400
  27.0 1.2 %collective-permute-start.11 = (f32[6,8,128]{2,1,0:T(8,128)S(1)}, f32[6,8,128]{2,1,0:T(8,128)S(1)}, u32[]{:S(2)}, u32[]{:S(2)}) collective-permute-start(f32[6,8,128]{2,1,0:T(8,128)S(1)} %get-tuple-element.56), channel_id=1, source_target_pairs={{0,8},{1,2},{2,1},{3,4},{4,3},{5,6},{6,5},{7,15},{8,0},{9,10},{10,... | collective-permute-start | bytes 73736 | tf_op jit(solution)/shard_map/ppermute | solution.py:400
  28.2 0.2 prolong_kernel.1
  28.4 0.0 collective-permute-done.8.x_near_in
  28.5 1.0 %collective-permute-done.9.x_far_in = f32[6,8,128]{2,1,0:T(8,128)S(1)} collective-permute-done((f32[6,8,128]{2,1,0:T(8,128)S(1)}, f32[6,8,128]{2,1,0:T(8,128)S(1)}, u32[]{:S(2)}, u32[]{:S(2)}) %collective-permute-start.9) | collective-permute-done | bytes 24608 | tf_op jit(solution)/shard_map/ppermute | solution.py:400
  29.5 0.0 collective-permute-done.10.y_near_in
  29.5 1.1 %collective-permute-done.11.y_far_in = f32[6,8,128]{2,1,0:T(8,128)S(1)} collective-permute-done((f32[6,8,128]{2,1,0:T(8,128)S(1)}, f32[6,8,128]{2,1,0:T(8,128)S(1)}, u32[]{:S(2)}, u32[]{:S(2)}) %collective-permute-start.11) | collective-permute-done | bytes 24608 | tf_op jit(solution)/shard_map/ppermute | solution.py:400
  30.6 2.5 %last_kernel.1 = f32[6,8,16,128]{3,2,1,0:T(8,128)} custom-call(s32[8,256]{1,0:T(8,128)S(1)} %get-tuple-element.31.layers, f32[6,8,16,128]{3,2,1,0:T(8,128)S(1)} %get-tuple-element.51.image, f32[6,8,16,128]{3,2,1,0:T(8,128)S(1)} %get-tuple-element.52.base, f32[6,8,128]{2,1,0:T(8,128)S(1)} %collective-permute-done.8.x_near_in, ...), custom_call_target="tpu_custom_call" | custom-call | tf_op jit(solution)/shard_map/last_kernel/pallas_call | solution.py:384
Async XLA Ops:
  0.0 13.5 %copy-start.1 = (f32[8]{0:T(128)S(1)}, f32[8]{0:T(128)}, u32[]{:S(2)}) copy-start(f32[8]{0:T(128)} %conductivity.1) | copy-start | bytes 100
  0.0 13.5 %copy-start = (s32[8,16,128]{2,1,0:T(8,128)S(1)}, s32[8,16,128]{2,1,0:T(8,128)}, u32[]{:S(2)}) copy-start(s32[8,16,128]{2,1,0:T(8,128)} %classes.1) | copy-start | bytes 196612
  4.4 11.2 %collective-permute-start = (f32[6,16,128]{2,1,0:T(8,128)S(1)}, f32[6,16,128]{2,1,0:T(8,128)S(1)}, u32[]{:S(2)}, u32[]{:S(2)}) collective-permute-start(f32[6,16,128]{2,1,0:T(8,128)S(1)} %get-tuple-element.35), channel_id=1, source_target_pairs={{0,8},{1,9},{2,10},{3,11},{4,12},{5,13},{6,14},{7,15},{8,0},{9,1},... | collective-permute-start | bytes 147464 | tf_op jit(solution)/shard_map/ppermute | solution.py:400
  6.2 9.5 %collective-permute-start.1 = (f32[6,16,128]{2,1,0:T(8,128)S(1)}, f32[6,16,128]{2,1,0:T(8,128)S(1)}, u32[]{:S(2)}, u32[]{:S(2)}) collective-permute-start(f32[6,16,128]{2,1,0:T(8,128)S(1)} %get-tuple-element.36), channel_id=1, source_target_pairs={{0,1},{1,0},{2,3},{3,2},{4,5},{5,4},{6,7},{7,6},{8,16},{9,17},{10,... | collective-permute-start | bytes 147464 | tf_op jit(solution)/shard_map/ppermute | solution.py:400
  11.1 4.6 %collective-permute-start.2 = (f32[6,16,128]{2,1,0:T(8,128)S(1)}, f32[6,16,128]{2,1,0:T(8,128)S(1)}, u32[]{:S(2)}, u32[]{:S(2)}) collective-permute-start(f32[6,16,128]{2,1,0:T(8,128)S(1)} %get-tuple-element.37), channel_id=1, source_target_pairs={{0,1},{1,0},{2,3},{3,2},{4,5},{5,4},{6,7},{7,6},{8,9},{9,8},{10,11... | collective-permute-start | bytes 147464 | tf_op jit(solution)/shard_map/ppermute | solution.py:400
  12.3 3.7 %collective-permute-start.3 = (f32[6,16,128]{2,1,0:T(8,128)S(1)}, f32[6,16,128]{2,1,0:T(8,128)S(1)}, u32[]{:S(2)}, u32[]{:S(2)}) collective-permute-start(f32[6,16,128]{2,1,0:T(8,128)S(1)} %get-tuple-element.38), channel_id=1, source_target_pairs={{0,8},{1,2},{2,1},{3,4},{4,3},{5,6},{6,5},{7,15},{8,0},{9,10},{10,... | collective-permute-start | bytes 147464 | tf_op jit(solution)/shard_map/ppermute | solution.py:400
  17.2 5.5 %collective-permute-start.4 = (f32[6,8,128]{2,1,0:T(8,128)S(1)}, f32[6,8,128]{2,1,0:T(8,128)S(1)}, u32[]{:S(2)}, u32[]{:S(2)}) collective-permute-start(f32[6,8,128]{2,1,0:T(8,128)S(1)} %get-tuple-element.45), channel_id=1, source_target_pairs={{0,8},{1,9},{2,10},{3,11},{4,12},{5,13},{6,14},{7,15},{8,0},{9,1},... | collective-permute-start | bytes 73736 | tf_op jit(solution)/shard_map/ppermute | solution.py:400
  17.3 5.4 %collective-permute-start.5 = (f32[6,8,128]{2,1,0:T(8,128)S(1)}, f32[6,8,128]{2,1,0:T(8,128)S(1)}, u32[]{:S(2)}, u32[]{:S(2)}) collective-permute-start(f32[6,8,128]{2,1,0:T(8,128)S(1)} %get-tuple-element.46), channel_id=1, source_target_pairs={{0,1},{1,0},{2,3},{3,2},{4,5},{5,4},{6,7},{7,6},{8,16},{9,17},{10,... | collective-permute-start | bytes 73736 | tf_op jit(solution)/shard_map/ppermute | solution.py:400
  18.7 4.0 %collective-permute-start.6 = (f32[6,8,128]{2,1,0:T(8,128)S(1)}, f32[6,8,128]{2,1,0:T(8,128)S(1)}, u32[]{:S(2)}, u32[]{:S(2)}) collective-permute-start(f32[6,8,128]{2,1,0:T(8,128)S(1)} %get-tuple-element.47), channel_id=1, source_target_pairs={{0,1},{1,0},{2,3},{3,2},{4,5},{5,4},{6,7},{7,6},{8,9},{9,8},{10,11... | collective-permute-start | bytes 73736 | tf_op jit(solution)/shard_map/ppermute | solution.py:400
  19.9 3.5 %collective-permute-start.7 = (f32[6,8,128]{2,1,0:T(8,128)S(1)}, f32[6,8,128]{2,1,0:T(8,128)S(1)}, u32[]{:S(2)}, u32[]{:S(2)}) collective-permute-start(f32[6,8,128]{2,1,0:T(8,128)S(1)} %get-tuple-element.48), channel_id=1, source_target_pairs={{0,8},{1,2},{2,1},{3,4},{4,3},{5,6},{6,5},{7,15},{8,0},{9,10},{10,... | collective-permute-start | bytes 73736 | tf_op jit(solution)/shard_map/ppermute | solution.py:400
  24.4 4.0 %collective-permute-start.8 = (f32[6,8,128]{2,1,0:T(8,128)S(1)}, f32[6,8,128]{2,1,0:T(8,128)S(1)}, u32[]{:S(2)}, u32[]{:S(2)}) collective-permute-start(f32[6,8,128]{2,1,0:T(8,128)S(1)} %get-tuple-element.53), channel_id=1, source_target_pairs={{0,8},{1,9},{2,10},{3,11},{4,12},{5,13},{6,14},{7,15},{8,0},{9,1},... | collective-permute-start | bytes 73736 | tf_op jit(solution)/shard_map/ppermute | solution.py:400
  24.7 4.8 %collective-permute-start.9 = (f32[6,8,128]{2,1,0:T(8,128)S(1)}, f32[6,8,128]{2,1,0:T(8,128)S(1)}, u32[]{:S(2)}, u32[]{:S(2)}) collective-permute-start(f32[6,8,128]{2,1,0:T(8,128)S(1)} %get-tuple-element.54), channel_id=1, source_target_pairs={{0,1},{1,0},{2,3},{3,2},{4,5},{5,4},{6,7},{7,6},{8,16},{9,17},{10,... | collective-permute-start | bytes 73736 | tf_op jit(solution)/shard_map/ppermute | solution.py:400
  26.4 3.1 %collective-permute-start.10 = (f32[6,8,128]{2,1,0:T(8,128)S(1)}, f32[6,8,128]{2,1,0:T(8,128)S(1)}, u32[]{:S(2)}, u32[]{:S(2)}) collective-permute-start(f32[6,8,128]{2,1,0:T(8,128)S(1)} %get-tuple-element.55), channel_id=1, source_target_pairs={{0,1},{1,0},{2,3},{3,2},{4,5},{5,4},{6,7},{7,6},{8,9},{9,8},{10,11... | collective-permute-start | bytes 73736 | tf_op jit(solution)/shard_map/ppermute | solution.py:400
  27.0 3.5 %collective-permute-start.11 = (f32[6,8,128]{2,1,0:T(8,128)S(1)}, f32[6,8,128]{2,1,0:T(8,128)S(1)}, u32[]{:S(2)}, u32[]{:S(2)}) collective-permute-start(f32[6,8,128]{2,1,0:T(8,128)S(1)} %get-tuple-element.56), channel_id=1, source_target_pairs={{0,8},{1,2},{2,1},{3,4},{4,3},{5,6},{6,5},{7,15},{8,0},{9,10},{10,... | collective-permute-start | bytes 73736 | tf_op jit(solution)/shard_map/ppermute | solution.py:400

commit v4 on v3

--- a/solution.py
+++ b/solution.py
@@ -71,7 +71,7 @@
 
 def fine_layers(depth_ref):
     v = depth_ref[...]
-    return jnp.concatenate([v, v, v, v], axis=1)
+    return jnp.concatenate([v] * 8, axis=1)
 
 
 def coarse_layers(depth_ref):
@@ -88,14 +88,16 @@
                 put(c * 32 + (x % 4) * 8, ((x // 4) * 2 + t) * 128, blocker.forward(v[8 * t : 8 * t + 8]))
 
 
-def fine_smooth(blocker, columns, high, low, layer, put):
+def fine_smooth(blocker, columns, high, low, layer, put, finish=lambda bx: None):
     for bx in range(2):
-        total = block_product(columns[:, bx * 256 : bx * 256 + 256], high, low, layer) * damping
+        half = slice(bx * 256, bx * 256 + 256)
+        total = block_product(columns[:, half], high, low, layer[:, half]) * damping
         for c in range(6):
             for x in range(4):
                 row = c * 32 + x * 8
                 for t in range(2):
                     put(c, 4 * bx + x, t, blocker.inverse(total[row : row + 8, 128 * t : 128 * t + 128]))
+        finish(bx)
 
 
 def store_columns(columns):
@@ -110,18 +112,27 @@
         for x in range(4):
             row = c * 32 + x * 8
             columns[row : row + 8, :] = blocker.forward(get(c, x))
-    total = block_product(columns[...], high, low, layer) * (damping * 4.0)
+    x = columns[...]
+    x_high = x.astype(BF16)
+    x_low = (x - x_high.astype(F32)).astype(BF16)
+    both = jnp.where(lane_of(x.shape) < 64, x_high.astype(F32), x_low.astype(F32)).astype(BF16)
+    total = jnp.zeros(x.shape, F32)
+    for index in range(high.shape[0]):
+        part = dot(high[index], both) + dot(low[index], both)
+        total = jnp.where(layer == index, part, total)
+    total = (total + pltpu.roll(total, 64, 1)) * (damping * 4.0)
     return lambda c, x: blocker.inverse(total[c * 32 + x * 8 : c * 32 + x * 8 + 8])
 
 
 def first_kernel(
-    source_hbm, depth_hbm, inverses_hbm, x0, b0, high, low, layers, x_near, x_far, y_near, y_far,
-    source, depth, inverses, columns, done,
+    source_hbm, depth_hbm, inverses_hbm, conductivity_hbm, x0, b0, high, low, layers, table, x_near, x_far, y_near, y_far,
+    source, depth, inverses, conductivity, columns, done,
 ):
     copies = [
         pltpu.make_async_copy(source_hbm, source, done.at[0]),
         pltpu.make_async_copy(depth_hbm, depth, done.at[1]),
         pltpu.make_async_copy(inverses_hbm, inverses, done.at[2]),
+        pltpu.make_async_copy(conductivity_hbm, conductivity, done.at[3]),
     ]
     for copy in copies:
         copy.start()
@@ -129,15 +140,17 @@
     split = split_index((16, 128))
     copies[0].wait()
 
-    def get(c, x):
-        v = take_lanes(source[c, x], split)
-        b0[c, x] = v
-        return v
-
-    fine_columns(blocker, get, store_columns(columns))
+    for c in range(6):
+        for x in range(8):
+            b0[c, x] = take_lanes(source[c, x], split)
+    fine_columns(blocker, lambda c, x: b0[c, x], store_columns(columns))
     copies[1].wait()
     layers[0:1, :] = fine_layers(depth)
     layers[1:2, 0:128] = coarse_layers(depth)
+    copies[3].wait()
+    values = jnp.broadcast_to(conductivity[...], (8, 8))
+    own = jnp.where(row_of((8, 8)) == lane_of((8, 8)), values, 0.0)
+    table[...] = jnp.broadcast_to(jnp.sum(own, axis=1, keepdims=True), (8, 128))
     copies[2].wait()
     for index in range(8):
         m = inverses[index]
@@ -178,28 +191,27 @@
     return ((j & 31) << 1) | ((j >> 5) & 1)
 
 
-def own_kernel(conductivity, classes, b0, x0, r0, b1, sigma0, sigma1, rows):
+def own_kernel(classes, table, b0, x0, r0, b1, sigma0, sigma1, rows, sums):
     shape = (16, 128)
     split = split_index(shape)
     other, keep = fine_other(shape)
     row = row_of(shape)
     pair = pair_index(shape)
 
-    def restrict(v, slot):
-        rows[slot] = take_lanes(v + pltpu.roll(v, 64, 1), pair)
-        return (rows[slot, pl.ds(0, 8, stride=2), :] + rows[slot, pl.ds(1, 8, stride=2), :]) * 0.125
-
+    for x in range(8):
+        kind = take_lanes(classes[x], split)
+        sigma = jnp.zeros(shape, F32)
+        for index in range(8):
+            sigma = jnp.where(kind == index, table[index : index + 1, :], sigma)
+        sigma0[x] = sigma
     for xx in range(4):
-        sums = [None] * 7
-        for x in (2 * xx, 2 * xx + 1):
-            kind = take_lanes(classes[x], split)
-            sigma = jnp.zeros(shape, F32)
-            for index in range(8):
-                sigma = jnp.where(kind == index, conductivity[index], sigma)
-            sigma0[x] = sigma
-            for c in range(3):
+        sums[xx * 7 + 6] = sigma0[2 * xx] + sigma0[2 * xx + 1]
+        for c in range(3):
+            total = {}
+            for x in (2 * xx, 2 * xx + 1):
                 re = x0[c, x]
                 im = x0[c + 3, x]
+                sigma = sigma0[x]
                 for comp, u, turn in ((c, re, -im), (c + 3, im, re)):
                     beside = around(u, 0.0, 0.0, 64, other, keep, row)
                     if x > 0:
@@ -208,11 +220,20 @@
                         beside = beside + x0[comp, x + 1]
                     rest = b0[comp, x] - (6.0 * u - beside + sigma * turn)
                     r0[comp, x] = rest
-                    sums[comp] = rest if sums[comp] is None else sums[comp] + rest
-            sums[6] = sigma if sums[6] is None else sums[6] + sigma
-        for c in range(6):
-            b1[c, xx] = restrict(sums[c], xx * 7 + c)
-        sigma1[xx] = restrict(sums[6], xx * 7 + 6)
+                    total[comp] = rest + total[comp] if comp in total else rest
+            for comp in total:
+                sums[xx * 7 + comp] = total[comp]
+    for slot in range(28):
+        v = sums[slot]
+        rows[slot] = take_lanes(v + pltpu.roll(v, 64, 1), pair)
+    for xx in range(4):
+        for c in range(7):
+            slot = xx * 7 + c
+            v = (rows[slot, pl.ds(0, 8, stride=2), :] + rows[slot, pl.ds(1, 8, stride=2), :]) * 0.125
+            if c < 6:
+                b1[c, xx] = v
+            else:
+                sigma1[xx] = v
 
 
 def second_kernel(
@@ -345,7 +366,7 @@
                     base[comp, x] = y0[comp, x] + rows[comp, xx]
 
 
-def last_kernel(layers, image, base, x_near_in, x_far_in, y_near_in, y_far_in, high, low, out, rows, columns):
+def last_kernel(layers, image, base, x_near_in, x_far_in, y_near_in, y_far_in, high, low, out, rows, columns, stage, done):
     shape = (8, 128)
     own_index = self_index(shape)
     row = row_of((16, 128))
@@ -369,23 +390,34 @@
 
     blocker = Blocker(64)
     fine_columns(blocker, get, store_columns(columns))
-    join = join_index(shape)
+    join = join_index((16, 128))
+    copies = []
 
     def put(c, x, t, v):
-        out[c, x, 8 * t : 8 * t + 8, :] = take_lanes(base[c, x, 8 * t : 8 * t + 8, :] - v, join)
-
-    fine_smooth(blocker, columns, high, low, layers[0:1, :], put)
+        stage[c, x, 8 * t : 8 * t + 8, :] = base[c, x, 8 * t : 8 * t + 8, :] - v
+
+    def finish(bx):
+        for c in range(6):
+            for x in range(4 * bx, 4 * bx + 4):
+                stage[c, x] = take_lanes(stage[c, x], join)
+        part = pl.ds(4 * bx, 4)
+        copies.append(pltpu.make_async_copy(stage.at[:, part], out.at[:, part], done.at[bx]))
+        copies[bx].start()
+
+    fine_smooth(blocker, columns, high, low, layers[0:1, :], put, finish)
+    for copy in copies:
+        copy.wait()
 
 
 def call(kernel, outs, args, scratch, spaces=(), last=False):
     vmem = pl.BlockSpec(memory_space=pltpu.VMEM)
     own = len(spaces)
-    args = [arg if space == pltpu.SMEM else pltpu.with_memory_space_constraint(arg, space) for arg, space in zip(args, spaces)] + [pltpu.with_memory_space_constraint(arg, pltpu.VMEM) for arg in args[own:]]
+    args = [pltpu.with_memory_space_constraint(arg, space) for arg, space in zip(args, spaces)] + [pltpu.with_memory_space_constraint(arg, pltpu.VMEM) for arg in args[own:]]
     return pl.pallas_call(
         kernel,
         out_shape=[jax.ShapeDtypeStruct(*out) if last else pltpu.VMEM(*out) for out in outs],
         in_specs=[pl.BlockSpec(memory_space=space) for space in spaces] + [vmem] * (len(args) - own),
-        out_specs=[vmem] * len(outs),
+        out_specs=[pl.BlockSpec(memory_space=pltpu.HBM) if last else vmem] * len(outs),
         scratch_shapes=scratch,
         compiler_params=pltpu.CompilerParams(vmem_limit_bytes=12 << 20),
         name=kernel.__name__,
@@ -438,26 +470,27 @@
     columns = pltpu.VMEM((192, 512), F32)
     coarse_columns = pltpu.VMEM((192, 128), F32)
 
-    x0, b0, high, low, layers, *faces = call(
+    x0, b0, high, low, layers, table, *faces = call(
         first_kernel,
-        [fine, fine, matrices, matrices, ((8, 256), jnp.int32)] + fine_faces,
-        (source, layer_of_depth.reshape(1, 64), inverses),
+        [fine, fine, matrices, matrices, ((8, 512), jnp.int32), ((8, 128), F32)] + fine_faces,
+        (source, layer_of_depth.reshape(1, 64), inverses, class_conductivity.reshape(1, 8)),
         [
             pltpu.VMEM(source.shape, F32),
             pltpu.VMEM((1, 64), jnp.int32),
             pltpu.VMEM(inverses.shape, F32),
+            pltpu.VMEM((1, 8), F32),
             columns,
-            pltpu.SemaphoreType.DMA((3,)),
+            pltpu.SemaphoreType.DMA((4,)),
         ],
-        spaces=(pltpu.HBM,) * 3,
+        spaces=(pltpu.HBM,) * 4,
     )
     halos = exchange(*faces)
     r0, own_b1, sigma0, sigma1 = call(
         own_kernel,
         [fine, coarse, ((8, 16, 128), F32), ((4, 8, 128), F32)],
-        (class_conductivity, cell_class, b0, x0),
-        [pltpu.VMEM((28, 16, 128), F32)],
-        spaces=(pltpu.SMEM, pltpu.VMEM),
+        (cell_class, table, b0, x0),
+        [pltpu.VMEM((28, 16, 128), F32)] * 2,
+        spaces=(pltpu.VMEM,),
     )
     b1, x1a, *faces = call(
         second_kernel,
@@ -482,7 +515,7 @@
         last_kernel,
         [fine],
         (layers, image, base, *halos, high, low),
-        [pltpu.VMEM((12, 16, 128), F32), columns],
+        [pltpu.VMEM((12, 16, 128), F32), columns, pltpu.VMEM(*fine), pltpu.SemaphoreType.DMA((2,))],
         last=True,
     )
     return out

time: 33.3 us -> 31.6 us (0.949)
  Pallas kernels: 13.1 us -> 10.8 us
  waiting for transfers between devices: 3.11 us -> 3.71 us
    pallas_call x7, Pallas kernels: 13.1 us -> 10.8 us  [call(): pl.pallas_call(kernel, out_shape=[jax.ShapeDtypeStruct(*out) if last else...]
    ppermute x12, waiting for transfers between devices: 3.11 us -> 3.71 us  [swapped(): lax.ppermute(array, ('gx', 'gy'), [(a, i * ny + j) for a, (i, j) in pairs])]
  transfers between devices with their start and end apart: 12 -> 12, of which waited for: 4 -> 4; matrix products, arithmetic and copies ran while one was open for 0% -> 0% of each run, Pallas kernels for 12% -> 11%
where the time goes in v4:
time: 31.6 us; the launch traced here: 31.5 us
  starting transfers between devices  16.8 us (53%)
  Pallas kernels  10.8 us (34%)
  waiting for transfers between devices  3.71 us (12%)
    ppermute x12, starting transfers between devices, swapped(): lax.ppermute(array, ('gx', 'gy'), [(a, i * ny + j) for a, (i, j) in pairs])  16.8 us
    pallas_call x7, Pallas kernels, call(): pl.pallas_call(kernel, out_shape=[jax.ShapeDtypeStruct(*out) if last else...  10.8 us
    ppermute x12, waiting for transfers between devices, swapped(): lax.ppermute(array, ('gx', 'gy'), [(a, i * ny + j) for a, (i, j) in pairs])  3.71 us
  transfers between devices with their start and end apart: 12, of which 4 were waited for; matrix products, arithmetic and copies ran while one was open for 0% of the time, Pallas kernels for 11%

profile of v4, /device:TPU:7, one launch (start us, length us, event | category | flops | bytes accessed | tf_op | source)
XLA Modules:
  0.0 31.5 jit_solution(8080373721977180446)
XLA Ops:
  0.0 0.0 copy-start
  0.0 3.1 %first_kernel.1 = (f32[6,8,16,128]{3,2,1,0:T(8,128)S(1)}, f32[6,8,16,128]{3,2,1,0:T(8,128)S(1)}, bf16[8,192,192]{2,1,0:T(8,128)(2,1)S(1)}, bf16[8,192,192]{2,1,0...) custom-call(f32[6,8,16,128]{3,2,1,0:T(8,128)} %source_hbm.1, ...), custom_call_target="tpu_custom_call" | custom-call | tf_op jit(solution)/shard_map/first_kernel/pallas_call | solution.py:416
  3.1 1.7 %collective-permute-start = (f32[6,16,128]{2,1,0:T(8,128)S(1)}, f32[6,16,128]{2,1,0:T(8,128)S(1)}, u32[]{:S(2)}, u32[]{:S(2)}) collective-permute-start(f32[6,16,128]{2,1,0:T(8,128)S(1)} %get-tuple-element.37), channel_id=1, source_target_pairs={{0,8},{1,9},{2,10},{3,11},{4,12},{5,13},{6,14},{7,15},{8,0},{9,1},... | collective-permute-start | bytes 147464 | tf_op jit(solution)/shard_map/ppermute | solution.py:432
  4.9 4.9 %collective-permute-start.1 = (f32[6,16,128]{2,1,0:T(8,128)S(1)}, f32[6,16,128]{2,1,0:T(8,128)S(1)}, u32[]{:S(2)}, u32[]{:S(2)}) collective-permute-start(f32[6,16,128]{2,1,0:T(8,128)S(1)} %get-tuple-element.38), channel_id=1, source_target_pairs={{0,1},{1,0},{2,3},{3,2},{4,5},{5,4},{6,7},{7,6},{8,16},{9,17},{10,... | collective-permute-start | bytes 147464 | tf_op jit(solution)/shard_map/ppermute | solution.py:432
  9.8 1.2 %collective-permute-start.2 = (f32[6,16,128]{2,1,0:T(8,128)S(1)}, f32[6,16,128]{2,1,0:T(8,128)S(1)}, u32[]{:S(2)}, u32[]{:S(2)}) collective-permute-start(f32[6,16,128]{2,1,0:T(8,128)S(1)} %get-tuple-element.39), channel_id=1, source_target_pairs={{0,1},{1,0},{2,3},{3,2},{4,5},{5,4},{6,7},{7,6},{8,9},{9,8},{10,11... | collective-permute-start | bytes 147464 | tf_op jit(solution)/shard_map/ppermute | solution.py:432
  11.0 1.2 %collective-permute-start.3 = (f32[6,16,128]{2,1,0:T(8,128)S(1)}, f32[6,16,128]{2,1,0:T(8,128)S(1)}, u32[]{:S(2)}, u32[]{:S(2)}) collective-permute-start(f32[6,16,128]{2,1,0:T(8,128)S(1)} %get-tuple-element.40), channel_id=1, source_target_pairs={{0,8},{1,2},{2,1},{3,4},{4,3},{5,6},{6,5},{7,15},{8,0},{9,10},{10,... | collective-permute-start | bytes 147464 | tf_op jit(solution)/shard_map/ppermute | solution.py:432
  12.2 0.0 copy-done
  12.2 1.6 %own_kernel.1 = (f32[6,8,16,128]{3,2,1,0:T(8,128)S(1)}, f32[6,4,8,128]{3,2,1,0:T(8,128)S(1)}, f32[8,16,128]{2,1,0:T(8,128)S(1)}, f32[4,8,128]{2,1,0:T(8,128)S(1)}) custom-call(s32[8,16,128]{2,1,0:T(8,128)S(1)} %copy-done, f32[8,128]{1,0:T(8,128)S(1)} %get-tuple-element.34.table, f32[6,8,16,128]{3,2,1,0:T(8,128)S(1)} %get-tuple-element.35.b0, ...), custom_call_target="tpu_custom_call" | custom-call | tf_op jit(solution)/shard_map/own_kernel/pallas_call | solution.py:416
  13.8 0.0 collective-permute-done.x_near_in
  13.8 0.0 collective-permute-done.1.x_far_in
  13.8 0.0 collective-permute-done.2.y_near_in
  13.8 0.9 %collective-permute-done.3.y_far_in = f32[6,16,128]{2,1,0:T(8,128)S(1)} collective-permute-done((f32[6,16,128]{2,1,0:T(8,128)S(1)}, f32[6,16,128]{2,1,0:T(8,128)S(1)}, u32[]{:S(2)}, u32[]{:S(2)}) %collective-permute-start.3) | collective-permute-done | bytes 49184 | tf_op jit(solution)/shard_map/ppermute | solution.py:432
  14.7 1.0 %second_kernel.1 = (f32[6,4,8,128]{3,2,1,0:T(8,128)S(1)}, f32[6,4,8,128]{3,2,1,0:T(8,128)S(1)}, f32[6,8,128]{2,1,0:T(8,128)S(1)}, f32[6,8,128]{2,1,0:T(8,128)S(1...) custom-call(f32[6,4,8,128]{3,2,1,0:T(8,128)S(1)} %get-tuple-element.43.own_b1, ...), custom_call_target="tpu_custom_call" | custom-call | tf_op jit(solution)/shard_map/second_kernel/pallas_call | solution.py:416
  15.7 0.1 collective-permute-start.4
  15.8 1.4 %collective-permute-start.5 = (f32[6,8,128]{2,1,0:T(8,128)S(1)}, f32[6,8,128]{2,1,0:T(8,128)S(1)}, u32[]{:S(2)}, u32[]{:S(2)}) collective-permute-start(f32[6,8,128]{2,1,0:T(8,128)S(1)} %get-tuple-element.48), channel_id=1, source_target_pairs={{0,1},{1,0},{2,3},{3,2},{4,5},{5,4},{6,7},{7,6},{8,16},{9,17},{10,... | collective-permute-start | bytes 73736 | tf_op jit(solution)/shard_map/ppermute | solution.py:432
  17.3 1.2 %collective-permute-start.6 = (f32[6,8,128]{2,1,0:T(8,128)S(1)}, f32[6,8,128]{2,1,0:T(8,128)S(1)}, u32[]{:S(2)}, u32[]{:S(2)}) collective-permute-start(f32[6,8,128]{2,1,0:T(8,128)S(1)} %get-tuple-element.49), channel_id=1, source_target_pairs={{0,1},{1,0},{2,3},{3,2},{4,5},{5,4},{6,7},{7,6},{8,9},{9,8},{10,11... | collective-permute-start | bytes 73736 | tf_op jit(solution)/shard_map/ppermute | solution.py:432
  18.4 1.2 %collective-permute-start.7 = (f32[6,8,128]{2,1,0:T(8,128)S(1)}, f32[6,8,128]{2,1,0:T(8,128)S(1)}, u32[]{:S(2)}, u32[]{:S(2)}) collective-permute-start(f32[6,8,128]{2,1,0:T(8,128)S(1)} %get-tuple-element.50), channel_id=1, source_target_pairs={{0,8},{1,2},{2,1},{3,4},{4,3},{5,6},{6,5},{7,15},{8,0},{9,10},{10,... | collective-permute-start | bytes 73736 | tf_op jit(solution)/shard_map/ppermute | solution.py:432
  19.6 1.6 %middle_kernel.1.y0 = f32[6,8,16,128]{3,2,1,0:T(8,128)S(1)} custom-call(s32[8,512]{1,0:T(8,128)S(1)} %get-tuple-element.32.layers, f32[6,8,16,128]{3,2,1,0:T(8,128)S(1)} %get-tuple-element.33.x0, f32[6,8,16,128]{3,2,1,0:T(8,128)S(1)} %get-tuple-element.36.r0, f32[6,16,128]{2,1,0:T(8,128)S(1)} %collective-permute-done.x_near_in, ...), custom_call_target="tpu_custom_call" | custom-call | tf_op jit(solution)/shard_map/middle_kernel/pallas_call | solution.py:416
  21.2 0.0 collective-permute-done.4.x_near_in
  21.2 0.0 collective-permute-done.5.x_far_in
  21.2 0.0 collective-permute-done.6.y_near_in
  21.2 0.6 %collective-permute-done.7.y_far_in = f32[6,8,128]{2,1,0:T(8,128)S(1)} collective-permute-done((f32[6,8,128]{2,1,0:T(8,128)S(1)}, f32[6,8,128]{2,1,0:T(8,128)S(1)}, u32[]{:S(2)}, u32[]{:S(2)}) %collective-permute-start.7) | collective-permute-done | bytes 24608 | tf_op jit(solution)/shard_map/ppermute | solution.py:432
  21.9 0.9 %third_kernel.1 = (f32[6,4,8,128]{3,2,1,0:T(8,128)S(1)}, f32[6,8,128]{2,1,0:T(8,128)S(1)}, f32[6,8,128]{2,1,0:T(8,128)S(1)}, f32[6,8,128]{2,1,0:T(8,128)S(1)}, f32[6,8,128]{2,1,0:T(8,128)S(1)}) custom-call(s32[8,512]{1,0:T(8,128)S(1)} %get-tuple-element.32.layers, f32[6,8,16,128]{3,2,1,0:T(8,128)S(1)} %middle_kernel.1.y0, ...), custom_call_target="tpu_custom_call" | custom-call | tf_op jit(solution)/shard_map/third_kernel/pallas_call | solution.py:416
  22.8 0.4 %collective-permute-start.8 = (f32[6,8,128]{2,1,0:T(8,128)S(1)}, f32[6,8,128]{2,1,0:T(8,128)S(1)}, u32[]{:S(2)}, u32[]{:S(2)}) collective-permute-start(f32[6,8,128]{2,1,0:T(8,128)S(1)} %get-tuple-element.55), channel_id=1, source_target_pairs={{0,8},{1,9},{2,10},{3,11},{4,12},{5,13},{6,14},{7,15},{8,0},{9,1},... | collective-permute-start | bytes 73736 | tf_op jit(solution)/shard_map/ppermute | solution.py:432
  23.2 1.7 %collective-permute-start.9 = (f32[6,8,128]{2,1,0:T(8,128)S(1)}, f32[6,8,128]{2,1,0:T(8,128)S(1)}, u32[]{:S(2)}, u32[]{:S(2)}) collective-permute-start(f32[6,8,128]{2,1,0:T(8,128)S(1)} %get-tuple-element.56), channel_id=1, source_target_pairs={{0,1},{1,0},{2,3},{3,2},{4,5},{5,4},{6,7},{7,6},{8,16},{9,17},{10,... | collective-permute-start | bytes 73736 | tf_op jit(solution)/shard_map/ppermute | solution.py:432
  24.8 0.7 %collective-permute-start.10 = (f32[6,8,128]{2,1,0:T(8,128)S(1)}, f32[6,8,128]{2,1,0:T(8,128)S(1)}, u32[]{:S(2)}, u32[]{:S(2)}) collective-permute-start(f32[6,8,128]{2,1,0:T(8,128)S(1)} %get-tuple-element.57), channel_id=1, source_target_pairs={{0,1},{1,0},{2,3},{3,2},{4,5},{5,4},{6,7},{7,6},{8,9},{9,8},{10,11... | collective-permute-start | bytes 73736 | tf_op jit(solution)/shard_map/ppermute | solution.py:432
  25.5 1.2 %collective-permute-start.11 = (f32[6,8,128]{2,1,0:T(8,128)S(1)}, f32[6,8,128]{2,1,0:T(8,128)S(1)}, u32[]{:S(2)}, u32[]{:S(2)}) collective-permute-start(f32[6,8,128]{2,1,0:T(8,128)S(1)} %get-tuple-element.58), channel_id=1, source_target_pairs={{0,8},{1,2},{2,1},{3,4},{4,3},{5,6},{6,5},{7,15},{8,0},{9,10},{10,... | collective-permute-start | bytes 73736 | tf_op jit(solution)/shard_map/ppermute | solution.py:432
  26.7 0.2 prolong_kernel.1
  26.9 0.0 collective-permute-done.8.x_near_in
  26.9 1.0 %collective-permute-done.9.x_far_in = f32[6,8,128]{2,1,0:T(8,128)S(1)} collective-permute-done((f32[6,8,128]{2,1,0:T(8,128)S(1)}, f32[6,8,128]{2,1,0:T(8,128)S(1)}, u32[]{:S(2)}, u32[]{:S(2)}) %collective-permute-start.9) | collective-permute-done | bytes 24608 | tf_op jit(solution)/shard_map/ppermute | solution.py:432
  27.9 0.0 collective-permute-done.10.y_near_in
  27.9 1.1 %collective-permute-done.11.y_far_in = f32[6,8,128]{2,1,0:T(8,128)S(1)} collective-permute-done((f32[6,8,128]{2,1,0:T(8,128)S(1)}, f32[6,8,128]{2,1,0:T(8,128)S(1)}, u32[]{:S(2)}, u32[]{:S(2)}) %collective-permute-start.11) | collective-permute-done | bytes 24608 | tf_op jit(solution)/shard_map/ppermute | solution.py:432
  29.0 2.4 %last_kernel.1 = f32[6,8,16,128]{3,2,1,0:T(8,128)} custom-call(s32[8,512]{1,0:T(8,128)S(1)} %get-tuple-element.32.layers, f32[6,8,16,128]{3,2,1,0:T(8,128)S(1)} %get-tuple-element.53.image, f32[6,8,16,128]{3,2,1,0:T(8,128)S(1)} %get-tuple-element.54.base, f32[6,8,128]{2,1,0:T(8,128)S(1)} %collective-permute-done.8.x_near_in, ...), custom_call_target="tpu_custom_call" | custom-call | tf_op jit(solution)/shard_map/last_kernel/pallas_call | solution.py:416
Async XLA Ops:
  0.0 12.2 %copy-start = (s32[8,16,128]{2,1,0:T(8,128)S(1)}, s32[8,16,128]{2,1,0:T(8,128)}, u32[]{:S(2)}) copy-start(s32[8,16,128]{2,1,0:T(8,128)} %classes.1) | copy-start | bytes 196612
  3.1 10.6 %collective-permute-start = (f32[6,16,128]{2,1,0:T(8,128)S(1)}, f32[6,16,128]{2,1,0:T(8,128)S(1)}, u32[]{:S(2)}, u32[]{:S(2)}) collective-permute-start(f32[6,16,128]{2,1,0:T(8,128)S(1)} %get-tuple-element.37), channel_id=1, source_target_pairs={{0,8},{1,9},{2,10},{3,11},{4,12},{5,13},{6,14},{7,15},{8,0},{9,1},... | collective-permute-start | bytes 147464 | tf_op jit(solution)/shard_map/ppermute | solution.py:432
  4.9 8.9 %collective-permute-start.1 = (f32[6,16,128]{2,1,0:T(8,128)S(1)}, f32[6,16,128]{2,1,0:T(8,128)S(1)}, u32[]{:S(2)}, u32[]{:S(2)}) collective-permute-start(f32[6,16,128]{2,1,0:T(8,128)S(1)} %get-tuple-element.38), channel_id=1, source_target_pairs={{0,1},{1,0},{2,3},{3,2},{4,5},{5,4},{6,7},{7,6},{8,16},{9,17},{10,... | collective-permute-start | bytes 147464 | tf_op jit(solution)/shard_map/ppermute | solution.py:432
  9.8 4.0 %collective-permute-start.2 = (f32[6,16,128]{2,1,0:T(8,128)S(1)}, f32[6,16,128]{2,1,0:T(8,128)S(1)}, u32[]{:S(2)}, u32[]{:S(2)}) collective-permute-start(f32[6,16,128]{2,1,0:T(8,128)S(1)} %get-tuple-element.39), channel_id=1, source_target_pairs={{0,1},{1,0},{2,3},{3,2},{4,5},{5,4},{6,7},{7,6},{8,9},{9,8},{10,11... | collective-permute-start | bytes 147464 | tf_op jit(solution)/shard_map/ppermute | solution.py:432
  11.0 3.7 %collective-permute-start.3 = (f32[6,16,128]{2,1,0:T(8,128)S(1)}, f32[6,16,128]{2,1,0:T(8,128)S(1)}, u32[]{:S(2)}, u32[]{:S(2)}) collective-permute-start(f32[6,16,128]{2,1,0:T(8,128)S(1)} %get-tuple-element.40), channel_id=1, source_target_pairs={{0,8},{1,2},{2,1},{3,4},{4,3},{5,6},{6,5},{7,15},{8,0},{9,10},{10,... | collective-permute-start | bytes 147464 | tf_op jit(solution)/shard_map/ppermute | solution.py:432
  15.7 5.5 %collective-permute-start.4 = (f32[6,8,128]{2,1,0:T(8,128)S(1)}, f32[6,8,128]{2,1,0:T(8,128)S(1)}, u32[]{:S(2)}, u32[]{:S(2)}) collective-permute-start(f32[6,8,128]{2,1,0:T(8,128)S(1)} %get-tuple-element.47), channel_id=1, source_target_pairs={{0,8},{1,9},{2,10},{3,11},{4,12},{5,13},{6,14},{7,15},{8,0},{9,1},... | collective-permute-start | bytes 73736 | tf_op jit(solution)/shard_map/ppermute | solution.py:432
  15.8 5.4 %collective-permute-start.5 = (f32[6,8,128]{2,1,0:T(8,128)S(1)}, f32[6,8,128]{2,1,0:T(8,128)S(1)}, u32[]{:S(2)}, u32[]{:S(2)}) collective-permute-start(f32[6,8,128]{2,1,0:T(8,128)S(1)} %get-tuple-element.48), channel_id=1, source_target_pairs={{0,1},{1,0},{2,3},{3,2},{4,5},{5,4},{6,7},{7,6},{8,16},{9,17},{10,... | collective-permute-start | bytes 73736 | tf_op jit(solution)/shard_map/ppermute | solution.py:432
  17.3 3.9 %collective-permute-start.6 = (f32[6,8,128]{2,1,0:T(8,128)S(1)}, f32[6,8,128]{2,1,0:T(8,128)S(1)}, u32[]{:S(2)}, u32[]{:S(2)}) collective-permute-start(f32[6,8,128]{2,1,0:T(8,128)S(1)} %get-tuple-element.49), channel_id=1, source_target_pairs={{0,1},{1,0},{2,3},{3,2},{4,5},{5,4},{6,7},{7,6},{8,9},{9,8},{10,11... | collective-permute-start | bytes 73736 | tf_op jit(solution)/shard_map/ppermute | solution.py:432
  18.4 3.4 %collective-permute-start.7 = (f32[6,8,128]{2,1,0:T(8,128)S(1)}, f32[6,8,128]{2,1,0:T(8,128)S(1)}, u32[]{:S(2)}, u32[]{:S(2)}) collective-permute-start(f32[6,8,128]{2,1,0:T(8,128)S(1)} %get-tuple-element.50), channel_id=1, source_target_pairs={{0,8},{1,2},{2,1},{3,4},{4,3},{5,6},{6,5},{7,15},{8,0},{9,10},{10,... | collective-permute-start | bytes 73736 | tf_op jit(solution)/shard_map/ppermute | solution.py:432
  22.8 4.1 %collective-permute-start.8 = (f32[6,8,128]{2,1,0:T(8,128)S(1)}, f32[6,8,128]{2,1,0:T(8,128)S(1)}, u32[]{:S(2)}, u32[]{:S(2)}) collective-permute-start(f32[6,8,128]{2,1,0:T(8,128)S(1)} %get-tuple-element.55), channel_id=1, source_target_pairs={{0,8},{1,9},{2,10},{3,11},{4,12},{5,13},{6,14},{7,15},{8,0},{9,1},... | collective-permute-start | bytes 73736 | tf_op jit(solution)/shard_map/ppermute | solution.py:432
  23.2 4.8 %collective-permute-start.9 = (f32[6,8,128]{2,1,0:T(8,128)S(1)}, f32[6,8,128]{2,1,0:T(8,128)S(1)}, u32[]{:S(2)}, u32[]{:S(2)}) collective-permute-start(f32[6,8,128]{2,1,0:T(8,128)S(1)} %get-tuple-element.56), channel_id=1, source_target_pairs={{0,1},{1,0},{2,3},{3,2},{4,5},{5,4},{6,7},{7,6},{8,16},{9,17},{10,... | collective-permute-start | bytes 73736 | tf_op jit(solution)/shard_map/ppermute | solution.py:432
  24.8 3.1 %collective-permute-start.10 = (f32[6,8,128]{2,1,0:T(8,128)S(1)}, f32[6,8,128]{2,1,0:T(8,128)S(1)}, u32[]{:S(2)}, u32[]{:S(2)}) collective-permute-start(f32[6,8,128]{2,1,0:T(8,128)S(1)} %get-tuple-element.57), channel_id=1, source_target_pairs={{0,1},{1,0},{2,3},{3,2},{4,5},{5,4},{6,7},{7,6},{8,9},{9,8},{10,11... | collective-permute-start | bytes 73736 | tf_op jit(solution)/shard_map/ppermute | solution.py:432
  25.5 3.5 %collective-permute-start.11 = (f32[6,8,128]{2,1,0:T(8,128)S(1)}, f32[6,8,128]{2,1,0:T(8,128)S(1)}, u32[]{:S(2)}, u32[]{:S(2)}) collective-permute-start(f32[6,8,128]{2,1,0:T(8,128)S(1)} %get-tuple-element.58), channel_id=1, source_target_pairs={{0,8},{1,2},{2,1},{3,4},{4,3},{5,6},{6,5},{7,15},{8,0},{9,10},{10,... | collective-permute-start | bytes 73736 | tf_op jit(solution)/shard_map/ppermute | solution.py:432

commit v5 on v4

--- a/solution.py
+++ b/solution.py
@@ -125,7 +125,7 @@
 
 
 def first_kernel(
-    source_hbm, depth_hbm, inverses_hbm, conductivity_hbm, x0, b0, high, low, layers, table, x_near, x_far, y_near, y_far,
+    source_hbm, depth_hbm, inverses_hbm, conductivity_hbm, x0, b0, high, low, layers, table, x_far, x_near, y_far, y_near,
     source, depth, inverses, conductivity, columns, done,
 ):
     copies = [
@@ -237,8 +237,8 @@
 
 
 def second_kernel(
-    own_b1, layers, x_near_in, x_far_in, y_near_in, y_far_in, high, low,
-    b1, x1, x_near, x_far, y_near, y_far, rows, columns,
+    own_b1, layers, x_far_in, x_near_in, y_far_in, y_near_in, high, low,
+    b1, x1, x_far, x_near, y_far, y_near, rows, columns,
 ):
     shape = (16, 128)
     pair = pair_index(shape)
@@ -263,10 +263,10 @@
                 v = v + added[1]
             b1[c, x] = v
     result = coarse_smooth(Blocker(32), columns, lambda c, x: b1[c, x], high, low, layers[1:2, 0:128])
-    store_coarse(result, x1, x_near, x_far, y_near, y_far)
-
-
-def store_coarse(result, x1, x_near, x_far, y_near, y_far):
+    store_coarse(result, x1, x_far, x_near, y_far, y_near)
+
+
+def store_coarse(result, x1, x_far, x_near, y_far, y_near):
     for c in range(6):
         for x in range(4):
             x1[c, x] = result(c, x)
@@ -276,7 +276,7 @@
         y_far[c, 4:8] = y_far[c, 0:4]
 
 
-def middle_kernel(layers, x0, r0, x_near_in, x_far_in, y_near_in, y_far_in, high, low, y0, columns):
+def middle_kernel(layers, x0, r0, x_far_in, x_near_in, y_far_in, y_near_in, high, low, y0, columns):
     blocker = Blocker(64)
     row = row_of((16, 128))
     x_halo = [before_after("gx", x_near_in[c], x_far_in[c]) for c in range(6)]
@@ -300,8 +300,8 @@
 
 
 def third_kernel(
-    layers, y0, b1, x1a, sigma1, x_near_in, x_far_in, y_near_in, y_far_in, high, low,
-    x1, x_near, x_far, y_near, y_far, columns,
+    layers, y0, b1, x1a, sigma1, x_far_in, x_near_in, y_far_in, y_near_in, high, low,
+    x1, x_far, x_near, y_far, y_near, columns,
 ):
     x_halo = [before_after("gx", x_near_in[c], x_far_in[c]) for c in range(6)]
     y_halo = [before_after("gy", y_near_in[c], y_far_in[c]) for c in range(6)]
@@ -318,7 +318,7 @@
         return b1[c, x] - ((6.0 * u - beside) * 0.25 + sigma1[x] * turn)
 
     more = coarse_smooth(Blocker(32), columns, residual, high, low, layers[1:2, 0:128])
-    store_coarse(lambda c, x: x1a[c, x] + more(c, x), x1, x_near, x_far, y_near, y_far)
+    store_coarse(lambda c, x: x1a[c, x] + more(c, x), x1, x_far, x_near, y_far, y_near)
 
 
 def self_index(shape):
@@ -366,7 +366,7 @@
                     base[comp, x] = y0[comp, x] + rows[comp, xx]
 
 
-def last_kernel(layers, image, base, x_near_in, x_far_in, y_near_in, y_far_in, high, low, out, rows, columns, stage, done):
+def last_kernel(layers, image, base, x_far_in, x_near_in, y_far_in, y_near_in, high, low, out, rows, columns, stage, done):
     shape = (8, 128)
     own_index = self_index(shape)
     row = row_of((16, 128))
@@ -424,7 +424,7 @@
     )(*args)
 
 
-def exchange(x_near, x_far, y_near, y_far):
+def exchange(x_far, x_near, y_far, y_near):
     nx, ny = lax.axis_size("gx"), lax.axis_size("gy")
 
     def swapped(array, partner):
@@ -441,10 +441,10 @@
         return (i ^ 1, j) if j in (0, ny - 1) else (i, far(j))
 
     return (
+        swapped(x_far, x_far_partner),
         swapped(x_near, lambda i, j: (i ^ 1, j)),
-        swapped(x_far, x_far_partner),
+        swapped(y_far, y_far_partner),
         swapped(y_near, lambda i, j: (i, j ^ 1)),
-        swapped(y_far, y_far_partner),
     )
 
 

time: 31.6 us -> 30.9 us (0.978)
  the two profiles are of different devices: /device:TPU:7 before, /device:TPU:6 now
where the time goes in v5:
time: 30.9 us; the launch traced here: 30.8 us
  starting transfers between devices  16.2 us (52%)
  Pallas kernels  10.8 us (35%)
  waiting for transfers between devices  3.71 us (12%)
    ppermute x12, starting transfers between devices, swapped(): lax.ppermute(array, ('gx', 'gy'), [(a, i * ny + j) for a, (i, j) in pairs])  16.2 us
    pallas_call x7, Pallas kernels, call(): pl.pallas_call(kernel, out_shape=[jax.ShapeDtypeStruct(*out) if last else...  10.8 us
    ppermute x12, waiting for transfers between devices, swapped(): lax.ppermute(array, ('gx', 'gy'), [(a, i * ny + j) for a, (i, j) in pairs])  3.71 us
  transfers between devices with their start and end apart: 12, of which 7 were waited for; matrix products, arithmetic and copies ran while one was open for 0% of the time, Pallas kernels for 11%

profile of v5, /device:TPU:6, one launch (start us, length us, event | category | flops | bytes accessed | tf_op | source)
XLA Modules:
  0.0 30.8 jit_solution(17389005358106667630)
XLA Ops:
  0.0 0.0 copy-start
  0.0 3.1 %first_kernel.1 = (f32[6,8,16,128]{3,2,1,0:T(8,128)S(1)}, f32[6,8,16,128]{3,2,1,0:T(8,128)S(1)}, bf16[8,192,192]{2,1,0:T(8,128)(2,1)S(1)}, bf16[8,192,192]{2,1,0...) custom-call(f32[6,8,16,128]{3,2,1,0:T(8,128)} %source_hbm.1, ...), custom_call_target="tpu_custom_call" | custom-call | tf_op jit(solution)/shard_map/first_kernel/pallas_call | solution.py:416
  3.1 6.2 %collective-permute-start = (f32[6,16,128]{2,1,0:T(8,128)S(1)}, f32[6,16,128]{2,1,0:T(8,128)S(1)}, u32[]{:S(2)}, u32[]{:S(2)}) collective-permute-start(f32[6,16,128]{2,1,0:T(8,128)S(1)} %get-tuple-element.37), channel_id=1, source_target_pairs={{0,1},{1,0},{2,3},{3,2},{4,5},{5,4},{6,7},{7,6},{8,16},{9,17},{10,... | collective-permute-start | bytes 147464 | tf_op jit(solution)/shard_map/ppermute | solution.py:432
  9.3 0.0 collective-permute-start.1
  9.4 2.0 %collective-permute-start.2 = (f32[6,16,128]{2,1,0:T(8,128)S(1)}, f32[6,16,128]{2,1,0:T(8,128)S(1)}, u32[]{:S(2)}, u32[]{:S(2)}) collective-permute-start(f32[6,16,128]{2,1,0:T(8,128)S(1)} %get-tuple-element.39), channel_id=1, source_target_pairs={{0,8},{1,2},{2,1},{3,4},{4,3},{5,6},{6,5},{7,15},{8,0},{9,10},{10,... | collective-permute-start | bytes 147464 | tf_op jit(solution)/shard_map/ppermute | solution.py:432
  11.4 0.0 collective-permute-start.3
  11.4 0.0 copy-done
  11.4 1.6 %own_kernel.1 = (f32[6,8,16,128]{3,2,1,0:T(8,128)S(1)}, f32[6,4,8,128]{3,2,1,0:T(8,128)S(1)}, f32[8,16,128]{2,1,0:T(8,128)S(1)}, f32[4,8,128]{2,1,0:T(8,128)S(1)}) custom-call(s32[8,16,128]{2,1,0:T(8,128)S(1)} %copy-done, f32[8,128]{1,0:T(8,128)S(1)} %get-tuple-element.34.table, f32[6,8,16,128]{3,2,1,0:T(8,128)S(1)} %get-tuple-element.35.b0, ...), custom_call_target="tpu_custom_call" | custom-call | tf_op jit(solution)/shard_map/own_kernel/pallas_call | solution.py:416
  12.9 0.0 collective-permute-done.x_far_in
  13.0 0.5 %collective-permute-done.1.x_near_in = f32[6,16,128]{2,1,0:T(8,128)S(1)} collective-permute-done((f32[6,16,128]{2,1,0:T(8,128)S(1)}, f32[6,16,128]{2,1,0:T(8,128)S(1)}, u32[]{:S(2)}, u32[]{:S(2)}) %collective-permute-start.1) | collective-permute-done | bytes 49184 | tf_op jit(solution)/shard_map/ppermute | solution.py:432
  13.4 0.5 %collective-permute-done.2.y_far_in = f32[6,16,128]{2,1,0:T(8,128)S(1)} collective-permute-done((f32[6,16,128]{2,1,0:T(8,128)S(1)}, f32[6,16,128]{2,1,0:T(8,128)S(1)}, u32[]{:S(2)}, u32[]{:S(2)}) %collective-permute-start.2) | collective-permute-done | bytes 49184 | tf_op jit(solution)/shard_map/ppermute | solution.py:432
  14.0 0.0 collective-permute-done.3.y_near_in
  14.0 1.0 %second_kernel.1 = (f32[6,4,8,128]{3,2,1,0:T(8,128)S(1)}, f32[6,4,8,128]{3,2,1,0:T(8,128)S(1)}, f32[6,8,128]{2,1,0:T(8,128)S(1)}, f32[6,8,128]{2,1,0:T(8,128)S(1...) custom-call(f32[6,4,8,128]{3,2,1,0:T(8,128)S(1)} %get-tuple-element.43.own_b1, ...), custom_call_target="tpu_custom_call" | custom-call | tf_op jit(solution)/shard_map/second_kernel/pallas_call | solution.py:416
  15.0 1.7 %collective-permute-start.4 = (f32[6,8,128]{2,1,0:T(8,128)S(1)}, f32[6,8,128]{2,1,0:T(8,128)S(1)}, u32[]{:S(2)}, u32[]{:S(2)}) collective-permute-start(f32[6,8,128]{2,1,0:T(8,128)S(1)} %get-tuple-element.47), channel_id=1, source_target_pairs={{0,1},{1,0},{2,3},{3,2},{4,5},{5,4},{6,7},{7,6},{8,16},{9,17},{10,... | collective-permute-start | bytes 73736 | tf_op jit(solution)/shard_map/ppermute | solution.py:432
  16.7 0.6 %collective-permute-start.5 = (f32[6,8,128]{2,1,0:T(8,128)S(1)}, f32[6,8,128]{2,1,0:T(8,128)S(1)}, u32[]{:S(2)}, u32[]{:S(2)}) collective-permute-start(f32[6,8,128]{2,1,0:T(8,128)S(1)} %get-tuple-element.48), channel_id=1, source_target_pairs={{0,8},{1,9},{2,10},{3,11},{4,12},{5,13},{6,14},{7,15},{8,0},{9,1},... | collective-permute-start | bytes 73736 | tf_op jit(solution)/shard_map/ppermute | solution.py:432
  17.3 1.4 %collective-permute-start.6 = (f32[6,8,128]{2,1,0:T(8,128)S(1)}, f32[6,8,128]{2,1,0:T(8,128)S(1)}, u32[]{:S(2)}, u32[]{:S(2)}) collective-permute-start(f32[6,8,128]{2,1,0:T(8,128)S(1)} %get-tuple-element.49), channel_id=1, source_target_pairs={{0,8},{1,2},{2,1},{3,4},{4,3},{5,6},{6,5},{7,15},{8,0},{9,10},{10,... | collective-permute-start | bytes 73736 | tf_op jit(solution)/shard_map/ppermute | solution.py:432
  18.7 0.0 collective-permute-start.7
  18.7 1.6 %middle_kernel.1.y0 = f32[6,8,16,128]{3,2,1,0:T(8,128)S(1)} custom-call(s32[8,512]{1,0:T(8,128)S(1)} %get-tuple-element.32.layers, f32[6,8,16,128]{3,2,1,0:T(8,128)S(1)} %get-tuple-element.33.x0, f32[6,8,16,128]{3,2,1,0:T(8,128)S(1)} %get-tuple-element.36.r0, f32[6,16,128]{2,1,0:T(8,128)S(1)} %collective-permute-done.x_far_in, ...), custom_call_target="tpu_custom_call" | custom-call | tf_op jit(solution)/shard_map/middle_kernel/pallas_call | solution.py:416
  20.3 0.7 %collective-permute-done.4.x_far_in = f32[6,8,128]{2,1,0:T(8,128)S(1)} collective-permute-done((f32[6,8,128]{2,1,0:T(8,128)S(1)}, f32[6,8,128]{2,1,0:T(8,128)S(1)}, u32[]{:S(2)}, u32[]{:S(2)}) %collective-permute-start.4) | collective-permute-done | bytes 24608 | tf_op jit(solution)/shard_map/ppermute | solution.py:432
  21.0 0.0 collective-permute-done.5.x_near_in
  21.0 0.1 collective-permute-done.6.y_far_in
  21.1 0.0 collective-permute-done.7.y_near_in
  21.1 0.9 %third_kernel.1 = (f32[6,4,8,128]{3,2,1,0:T(8,128)S(1)}, f32[6,8,128]{2,1,0:T(8,128)S(1)}, f32[6,8,128]{2,1,0:T(8,128)S(1)}, f32[6,8,128]{2,1,0:T(8,128)S(1)}, f32[6,8,128]{2,1,0:T(8,128)S(1)}) custom-call(s32[8,512]{1,0:T(8,128)S(1)} %get-tuple-element.32.layers, f32[6,8,16,128]{3,2,1,0:T(8,128)S(1)} %middle_kernel.1.y0, ...), custom_call_target="tpu_custom_call" | custom-call | tf_op jit(solution)/shard_map/third_kernel/pallas_call | solution.py:416
  22.1 2.3 %collective-permute-start.8 = (f32[6,8,128]{2,1,0:T(8,128)S(1)}, f32[6,8,128]{2,1,0:T(8,128)S(1)}, u32[]{:S(2)}, u32[]{:S(2)}) collective-permute-start(f32[6,8,128]{2,1,0:T(8,128)S(1)} %get-tuple-element.55), channel_id=1, source_target_pairs={{0,1},{1,0},{2,3},{3,2},{4,5},{5,4},{6,7},{7,6},{8,16},{9,17},{10,... | collective-permute-start | bytes 73736 | tf_op jit(solution)/shard_map/ppermute | solution.py:432
  24.3 0.0 collective-permute-start.9
  24.3 2.0 %collective-permute-start.10 = (f32[6,8,128]{2,1,0:T(8,128)S(1)}, f32[6,8,128]{2,1,0:T(8,128)S(1)}, u32[]{:S(2)}, u32[]{:S(2)}) collective-permute-start(f32[6,8,128]{2,1,0:T(8,128)S(1)} %get-tuple-element.57), channel_id=1, source_target_pairs={{0,8},{1,2},{2,1},{3,4},{4,3},{5,6},{6,5},{7,15},{8,0},{9,10},{10,... | collective-permute-start | bytes 73736 | tf_op jit(solution)/shard_map/ppermute | solution.py:432
  26.3 0.0 collective-permute-start.11
  26.3 0.2 prolong_kernel.1
  26.5 1.5 %collective-permute-done.8.x_far_in = f32[6,8,128]{2,1,0:T(8,128)S(1)} collective-permute-done((f32[6,8,128]{2,1,0:T(8,128)S(1)}, f32[6,8,128]{2,1,0:T(8,128)S(1)}, u32[]{:S(2)}, u32[]{:S(2)}) %collective-permute-start.8) | collective-permute-done | bytes 24608 | tf_op jit(solution)/shard_map/ppermute | solution.py:432
  28.1 0.1 collective-permute-done.9.x_near_in
  28.1 0.3 collective-permute-done.10.y_far_in
  28.4 0.0 collective-permute-done.11.y_near_in
  28.4 2.4 %last_kernel.1 = f32[6,8,16,128]{3,2,1,0:T(8,128)} custom-call(s32[8,512]{1,0:T(8,128)S(1)} %get-tuple-element.32.layers, f32[6,8,16,128]{3,2,1,0:T(8,128)S(1)} %get-tuple-element.53.image, f32[6,8,16,128]{3,2,1,0:T(8,128)S(1)} %get-tuple-element.54.base, f32[6,8,128]{2,1,0:T(8,128)S(1)} %collective-permute-done.8.x_far_in, ...), custom_call_target="tpu_custom_call" | custom-call | tf_op jit(solution)/shard_map/last_kernel/pallas_call | solution.py:416
Async XLA Ops:
  0.0 11.4 %copy-start = (s32[8,16,128]{2,1,0:T(8,128)S(1)}, s32[8,16,128]{2,1,0:T(8,128)}, u32[]{:S(2)}) copy-start(s32[8,16,128]{2,1,0:T(8,128)} %classes.1) | copy-start | bytes 196612
  3.1 9.8 %collective-permute-start = (f32[6,16,128]{2,1,0:T(8,128)S(1)}, f32[6,16,128]{2,1,0:T(8,128)S(1)}, u32[]{:S(2)}, u32[]{:S(2)}) collective-permute-start(f32[6,16,128]{2,1,0:T(8,128)S(1)} %get-tuple-element.37), channel_id=1, source_target_pairs={{0,1},{1,0},{2,3},{3,2},{4,5},{5,4},{6,7},{7,6},{8,16},{9,17},{10,... | collective-permute-start | bytes 147464 | tf_op jit(solution)/shard_map/ppermute | solution.py:432
  9.3 4.1 %collective-permute-start.1 = (f32[6,16,128]{2,1,0:T(8,128)S(1)}, f32[6,16,128]{2,1,0:T(8,128)S(1)}, u32[]{:S(2)}, u32[]{:S(2)}) collective-permute-start(f32[6,16,128]{2,1,0:T(8,128)S(1)} %get-tuple-element.38), channel_id=1, source_target_pairs={{0,8},{1,9},{2,10},{3,11},{4,12},{5,13},{6,14},{7,15},{8,0},{9,1},... | collective-permute-start | bytes 147464 | tf_op jit(solution)/shard_map/ppermute | solution.py:432
  9.4 4.6 %collective-permute-start.2 = (f32[6,16,128]{2,1,0:T(8,128)S(1)}, f32[6,16,128]{2,1,0:T(8,128)S(1)}, u32[]{:S(2)}, u32[]{:S(2)}) collective-permute-start(f32[6,16,128]{2,1,0:T(8,128)S(1)} %get-tuple-element.39), channel_id=1, source_target_pairs={{0,8},{1,2},{2,1},{3,4},{4,3},{5,6},{6,5},{7,15},{8,0},{9,10},{10,... | collective-permute-start | bytes 147464 | tf_op jit(solution)/shard_map/ppermute | solution.py:432
  11.4 2.6 %collective-permute-start.3 = (f32[6,16,128]{2,1,0:T(8,128)S(1)}, f32[6,16,128]{2,1,0:T(8,128)S(1)}, u32[]{:S(2)}, u32[]{:S(2)}) collective-permute-start(f32[6,16,128]{2,1,0:T(8,128)S(1)} %get-tuple-element.40), channel_id=1, source_target_pairs={{0,1},{1,0},{2,3},{3,2},{4,5},{5,4},{6,7},{7,6},{8,9},{9,8},{10,11... | collective-permute-start | bytes 147464 | tf_op jit(solution)/shard_map/ppermute | solution.py:432
  15.0 6.0 %collective-permute-start.4 = (f32[6,8,128]{2,1,0:T(8,128)S(1)}, f32[6,8,128]{2,1,0:T(8,128)S(1)}, u32[]{:S(2)}, u32[]{:S(2)}) collective-permute-start(f32[6,8,128]{2,1,0:T(8,128)S(1)} %get-tuple-element.47), channel_id=1, source_target_pairs={{0,1},{1,0},{2,3},{3,2},{4,5},{5,4},{6,7},{7,6},{8,16},{9,17},{10,... | collective-permute-start | bytes 73736 | tf_op jit(solution)/shard_map/ppermute | solution.py:432
  16.7 4.3 %collective-permute-start.5 = (f32[6,8,128]{2,1,0:T(8,128)S(1)}, f32[6,8,128]{2,1,0:T(8,128)S(1)}, u32[]{:S(2)}, u32[]{:S(2)}) collective-permute-start(f32[6,8,128]{2,1,0:T(8,128)S(1)} %get-tuple-element.48), channel_id=1, source_target_pairs={{0,8},{1,9},{2,10},{3,11},{4,12},{5,13},{6,14},{7,15},{8,0},{9,1},... | collective-permute-start | bytes 73736 | tf_op jit(solution)/shard_map/ppermute | solution.py:432
  17.3 3.8 %collective-permute-start.6 = (f32[6,8,128]{2,1,0:T(8,128)S(1)}, f32[6,8,128]{2,1,0:T(8,128)S(1)}, u32[]{:S(2)}, u32[]{:S(2)}) collective-permute-start(f32[6,8,128]{2,1,0:T(8,128)S(1)} %get-tuple-element.49), channel_id=1, source_target_pairs={{0,8},{1,2},{2,1},{3,4},{4,3},{5,6},{6,5},{7,15},{8,0},{9,10},{10,... | collective-permute-start | bytes 73736 | tf_op jit(solution)/shard_map/ppermute | solution.py:432
  18.7 2.4 %collective-permute-start.7 = (f32[6,8,128]{2,1,0:T(8,128)S(1)}, f32[6,8,128]{2,1,0:T(8,128)S(1)}, u32[]{:S(2)}, u32[]{:S(2)}) collective-permute-start(f32[6,8,128]{2,1,0:T(8,128)S(1)} %get-tuple-element.50), channel_id=1, source_target_pairs={{0,1},{1,0},{2,3},{3,2},{4,5},{5,4},{6,7},{7,6},{8,9},{9,8},{10,11... | collective-permute-start | bytes 73736 | tf_op jit(solution)/shard_map/ppermute | solution.py:432
  22.1 6.0 %collective-permute-start.8 = (f32[6,8,128]{2,1,0:T(8,128)S(1)}, f32[6,8,128]{2,1,0:T(8,128)S(1)}, u32[]{:S(2)}, u32[]{:S(2)}) collective-permute-start(f32[6,8,128]{2,1,0:T(8,128)S(1)} %get-tuple-element.55), channel_id=1, source_target_pairs={{0,1},{1,0},{2,3},{3,2},{4,5},{5,4},{6,7},{7,6},{8,16},{9,17},{10,... | collective-permute-start | bytes 73736 | tf_op jit(solution)/shard_map/ppermute | solution.py:432
  24.3 3.8 %collective-permute-start.9 = (f32[6,8,128]{2,1,0:T(8,128)S(1)}, f32[6,8,128]{2,1,0:T(8,128)S(1)}, u32[]{:S(2)}, u32[]{:S(2)}) collective-permute-start(f32[6,8,128]{2,1,0:T(8,128)S(1)} %get-tuple-element.56), channel_id=1, source_target_pairs={{0,8},{1,9},{2,10},{3,11},{4,12},{5,13},{6,14},{7,15},{8,0},{9,1},... | collective-permute-start | bytes 73736 | tf_op jit(solution)/shard_map/ppermute | solution.py:432
  24.3 4.1 %collective-permute-start.10 = (f32[6,8,128]{2,1,0:T(8,128)S(1)}, f32[6,8,128]{2,1,0:T(8,128)S(1)}, u32[]{:S(2)}, u32[]{:S(2)}) collective-permute-start(f32[6,8,128]{2,1,0:T(8,128)S(1)} %get-tuple-element.57), channel_id=1, source_target_pairs={{0,8},{1,2},{2,1},{3,4},{4,3},{5,6},{6,5},{7,15},{8,0},{9,10},{10,... | collective-permute-start | bytes 73736 | tf_op jit(solution)/shard_map/ppermute | solution.py:432
  26.3 2.1 %collective-permute-start.11 = (f32[6,8,128]{2,1,0:T(8,128)S(1)}, f32[6,8,128]{2,1,0:T(8,128)S(1)}, u32[]{:S(2)}, u32[]{:S(2)}) collective-permute-start(f32[6,8,128]{2,1,0:T(8,128)S(1)} %get-tuple-element.58), channel_id=1, source_target_pairs={{0,1},{1,0},{2,3},{3,2},{4,5},{5,4},{6,7},{7,6},{8,9},{9,8},{10,11... | collective-permute-start | bytes 73736 | tf_op jit(solution)/shard_map/ppermute | solution.py:432

commit v6 on v5

--- a/solution.py
+++ b/solution.py
@@ -237,7 +237,7 @@
 
 
 def second_kernel(
-    own_b1, layers, x_far_in, x_near_in, y_far_in, y_near_in, high, low,
+    own_b1, edges, layers, x_far_in, x_near_in, y_far_in, y_near_in, high, low,
     b1, x1, x_far, x_near, y_far, y_near, rows, columns,
 ):
     shape = (16, 128)
@@ -326,7 +326,7 @@
     return ((k & 1) << 5) | (k >> 1)
 
 
-def prolong_kernel(x1, sigma0, y0, image, base, coarse, rows):
+def prolong_kernel(x1, sigma0, y0, layers, high, low, base, image, coarse, rows, columns):
     shape = (8, 128)
     j = lane_of(shape)
     row = row_of(shape)
@@ -365,46 +365,91 @@
                 for comp in (c, c + 3):
                     base[comp, x] = y0[comp, x] + rows[comp, xx]
 
-
-def last_kernel(layers, image, base, x_far_in, x_near_in, y_far_in, y_near_in, high, low, out, rows, columns, stage, done):
+    blocker = Blocker(64)
+    fine_columns(blocker, lambda c, x: image[c, x], store_columns(columns))
+
+    def put(c, x, t, v):
+        part = slice(8 * t, 8 * t + 8)
+        base[c, x, part, :] = base[c, x, part, :] - v
+
+    fine_smooth(blocker, columns, high, low, layers[0:1, :], put)
+
+
+FACES = 36
+
+
+def edge_kernel(high, low, edges):
+    i = row_of((192, 128))
+    n = lane_of((192, 128))
+    n = n - jnp.where(n >= FACES, FACES, 0) - jnp.where(n >= 2 * FACES, FACES, 0)
+    face = jnp.where(n >= 12, 1, 0) + jnp.where(n >= 24, 1, 0)
+    n = n - 12 * face
+    x = (i >> 3) & 3
+    y = (i >> 1) & 3
+    same = ((i >> 5) == (n >> 1)) & (n < 12)
+    lane = lane_of((192, 128))
+    middle = (lane >= FACES) & (lane < 2 * FACES)
+    for bx in range(2):
+        on_x = (face == 0) & (x == 3 * bx) & ((y >> 1) == (n & 1))
+        on_first = (face == 1) & (y == 0) & ((x >> 1) == (n & 1))
+        on_last = (face == 2) & (y == 3) & ((x >> 1) == (n & 1))
+        sums = jnp.where(same & (on_x | on_first | on_last), 1.0, 0.0).astype(BF16)
+        for index in range(8):
+            v = dot(high[index], sums) + dot(low[index], sums)
+            v_high = v.astype(BF16).astype(F32)
+            edges[bx * 8 + index] = jnp.where(middle, v - v_high, v_high).astype(BF16)
+
+
+def last_kernel(layers, base, x_far_in, x_near_in, y_far_in, y_near_in, edges, out, stage, values, done):
     shape = (8, 128)
     own_index = self_index(shape)
-    row = row_of((16, 128))
-    y_halo = []
-    for c in range(6):
-        for side, v in enumerate(before_after("gx", x_near_in[c], x_far_in[c])):
-            v = take_lanes(v, own_index)
-            slot = 2 * c + side
-            rows[slot, pl.ds(0, 8, stride=2), :] = v
-            rows[slot, pl.ds(1, 8, stride=2), :] = v
-        y_halo.append([take_lanes(v, own_index) for v in before_after("gy", y_near_in[c], y_far_in[c])])
-
-    def get(c, x):
-        v = image[c, x] - jnp.where(row == 0, y_halo[c][0][x // 2 : x // 2 + 1], 0.0)
-        v = v - jnp.where(row == 15, y_halo[c][1][x // 2 : x // 2 + 1], 0.0)
-        if x == 0:
-            v = v - rows[2 * c]
-        if x == 7:
-            v = v - rows[2 * c + 1]
-        return v
-
+    first_half = lane_of((1, 128)) < 64
+    zero = jnp.zeros((1, 128), F32)
+    for bx in range(2):
+        values[bx, FACES:128] = jnp.zeros((128 - FACES, 256), F32)
+    for c in range(6):
+        x_faces = [take_lanes(v, own_index) for v in before_after("gx", x_near_in[c], x_far_in[c])]
+        y_faces = [take_lanes(v, own_index) for v in before_after("gy", y_near_in[c], y_far_in[c])]
+        for bx in range(2):
+            v = x_faces[bx]
+            for q in range(2):
+                row = c * 2 + q
+                x = 2 * bx + q
+                for t in range(2):
+                    y = 4 * t + q
+                    values[bx, row : row + 1, 128 * t : 128 * t + 128] = jnp.where(
+                        first_half, v[y : y + 1], v[y + 2 : y + 3]
+                    )
+                values[bx, 12 + row : 13 + row, 0:128] = jnp.where(first_half, y_faces[0][x : x + 1], 0.0)
+                values[bx, 12 + row : 13 + row, 128:256] = zero
+                values[bx, 24 + row : 25 + row, 0:128] = zero
+                values[bx, 24 + row : 25 + row, 128:256] = jnp.where(first_half, 0.0, y_faces[1][x : x + 1])
     blocker = Blocker(64)
-    fine_columns(blocker, get, store_columns(columns))
     join = join_index((16, 128))
     copies = []
-
-    def put(c, x, t, v):
-        stage[c, x, 8 * t : 8 * t + 8, :] = base[c, x, 8 * t : 8 * t + 8, :] - v
-
-    def finish(bx):
+    for bx in range(2):
+        v = values[bx]
+        v_high = v.astype(BF16).astype(F32)
+        values[bx, FACES : 2 * FACES] = v_high[0:FACES]
+        values[bx, 2 * FACES : 3 * FACES] = (v - v_high)[0:FACES]
+        columns = values[bx].astype(BF16)
+        total = jnp.zeros((192, 256), F32)
+        for index in range(8):
+            total = jnp.where(layers[0:1, 0:256] == index, dot(edges[bx * 8 + index], columns), total)
+        total = total * damping
+        for c in range(6):
+            for x in range(4):
+                row = c * 32 + x * 8
+                for t in range(2):
+                    part = slice(8 * t, 8 * t + 8)
+                    v = blocker.inverse(total[row : row + 8, 128 * t : 128 * t + 128])
+                    stage[c, 4 * bx + x, part, :] = base[c, 4 * bx + x, part, :] + v
         for c in range(6):
             for x in range(4 * bx, 4 * bx + 4):
                 stage[c, x] = take_lanes(stage[c, x], join)
         part = pl.ds(4 * bx, 4)
         copies.append(pltpu.make_async_copy(stage.at[:, part], out.at[:, part], done.at[bx]))
         copies[bx].start()
-
-    fine_smooth(blocker, columns, high, low, layers[0:1, :], put, finish)
     for copy in copies:
         copy.wait()
 
@@ -492,10 +537,11 @@
         [pltpu.VMEM((28, 16, 128), F32)] * 2,
         spaces=(pltpu.VMEM,),
     )
+    (edges,) = call(edge_kernel, [((16, 192, 128), BF16)], (high, low), [])
     b1, x1a, *faces = call(
         second_kernel,
         [coarse, coarse] + coarse_faces,
-        (own_b1, layers, *halos, high, low),
+        (own_b1, edges, layers, *halos, high, low),
         [pltpu.VMEM((12, 16, 128), F32), coarse_columns],
     )
     fine_halos = halos
@@ -505,17 +551,17 @@
         third_kernel, [coarse] + coarse_faces, (layers, y0, b1, x1a, sigma1, *halos, high, low), [coarse_columns]
     )
     halos = exchange(*faces)
-    image, base = call(
+    (base,) = call(
         prolong_kernel,
-        [fine, fine],
-        (x1, sigma0, y0),
-        [pltpu.VMEM((6, 4, 8, 128), F32), pltpu.VMEM((6, 4, 16, 128), F32)],
+        [fine],
+        (x1, sigma0, y0, layers, high, low),
+        [pltpu.VMEM(*fine), pltpu.VMEM((6, 4, 8, 128), F32), pltpu.VMEM((6, 4, 16, 128), F32), columns],
     )
     (out,) = call(
         last_kernel,
         [fine],
-        (layers, image, base, *halos, high, low),
-        [pltpu.VMEM((12, 16, 128), F32), columns, pltpu.VMEM(*fine), pltpu.SemaphoreType.DMA((2,))],
+        (layers, base, *halos, edges),
+        [pltpu.VMEM(*fine), pltpu.VMEM((2, 128, 256), F32), pltpu.SemaphoreType.DMA((2,))],
         last=True,
     )
     return out

time: 30.9 us -> 30.5 us (0.987)
  the two profiles are of different devices: /device:TPU:6 before, /device:TPU:7 now
where the time goes in v6:
time: 30.5 us; the launch traced here: 30.4 us
  starting transfers between devices  17.7 us (58%)
  Pallas kernels  12.5 us (41%)
    ppermute x12, starting transfers between devices, swapped(): lax.ppermute(array, ('gx', 'gy'), [(a, i * ny + j) for a, (i, j) in pairs])  17.7 us
    pallas_call x8, Pallas kernels, call(): pl.pallas_call(kernel, out_shape=[jax.ShapeDtypeStruct(*out) if last else...  12.5 us
  transfers between devices with their start and end apart: 12, of which 1 were waited for; matrix products, arithmetic and copies ran while one was open for 0% of the time, Pallas kernels for 20%

profile of v6, /device:TPU:7, one launch (start us, length us, event | category | flops | bytes accessed | tf_op | source)
XLA Modules:
  0.0 30.4 jit_solution(7038180805299331834)
XLA Ops:
  0.0 3.1 %first_kernel.1 = (f32[6,8,16,128]{3,2,1,0:T(8,128)S(1)}, f32[6,8,16,128]{3,2,1,0:T(8,128)S(1)}, bf16[8,192,192]{2,1,0:T(8,128)(2,1)S(1)}, bf16[8,192,192]{2,1,0...) custom-call(f32[6,8,16,128]{3,2,1,0:T(8,128)} %source_hbm.1, ...), custom_call_target="tpu_custom_call" | custom-call | tf_op jit(solution)/shard_map/first_kernel/pallas_call | solution.py:461
  3.1 0.0 copy-start
  3.1 5.9 %collective-permute-start = (f32[6,16,128]{2,1,0:T(8,128)S(1)}, f32[6,16,128]{2,1,0:T(8,128)S(1)}, u32[]{:S(2)}, u32[]{:S(2)}) collective-permute-start(f32[6,16,128]{2,1,0:T(8,128)S(1)} %get-tuple-element.35), channel_id=1, source_target_pairs={{0,1},{1,0},{2,3},{3,2},{4,5},{5,4},{6,7},{7,6},{8,16},{9,17},{10,... | collective-permute-start | bytes 147464 | tf_op jit(solution)/shard_map/ppermute | solution.py:477
  9.0 0.0 collective-permute-start.1
  9.1 2.1 %collective-permute-start.2 = (f32[6,16,128]{2,1,0:T(8,128)S(1)}, f32[6,16,128]{2,1,0:T(8,128)S(1)}, u32[]{:S(2)}, u32[]{:S(2)}) collective-permute-start(f32[6,16,128]{2,1,0:T(8,128)S(1)} %get-tuple-element.37), channel_id=1, source_target_pairs={{0,8},{1,2},{2,1},{3,4},{4,3},{5,6},{6,5},{7,15},{8,0},{9,10},{10,... | collective-permute-start | bytes 147464 | tf_op jit(solution)/shard_map/ppermute | solution.py:477
  11.2 0.8 %collective-permute-start.3 = (f32[6,16,128]{2,1,0:T(8,128)S(1)}, f32[6,16,128]{2,1,0:T(8,128)S(1)}, u32[]{:S(2)}, u32[]{:S(2)}) collective-permute-start(f32[6,16,128]{2,1,0:T(8,128)S(1)} %get-tuple-element.38), channel_id=1, source_target_pairs={{0,1},{1,0},{2,3},{3,2},{4,5},{5,4},{6,7},{7,6},{8,9},{9,8},{10,11... | collective-permute-start | bytes 147464 | tf_op jit(solution)/shard_map/ppermute | solution.py:477
  12.0 1.1 %edge_kernel.1.edges = bf16[16,192,128]{2,1,0:T(8,128)(2,1)S(1)} custom-call(bf16[8,192,192]{2,1,0:T(8,128)(2,1)S(1)} %get-tuple-element.39.high, bf16[8,192,192]{2,1,0:T(8,128)(2,1)S(1)} %get-tuple-element.40.low), custom_call_target="tpu_custom_call" | custom-call | tf_op jit(solution)/shard_map/edge_kernel/pallas_call | solution.py:461
  13.2 0.0 copy-done
  13.2 1.6 %own_kernel.1 = (f32[6,8,16,128]{3,2,1,0:T(8,128)S(1)}, f32[6,4,8,128]{3,2,1,0:T(8,128)S(1)}, f32[8,16,128]{2,1,0:T(8,128)S(1)}, f32[4,8,128]{2,1,0:T(8,128)S(1)}) custom-call(s32[8,16,128]{2,1,0:T(8,128)S(1)} %copy-done, f32[8,128]{1,0:T(8,128)S(1)} %get-tuple-element.32.table, f32[6,8,16,128]{3,2,1,0:T(8,128)S(1)} %get-tuple-element.33.b0, ...), custom_call_target="tpu_custom_call" | custom-call | tf_op jit(solution)/shard_map/own_kernel/pallas_call | solution.py:461
  14.8 0.0 collective-permute-done.x_far_in
  14.8 0.0 collective-permute-done.1.x_near_in
  14.8 0.0 collective-permute-done.2.y_far_in
  14.8 0.0 collective-permute-done.3.y_near_in
  14.8 1.0 %second_kernel.1 = (f32[6,4,8,128]{3,2,1,0:T(8,128)S(1)}, f32[6,4,8,128]{3,2,1,0:T(8,128)S(1)}, f32[6,8,128]{2,1,0:T(8,128)S(1)}, f32[6,8,128]{2,1,0:T(8,128)S(1...) custom-call(f32[6,4,8,128]{3,2,1,0:T(8,128)S(1)} %get-tuple-element.41.own_b1, ...), custom_call_target="tpu_custom_call" | custom-call | tf_op jit(solution)/shard_map/second_kernel/pallas_call | solution.py:461
  15.8 1.0 %collective-permute-start.4 = (f32[6,8,128]{2,1,0:T(8,128)S(1)}, f32[6,8,128]{2,1,0:T(8,128)S(1)}, u32[]{:S(2)}, u32[]{:S(2)}) collective-permute-start(f32[6,8,128]{2,1,0:T(8,128)S(1)} %get-tuple-element.45), channel_id=1, source_target_pairs={{0,1},{1,0},{2,3},{3,2},{4,5},{5,4},{6,7},{7,6},{8,16},{9,17},{10,... | collective-permute-start | bytes 73736 | tf_op jit(solution)/shard_map/ppermute | solution.py:477
  16.8 0.5 %collective-permute-start.5 = (f32[6,8,128]{2,1,0:T(8,128)S(1)}, f32[6,8,128]{2,1,0:T(8,128)S(1)}, u32[]{:S(2)}, u32[]{:S(2)}) collective-permute-start(f32[6,8,128]{2,1,0:T(8,128)S(1)} %get-tuple-element.46), channel_id=1, source_target_pairs={{0,8},{1,9},{2,10},{3,11},{4,12},{5,13},{6,14},{7,15},{8,0},{9,1},... | collective-permute-start | bytes 73736 | tf_op jit(solution)/shard_map/ppermute | solution.py:477
  17.3 2.2 %collective-permute-start.6 = (f32[6,8,128]{2,1,0:T(8,128)S(1)}, f32[6,8,128]{2,1,0:T(8,128)S(1)}, u32[]{:S(2)}, u32[]{:S(2)}) collective-permute-start(f32[6,8,128]{2,1,0:T(8,128)S(1)} %get-tuple-element.47), channel_id=1, source_target_pairs={{0,8},{1,2},{2,1},{3,4},{4,3},{5,6},{6,5},{7,15},{8,0},{9,10},{10,... | collective-permute-start | bytes 73736 | tf_op jit(solution)/shard_map/ppermute | solution.py:477
  19.5 0.1 collective-permute-start.7
  19.6 1.6 %middle_kernel.1.y0 = f32[6,8,16,128]{3,2,1,0:T(8,128)S(1)} custom-call(s32[8,512]{1,0:T(8,128)S(1)} %get-tuple-element.30.layers, f32[6,8,16,128]{3,2,1,0:T(8,128)S(1)} %get-tuple-element.31.x0, f32[6,8,16,128]{3,2,1,0:T(8,128)S(1)} %get-tuple-element.34.r0, f32[6,16,128]{2,1,0:T(8,128)S(1)} %collective-permute-done.x_far_in, ...), custom_call_target="tpu_custom_call" | custom-call | tf_op jit(solution)/shard_map/middle_kernel/pallas_call | solution.py:461
  21.2 0.0 collective-permute-done.4.x_far_in
  21.2 0.0 collective-permute-done.5.x_near_in
  21.2 0.1 collective-permute-done.6.y_far_in
  21.3 0.0 collective-permute-done.7.y_near_in
  21.3 0.9 %third_kernel.1 = (f32[6,4,8,128]{3,2,1,0:T(8,128)S(1)}, f32[6,8,128]{2,1,0:T(8,128)S(1)}, f32[6,8,128]{2,1,0:T(8,128)S(1)}, f32[6,8,128]{2,1,0:T(8,128)S(1)}, f32[6,8,128]{2,1,0:T(8,128)S(1)}) custom-call(s32[8,512]{1,0:T(8,128)S(1)} %get-tuple-element.30.layers, f32[6,8,16,128]{3,2,1,0:T(8,128)S(1)} %middle_kernel.1.y0, ...), custom_call_target="tpu_custom_call" | custom-call | tf_op jit(solution)/shard_map/third_kernel/pallas_call | solution.py:461
  22.2 2.2 %collective-permute-start.8 = (f32[6,8,128]{2,1,0:T(8,128)S(1)}, f32[6,8,128]{2,1,0:T(8,128)S(1)}, u32[]{:S(2)}, u32[]{:S(2)}) collective-permute-start(f32[6,8,128]{2,1,0:T(8,128)S(1)} %get-tuple-element.51), channel_id=1, source_target_pairs={{0,1},{1,0},{2,3},{3,2},{4,5},{5,4},{6,7},{7,6},{8,16},{9,17},{10,... | collective-permute-start | bytes 73736 | tf_op jit(solution)/shard_map/ppermute | solution.py:477
  24.4 0.0 collective-permute-start.9
  24.4 1.4 %collective-permute-start.10 = (f32[6,8,128]{2,1,0:T(8,128)S(1)}, f32[6,8,128]{2,1,0:T(8,128)S(1)}, u32[]{:S(2)}, u32[]{:S(2)}) collective-permute-start(f32[6,8,128]{2,1,0:T(8,128)S(1)} %get-tuple-element.53), channel_id=1, source_target_pairs={{0,8},{1,2},{2,1},{3,4},{4,3},{5,6},{6,5},{7,15},{8,0},{9,10},{10,... | collective-permute-start | bytes 73736 | tf_op jit(solution)/shard_map/ppermute | solution.py:477
  25.8 1.3 %collective-permute-start.11 = (f32[6,8,128]{2,1,0:T(8,128)S(1)}, f32[6,8,128]{2,1,0:T(8,128)S(1)}, u32[]{:S(2)}, u32[]{:S(2)}) collective-permute-start(f32[6,8,128]{2,1,0:T(8,128)S(1)} %get-tuple-element.54), channel_id=1, source_target_pairs={{0,1},{1,0},{2,3},{3,2},{4,5},{5,4},{6,7},{7,6},{8,9},{9,8},{10,11... | collective-permute-start | bytes 73736 | tf_op jit(solution)/shard_map/ppermute | solution.py:477
  27.2 1.7 %prolong_kernel.1.base = f32[6,8,16,128]{3,2,1,0:T(8,128)S(1)} custom-call(f32[6,4,8,128]{3,2,1,0:T(8,128)S(1)} %get-tuple-element.49.x1, f32[8,16,128]{2,1,0:T(8,128)S(1)} %get-tuple-element.50.sigma0, f32[6,8,16,128]{3,2,1,0:T(8,128)S(1)} %middle_kernel.1.y0, s32[8,512]{1,0:T(8,128)S(1)} %get-tuple-element.30.layers, ...), custom_call_target="tpu_custom_call" | custom-call | tf_op jit(solution)/shard_map/prolong_kernel/pallas_call | solution.py:461
  28.9 0.0 collective-permute-done.8.x_far_in
  28.9 0.0 collective-permute-done.9.x_near_in
  28.9 0.0 collective-permute-done.10.y_far_in
  28.9 0.0 collective-permute-done.11.y_near_in
  28.9 1.5 %last_kernel.1 = f32[6,8,16,128]{3,2,1,0:T(8,128)} custom-call(s32[8,512]{1,0:T(8,128)S(1)} %get-tuple-element.30.layers, f32[6,8,16,128]{3,2,1,0:T(8,128)S(1)} %prolong_kernel.1.base, f32[6,8,128]{2,1,0:T(8,128)S(1)} %collective-permute-done.8.x_far_in, f32[6,8,128]{2,1,0:T(8,128)S(1)} %collective-permute-done.9.x_near_in, ...), custom_call_target="tpu_custom_call" | custom-call | tf_op jit(solution)/shard_map/last_kernel/pallas_call | solution.py:461
Async XLA Ops:
  3.1 10.1 %copy-start = (s32[8,16,128]{2,1,0:T(8,128)S(1)}, s32[8,16,128]{2,1,0:T(8,128)}, u32[]{:S(2)}) copy-start(s32[8,16,128]{2,1,0:T(8,128)} %classes.1) | copy-start | bytes 196612
  3.1 11.6 %collective-permute-start = (f32[6,16,128]{2,1,0:T(8,128)S(1)}, f32[6,16,128]{2,1,0:T(8,128)S(1)}, u32[]{:S(2)}, u32[]{:S(2)}) collective-permute-start(f32[6,16,128]{2,1,0:T(8,128)S(1)} %get-tuple-element.35), channel_id=1, source_target_pairs={{0,1},{1,0},{2,3},{3,2},{4,5},{5,4},{6,7},{7,6},{8,16},{9,17},{10,... | collective-permute-start | bytes 147464 | tf_op jit(solution)/shard_map/ppermute | solution.py:477
  9.0 5.7 %collective-permute-start.1 = (f32[6,16,128]{2,1,0:T(8,128)S(1)}, f32[6,16,128]{2,1,0:T(8,128)S(1)}, u32[]{:S(2)}, u32[]{:S(2)}) collective-permute-start(f32[6,16,128]{2,1,0:T(8,128)S(1)} %get-tuple-element.36), channel_id=1, source_target_pairs={{0,8},{1,9},{2,10},{3,11},{4,12},{5,13},{6,14},{7,15},{8,0},{9,1},... | collective-permute-start | bytes 147464 | tf_op jit(solution)/shard_map/ppermute | solution.py:477
  9.1 5.7 %collective-permute-start.2 = (f32[6,16,128]{2,1,0:T(8,128)S(1)}, f32[6,16,128]{2,1,0:T(8,128)S(1)}, u32[]{:S(2)}, u32[]{:S(2)}) collective-permute-start(f32[6,16,128]{2,1,0:T(8,128)S(1)} %get-tuple-element.37), channel_id=1, source_target_pairs={{0,8},{1,2},{2,1},{3,4},{4,3},{5,6},{6,5},{7,15},{8,0},{9,10},{10,... | collective-permute-start | bytes 147464 | tf_op jit(solution)/shard_map/ppermute | solution.py:477
  11.2 3.6 %collective-permute-start.3 = (f32[6,16,128]{2,1,0:T(8,128)S(1)}, f32[6,16,128]{2,1,0:T(8,128)S(1)}, u32[]{:S(2)}, u32[]{:S(2)}) collective-permute-start(f32[6,16,128]{2,1,0:T(8,128)S(1)} %get-tuple-element.38), channel_id=1, source_target_pairs={{0,1},{1,0},{2,3},{3,2},{4,5},{5,4},{6,7},{7,6},{8,9},{9,8},{10,11... | collective-permute-start | bytes 147464 | tf_op jit(solution)/shard_map/ppermute | solution.py:477
  15.8 5.4 %collective-permute-start.4 = (f32[6,8,128]{2,1,0:T(8,128)S(1)}, f32[6,8,128]{2,1,0:T(8,128)S(1)}, u32[]{:S(2)}, u32[]{:S(2)}) collective-permute-start(f32[6,8,128]{2,1,0:T(8,128)S(1)} %get-tuple-element.45), channel_id=1, source_target_pairs={{0,1},{1,0},{2,3},{3,2},{4,5},{5,4},{6,7},{7,6},{8,16},{9,17},{10,... | collective-permute-start | bytes 73736 | tf_op jit(solution)/shard_map/ppermute | solution.py:477
  16.8 4.4 %collective-permute-start.5 = (f32[6,8,128]{2,1,0:T(8,128)S(1)}, f32[6,8,128]{2,1,0:T(8,128)S(1)}, u32[]{:S(2)}, u32[]{:S(2)}) collective-permute-start(f32[6,8,128]{2,1,0:T(8,128)S(1)} %get-tuple-element.46), channel_id=1, source_target_pairs={{0,8},{1,9},{2,10},{3,11},{4,12},{5,13},{6,14},{7,15},{8,0},{9,1},... | collective-permute-start | bytes 73736 | tf_op jit(solution)/shard_map/ppermute | solution.py:477
  17.3 4.0 %collective-permute-start.6 = (f32[6,8,128]{2,1,0:T(8,128)S(1)}, f32[6,8,128]{2,1,0:T(8,128)S(1)}, u32[]{:S(2)}, u32[]{:S(2)}) collective-permute-start(f32[6,8,128]{2,1,0:T(8,128)S(1)} %get-tuple-element.47), channel_id=1, source_target_pairs={{0,8},{1,2},{2,1},{3,4},{4,3},{5,6},{6,5},{7,15},{8,0},{9,10},{10,... | collective-permute-start | bytes 73736 | tf_op jit(solution)/shard_map/ppermute | solution.py:477
  19.5 1.8 %collective-permute-start.7 = (f32[6,8,128]{2,1,0:T(8,128)S(1)}, f32[6,8,128]{2,1,0:T(8,128)S(1)}, u32[]{:S(2)}, u32[]{:S(2)}) collective-permute-start(f32[6,8,128]{2,1,0:T(8,128)S(1)} %get-tuple-element.48), channel_id=1, source_target_pairs={{0,1},{1,0},{2,3},{3,2},{4,5},{5,4},{6,7},{7,6},{8,9},{9,8},{10,11... | collective-permute-start | bytes 73736 | tf_op jit(solution)/shard_map/ppermute | solution.py:477
  22.2 6.6 %collective-permute-start.8 = (f32[6,8,128]{2,1,0:T(8,128)S(1)}, f32[6,8,128]{2,1,0:T(8,128)S(1)}, u32[]{:S(2)}, u32[]{:S(2)}) collective-permute-start(f32[6,8,128]{2,1,0:T(8,128)S(1)} %get-tuple-element.51), channel_id=1, source_target_pairs={{0,1},{1,0},{2,3},{3,2},{4,5},{5,4},{6,7},{7,6},{8,16},{9,17},{10,... | collective-permute-start | bytes 73736 | tf_op jit(solution)/shard_map/ppermute | solution.py:477
  24.4 4.5 %collective-permute-start.9 = (f32[6,8,128]{2,1,0:T(8,128)S(1)}, f32[6,8,128]{2,1,0:T(8,128)S(1)}, u32[]{:S(2)}, u32[]{:S(2)}) collective-permute-start(f32[6,8,128]{2,1,0:T(8,128)S(1)} %get-tuple-element.52), channel_id=1, source_target_pairs={{0,8},{1,9},{2,10},{3,11},{4,12},{5,13},{6,14},{7,15},{8,0},{9,1},... | collective-permute-start | bytes 73736 | tf_op jit(solution)/shard_map/ppermute | solution.py:477
  24.4 4.5 %collective-permute-start.10 = (f32[6,8,128]{2,1,0:T(8,128)S(1)}, f32[6,8,128]{2,1,0:T(8,128)S(1)}, u32[]{:S(2)}, u32[]{:S(2)}) collective-permute-start(f32[6,8,128]{2,1,0:T(8,128)S(1)} %get-tuple-element.53), channel_id=1, source_target_pairs={{0,8},{1,2},{2,1},{3,4},{4,3},{5,6},{6,5},{7,15},{8,0},{9,10},{10,... | collective-permute-start | bytes 73736 | tf_op jit(solution)/shard_map/ppermute | solution.py:477
  25.8 3.1 %collective-permute-start.11 = (f32[6,8,128]{2,1,0:T(8,128)S(1)}, f32[6,8,128]{2,1,0:T(8,128)S(1)}, u32[]{:S(2)}, u32[]{:S(2)}) collective-permute-start(f32[6,8,128]{2,1,0:T(8,128)S(1)} %get-tuple-element.54), channel_id=1, source_target_pairs={{0,1},{1,0},{2,3},{3,2},{4,5},{5,4},{6,7},{7,6},{8,9},{9,8},{10,11... | collective-permute-start | bytes 73736 | tf_op jit(solution)/shard_map/ppermute | solution.py:477
